TPU v7x, 32 devices: a whole 2x2x4 slice. The times are simulated.
32 devices in a mesh: frames: 2 (over x), date: 16 (over z, y, core).
Axes of the slice: x: 2, y: 2, z: 4, core: 2. Of those that a mesh axis runs over, the one named last changes fastest.
Arguments:
- slc: float32 [2, 256, 288, 48], P(None, 'date', 'frames'), parts along dimension 2, may hold values from -6 to 6
Outputs:
- coherence: bfloat16 [96, 8, 256, 256], P(('frames', 'date')), parts along dimension 0
There are 2 independent parts, one for each index of `frames`. A program takes and returns all parts, laid end to end along the dimension named above; each array names one. Nothing has to cross between parts.
All inputs are finite; a program needn't handle non-finite values.
Results may differ from a plain program's by a relative error of at most 0.001.
Values sent between devices are 32-bit elements; how exact they have to be, the bound alone decides.
No kernel may reach another device: no remote copies, remote signals or barrier semaphores. Data moves between devices by JAX's collectives and lax.ppermute only.
A program may use at most 128 MiB of HBM per device.

v0:
```python
import functools

import jax
import jax.numpy as jnp
from jax import lax
from jax.experimental import pallas as pl
from jax.experimental.pallas import tpu as pltpu
from jax.sharding import PartitionSpec as P


BOX_AZ = 11
STEP_AZ = 3
STEP_RG = 6
MARGIN = 8
LANES = 128
CORES = 2
PAD_AZ = 16


def split(value):
    high = value.astype(jnp.bfloat16)
    low = (value - high.astype(jnp.float32)).astype(jnp.bfloat16)
    return high, low


def windows(planes, group, first_row):
    per_az = 2 * STEP_RG
    inside = lax.broadcasted_iota(jnp.int32, (PAD_AZ, LANES), 0) < BOX_AZ
    highs, lows = {}, {}
    for part in range(2):
        for col in range(STEP_RG):
            start = first_row * per_az + part * STEP_RG + col
            window = planes[group, pl.ds(start, PAD_AZ, stride=per_az), :]
            highs[part, col], lows[part, col] = split(jnp.where(inside, window, 0.0))
    return highs, lows


def stacked(pieces, keys):
    return jnp.concatenate(
        [pieces[which][part, col] if sign > 0 else -pieces[which][part, col] for which, part, col, sign in keys], axis=0
    )


def real_keys(thirds, cols):
    return [(which, part, col, 1) for which in thirds for part in range(2) for col in cols]


def imag_keys(thirds, cols):
    return [(which, 1 - part, col, 1 if part else -1) for which in thirds for part in range(2) for col in cols]


BULK, REST, LAST = range(STEP_RG - 2), [STEP_RG - 2], [STEP_RG - 1]
LEFT, RIGHT = (0, 0, 1), (0, 1, 0)


def products(left, rights):
    def lhs_of(thirds, cols):
        return stacked(left, real_keys(thirds, cols)).T

    def rhs_of(cols):
        sides = [stacked(right, keys(RIGHT, cols)) for right in rights for keys in (real_keys, imag_keys)]
        return jnp.concatenate(sides, axis=1)

    dot = functools.partial(
        lax.dot_general, dimension_numbers=(((1,), (0,)), ((), ())), preferred_element_type=jnp.float32
    )
    high, low = lhs_of([0], BULK), lhs_of([1], BULK)
    lhs = jnp.concatenate([high, high, low, lhs_of(LEFT, REST)], axis=1)
    rhs = jnp.concatenate([rhs_of(BULK), rhs_of(REST)], axis=0)
    return dot(lhs, rhs), dot(lhs_of(LEFT, LAST), rhs_of(LAST))


def square_iotas():
    return (lax.broadcasted_iota(jnp.int32, (LANES, LANES), dimension) for dimension in range(2))


def blocks_of(both):
    low, up = square_iotas()
    cut = [both[:, i * LANES : (i + 1) * LANES] for i in range(both.shape[1] // LANES)]
    return [jnp.where(up >= low, cut[0], cut[1])] + cut[2:]


def box_sums(made, last_partial, pending, pair):
    boxes = []
    for i, (partial, last) in enumerate(zip(blocks_of(made[0]), blocks_of(made[1]))):
        full = partial + last
        boxes.append(full + pending[i])
        pending[i] = full + pair[i]
        pair[i] = full + last_partial[i]
        last_partial[i] = partial
    return boxes


def inverse_roots(box):
    low, up = square_iotas()
    return lax.rsqrt(jnp.sum(jnp.where(up == low, box, 0.0), axis=0, keepdims=True))


def spread(row):
    return jnp.broadcast_to(row, (LANES, LANES))


def over_groups(groups, sums, make, finish):
    for ref in sums:
        ref[...] = jnp.zeros_like(ref)
    ready = None
    for group in reversed(range(groups)):
        made = make(group)
        if ready is not None:
            finish(group + 1, box_sums(ready, *sums))
        ready = made
    finish(0, box_sums(ready, *sums))


def near_body(planes, out_ref, roots_ref, sums, groups):
    first_row = pl.program_id(0) * STEP_AZ

    def make(group):
        pieces = windows(planes, group, first_row)
        return products(pieces, [pieces])

    def finish(group, boxes):
        roots = inverse_roots(boxes[0])
        roots_ref[0, group] = roots
        out_ref[0, group] = (boxes[0] * (spread(roots).T * spread(roots))).astype(jnp.bfloat16)

    over_groups(groups, sums, make, finish)


def far_body(far_half, planes, near_planes, near_ref, roots_ref, out_ref, sums, groups):
    first_row = pl.program_id(0) * STEP_AZ
    upper = far_half == 1
    far_rows = pl.ds(pl.multiple_of(far_half * LANES, LANES), LANES)
    near_rows = pl.ds(pl.multiple_of((1 - far_half) * LANES, LANES), LANES)

    def make(group):
        pieces = windows(planes, group, first_row)
        return products(pieces, [pieces, windows(near_planes, group, first_row)])

    def finish(group, boxes):
        square, real, imag = boxes
        far_across = spread(inverse_roots(square))
        far_down = far_across.T
        near_across = spread(roots_ref[0, group])
        square = square * (far_down * far_across)
        scale = far_down * near_across
        real, imag = real * scale, imag * scale
        straight = jnp.where(upper, imag, real).astype(jnp.bfloat16)
        turned = jnp.where(upper, real, -imag).T.astype(jnp.bfloat16)
        out_ref[0, group, near_rows, near_rows] = near_ref[0, group]
        out_ref[0, group, far_rows, far_rows] = square.astype(jnp.bfloat16)
        out_ref[0, group, far_rows, near_rows] = straight
        out_ref[0, group, near_rows, far_rows] = turned

    over_groups(groups, sums, make, finish)


def plane_rows(out_rows):
    return (STEP_AZ * (out_rows - 1) + PAD_AZ) * 2 * STEP_RG


def sums_scratch(count):
    return [pltpu.VMEM((count, LANES, LANES), jnp.float32)] * 3


def row_spec(*shape):
    return pl.BlockSpec((1, *shape), lambda a: (a,) + (0,) * len(shape))


def whole_spec(array):
    return pl.BlockSpec(array.shape, lambda a: (0,) * len(array.shape))


def need_rows(out_rows):
    return (STEP_AZ * (out_rows - 1) + BOX_AZ) * 2 * STEP_RG


def near_grams(blocks, out_rows, groups, slab):
    def body(*refs):
        block_refs, (planes, out_ref, roots_ref, *sums) = refs[: len(blocks)], refs[len(blocks) :]

        @pl.when(pl.program_id(0) == 0)
        def _():
            assemble(block_refs, planes, groups, slab, need_rows(out_rows))

        near_body(planes, out_ref, roots_ref, sums, groups)

    planes = jax.ShapeDtypeStruct((groups, plane_rows(out_rows), LANES), jnp.float32)
    return pl.pallas_call(
        body,
        grid=(out_rows,),
        in_specs=[whole_spec(block) for block in blocks],
        out_specs=[whole_spec(planes), row_spec(groups, LANES, LANES), row_spec(groups, 1, LANES)],
        out_shape=[
            planes,
            jax.ShapeDtypeStruct((out_rows, groups, LANES, LANES), jnp.bfloat16),
            jax.ShapeDtypeStruct((out_rows, groups, 1, LANES), jnp.float32),
        ],
        scratch_shapes=sums_scratch(1),
    )(*blocks)


def far_grams(blocks, near, out_rows, groups, slab):
    def body(*refs):
        block_refs, (near_planes, near_ref, roots_ref, out_ref, planes, *sums) = refs[: len(blocks)], refs[len(blocks) :]

        @pl.when(pl.program_id(0) == 0)
        def _():
            assemble(block_refs, planes, groups, slab, need_rows(out_rows))

        far_half = 1 - lax.axis_index("date") // groups
        far_body(far_half, planes, near_planes, near_ref, roots_ref, out_ref, sums, groups)

    near_planes, _, _ = near
    dates = 2 * LANES
    return pl.pallas_call(
        body,
        grid=(out_rows,),
        in_specs=[whole_spec(block) for block in blocks]
        + [whole_spec(near_planes), row_spec(groups, LANES, LANES), row_spec(groups, 1, LANES)],
        out_specs=row_spec(groups, dates, dates),
        out_shape=jax.ShapeDtypeStruct((out_rows, groups, dates, dates), jnp.bfloat16),
        scratch_shapes=[pltpu.VMEM(near_planes.shape, jnp.float32)] + sums_scratch(3),
    )(*blocks, *near)


def grams_of_planes(planes, out_rows):
    groups = planes.shape[1]
    dates = 2 * LANES

    def near(planes_ref, out_ref, roots_ref, *sums):
        near_body(planes_ref, out_ref, roots_ref, sums, groups)

    def far(planes_ref, near_planes, near_ref, roots_ref, out_ref, *sums):
        far_body(jnp.int32(1), planes_ref, near_planes, near_ref, roots_ref, out_ref, sums, groups)

    kept = [row_spec(groups, LANES, LANES), row_spec(groups, 1, LANES)]
    near_out = pl.pallas_call(
        near,
        grid=(out_rows,),
        in_specs=[whole_spec(planes[0])],
        out_specs=kept,
        out_shape=[
            jax.ShapeDtypeStruct((out_rows, groups, LANES, LANES), jnp.bfloat16),
            jax.ShapeDtypeStruct((out_rows, groups, 1, LANES), jnp.float32),
        ],
        scratch_shapes=sums_scratch(1),
    )(planes[0])
    return pl.pallas_call(
        far,
        grid=(out_rows,),
        in_specs=[whole_spec(planes[1]), whole_spec(planes[0])] + kept,
        out_specs=row_spec(groups, dates, dates),
        out_shape=jax.ShapeDtypeStruct((out_rows, groups, dates, dates), jnp.bfloat16),
        scratch_shapes=sums_scratch(3),
    )(planes[1], planes[0], *near_out)


def pack_kernel(chips, groups, slab, x0_ref, x1_ref, *rest):
    out_refs, (rows_ref, sems) = rest[:chips], rest[chips:]
    me = lax.axis_index("date")
    chip, slot = me // CORES, lax.rem(me, groups)
    width = groups * STEP_RG
    dates = LANES // groups
    per_az = 2 * STEP_RG
    azimuths = chips * CORES * slab
    rows_ref[pl.ds(azimuths * per_az, MARGIN * per_az), :] = jnp.zeros((MARGIN * per_az, LANES), jnp.float32)
    tail = azimuths - LANES
    for part in range(2):
        for col in range(STEP_RG):
            at = part * STEP_RG + col
            for x_ref, first, count in ((x0_ref, 0, LANES), (x1_ref, LANES, tail)):
                pieces = []
                for place in range(groups):
                    group = lax.rem(place - slot + groups, groups)
                    start = part * dates * width + col + group * STEP_RG
                    pieces.append(x_ref[pl.ds(start, dates, stride=width), :])
                turned = jnp.concatenate(pieces, axis=0).T
                rows_ref[pl.ds(first * per_az + at, count, stride=per_az), :] = turned[:count]
    chip_rows = CORES * slab * per_az
    copies = []
    for step in range(chips):
        start = pl.multiple_of(jnp.bitwise_xor(chip, step) * chip_rows, 8)
        copy = pltpu.make_async_copy(
            rows_ref.at[pl.ds(start, chip_rows + MARGIN * per_az), :], out_refs[step], sems.at[step]
        )
        copy.start()
        copies.append(copy)
    for copy in copies:
        copy.wait()


def pack(flat, chips, groups, slab):
    per_az = 2 * STEP_RG
    azimuths = chips * CORES * slab
    rows = (CORES * slab + MARGIN) * per_az
    spec0 = pl.BlockSpec((flat.shape[0], LANES), lambda i: (0, 0))
    spec1 = pl.BlockSpec((flat.shape[0], LANES), lambda i: (0, 1))
    return pl.pallas_call(
        functools.partial(pack_kernel, chips, groups, slab),
        grid=(1,),
        in_specs=[spec0, spec1],
        out_specs=[pl.BlockSpec(memory_space=pl.ANY)] * chips,
        out_shape=[jax.ShapeDtypeStruct((rows, LANES), jnp.float32)] * chips,
        scratch_shapes=[
            pltpu.VMEM(((azimuths + MARGIN) * per_az, LANES), jnp.float32),
            pltpu.SemaphoreType.DMA((chips,)),
        ],
    )(flat, flat)


def assemble(blocks, planes, groups, slab, need):
    me = lax.axis_index("date")
    slot = lax.rem(me, groups)
    width = LANES // groups
    place = lax.broadcasted_iota(jnp.int32, (8, LANES), 1) // width
    held = [lax.rem(place - jnp.bitwise_xor(slot, source) + groups, groups) for source in range(groups)]
    first = lax.rem(me, CORES) * (slab * 2 * STEP_RG)
    starts = [8 * i for i in range(need // 8)] + ([need - 8] if need % 8 else [])
    for start in starts:
        loaded = [block[pl.ds(first + start, 8), :] for block in blocks]
        for group in range(groups):
            merged = loaded[0]
            for source in range(1, groups):
                merged = jnp.where(held[source] == group, loaded[source], merged)
            if group:
                merged = pltpu.roll(merged, LANES - width * group, 1)
            planes[group, pl.ds(start, 8), :] = merged


def swap(value, distance):
    count = lax.axis_size("date")
    return lax.ppermute(value, "date", [(i, i ^ distance) for i in range(count)])


def legs_in_order(chips):
    far = [step for step in range(chips // 2, chips) if step % 2 == 0]
    rest = [step for step in range(chips // 2, chips) if step % 2]
    near = list(range(2, chips // 2)) + [1]
    return far + near + rest


def by_chips(slc, slab, out_rows, groups):
    chips = lax.axis_size("date") // CORES
    flat = jnp.swapaxes(slc, 2, 3).reshape(-1, slc.shape[2])
    sent = pack(flat, chips, groups, slab)
    arrived = {0: sent[0]}
    for step in legs_in_order(chips):
        arrived[step] = swap(sent[step], CORES * step)
    blocks = []
    for step in range(chips):
        blocks += [arrived[step], swap(arrived[step], 1)]
    near = near_grams(blocks[:groups], out_rows, groups, slab)
    return far_grams(blocks[groups:], near, out_rows, groups, slab)


def by_slabs(slc, slab, out_rows, groups):
    slab_pixels = lax.all_to_all(slc, "date", split_axis=2, concat_axis=1, tiled=True)
    count = lax.axis_size("date")
    below = lax.ppermute(slab_pixels[:, :, :MARGIN, :], "date", [(i, i - 1) for i in range(1, count)])
    whole = jnp.concatenate([slab_pixels, below], axis=2)
    parts, dates, rows, _ = whole.shape
    planes = whole.reshape(parts, 2, dates // 2, rows, groups, STEP_RG).transpose(1, 4, 3, 0, 5, 2)
    planes = planes.reshape(2, groups, rows * parts * STEP_RG, dates // 2)
    planes = jnp.pad(planes, ((0, 0), (0, 0), (0, plane_rows(out_rows) - planes.shape[2]), (0, 0)))
    return grams_of_planes(planes, out_rows)


def on_device(slc):
    count = lax.axis_size("date")
    slab = slc.shape[2] // count
    groups = slc.shape[3] // STEP_RG
    fits = (
        groups * slc.shape[1] == LANES
        and count == 2 * groups
        and LANES < slc.shape[2] <= 2 * LANES
        and (CORES * slab * 2 * STEP_RG) % 8 == 0
    )
    return (by_chips if fits else by_slabs)(slc, slab, slab // STEP_AZ, groups)


def solution(mesh):
    in_specs = (P(None, "date", "frames", None),)
    out_specs = P(("frames", "date"), None, None, None)
    return jax.shard_map(on_device, mesh=mesh, in_specs=in_specs, out_specs=out_specs, check_vma=False)
```

profile of v0, /device:TPU:9, one launch (start us, length us, event | category | flops | bytes accessed | tf_op | source)
XLA Modules:
  0.0 51.8 jit_solution(14424821436316258050)
XLA Ops:
  0.0 3.0 %shard_map.17 = (f32[312,128]{1,0:T(8,128)}, f32[312,128]{1,0:T(8,128)}, f32[312,128]{1,0:T(8,128)}, f32[312,128]{1,0:T(8,128)}, f32[312,128]{1,0:T(8,128)}, /*i...) custom-call(f32[1536,144]{1,0:T(8,128)} %bitcast.3, f32[1536,144]{1,0:T(8,128)} %bitcast.4), custom_call_target="tpu_custom_call" | custom-call | tf_op jit(solution)/shard_map/pallas_call | solution.py:299
  3.0 2.4 %collective-permute-start = (f32[312,128]{1,0:T(8,128)}, f32[312,128]{1,0:T(8,128)S(1)}, u32[]{:S(2)}, u32[]{:S(2)}) collective-permute-start(f32[312,128]{1,0:T(8,128)} %get-tuple-element.16), channel_id=1, source_target_pairs={{0,8},{1,9},{2,10},{3,11},{4,12},{5,13},{6,14},{7,15},{8,0},{9,1},... | collective-permute-start | bytes 479240 | tf_op jit(solution)/shard_map/ppermute | solution.py:333
  5.4 1.0 %collective-permute-start.2 = (f32[312,128]{1,0:T(8,128)}, f32[312,128]{1,0:T(8,128)S(1)}, u32[]{:S(2)}, u32[]{:S(2)}) collective-permute-start(f32[312,128]{1,0:T(8,128)} %get-tuple-element.17), channel_id=1, source_target_pairs={{0,10},{1,11},{2,8},{3,9},{4,14},{5,15},{6,12},{7,13},{8,2},{9,3},... | collective-permute-start | bytes 479240 | tf_op jit(solution)/shard_map/ppermute | solution.py:333
  6.4 1.3 %collective-permute-start.4 = (f32[312,128]{1,0:T(8,128)}, f32[312,128]{1,0:T(8,128)S(1)}, u32[]{:S(2)}, u32[]{:S(2)}) collective-permute-start(f32[312,128]{1,0:T(8,128)} %get-tuple-element.18), channel_id=1, source_target_pairs={{0,12},{1,13},{2,14},{3,15},{4,8},{5,9},{6,10},{7,11},{8,4},{9,5},... | collective-permute-start | bytes 479240 | tf_op jit(solution)/shard_map/ppermute | solution.py:333
  7.7 0.2 collective-permute-start.9
  7.9 2.2 %collective-permute-start.11 = (f32[312,128]{1,0:T(8,128)}, f32[312,128]{1,0:T(8,128)S(1)}, u32[]{:S(2)}, u32[]{:S(2)}) collective-permute-start(f32[312,128]{1,0:T(8,128)} %get-tuple-element.22), channel_id=1, source_target_pairs={{0,4},{1,5},{2,6},{3,7},{4,0},{5,1},{6,2},{7,3},{8,12},{9,13},{10,... | collective-permute-start | bytes 479240 | tf_op jit(solution)/shard_map/ppermute | solution.py:333
  10.1 9.6 %collective-permute-done.refs_0_ = f32[312,128]{1,0:T(8,128)S(1)} collective-permute-done((f32[312,128]{1,0:T(8,128)}, f32[312,128]{1,0:T(8,128)S(1)}, u32[]{:S(2)}, u32[]{:S(2)}) %collective-permute-start) | collective-permute-done | bytes 159776 | tf_op jit(solution)/shard_map/ppermute | solution.py:333
  19.7 0.0 copy-start.7
  19.7 0.0 collective-permute-start.6
  19.7 3.4 %collective-permute-done.2.refs_2_ = f32[312,128]{1,0:T(8,128)S(1)} collective-permute-done((f32[312,128]{1,0:T(8,128)}, f32[312,128]{1,0:T(8,128)S(1)}, u32[]{:S(2)}, u32[]{:S(2)}) %collective-permute-start.2) | collective-permute-done | bytes 159776 | tf_op jit(solution)/shard_map/ppermute | solution.py:333
  23.1 0.0 copy-start.8
  23.1 1.7 %collective-permute-start.13 = (f32[312,128]{1,0:T(8,128)}, f32[312,128]{1,0:T(8,128)S(1)}, u32[]{:S(2)}, u32[]{:S(2)}) collective-permute-start(f32[312,128]{1,0:T(8,128)} %get-tuple-element.23), channel_id=1, source_target_pairs={{0,6},{1,7},{2,4},{3,5},{4,2},{5,3},{6,0},{7,1},{8,14},{9,15},{10,... | collective-permute-start | bytes 479240 | tf_op jit(solution)/shard_map/ppermute | solution.py:333
  24.8 4.8 %collective-permute-done.4.refs_4_ = f32[312,128]{1,0:T(8,128)S(1)} collective-permute-done((f32[312,128]{1,0:T(8,128)}, f32[312,128]{1,0:T(8,128)S(1)}, u32[]{:S(2)}, u32[]{:S(2)}) %collective-permute-start.4) | collective-permute-done | bytes 159776 | tf_op jit(solution)/shard_map/ppermute | solution.py:333
  29.6 0.0 copy-start.9
  29.6 1.5 %collective-permute-start.8 = (f32[312,128]{1,0:T(8,128)}, f32[312,128]{1,0:T(8,128)S(1)}, u32[]{:S(2)}, u32[]{:S(2)}) collective-permute-start(f32[312,128]{1,0:T(8,128)} %get-tuple-element.20.refs_0_), channel_id=1, source_target_pairs={{0,1},{1,0},{2,3},{3,2},{4,5},{5,4},{6,7},{7,6},{8,9},{9,8},{10,11... | collective-permute-start | bytes 479240 | tf_op jit(solution)/shard_map/ppermute | solution.py:333
  31.1 0.0 collective-permute-done.9.refs_2_
  31.1 0.0 copy-start
  31.1 0.1 collective-permute-start.10
  31.2 0.0 collective-permute-done.11.refs_4_
  31.2 0.0 copy-start.1
  31.2 0.4 collective-permute-start.12
  31.6 2.9 %collective-permute-done.6.refs_6_ = f32[312,128]{1,0:T(8,128)S(1)} collective-permute-done((f32[312,128]{1,0:T(8,128)}, f32[312,128]{1,0:T(8,128)S(1)}, u32[]{:S(2)}, u32[]{:S(2)}) %collective-permute-start.6) | collective-permute-done | bytes 159776 | tf_op jit(solution)/shard_map/ppermute | solution.py:333
  34.5 0.0 copy-start.10
  34.5 1.9 %collective-permute-start.1 = (f32[312,128]{1,0:T(8,128)S(1)}, f32[312,128]{1,0:T(8,128)S(1)}, u32[]{:S(2)}, u32[]{:S(2)}) collective-permute-start(f32[312,128]{1,0:T(8,128)S(1)} %collective-permute-done.refs_0_), channel_id=1, source_target_pairs={{0,1},{1,0},{2,3},{3,2},{4,5},{5,4},{6,7},{7,6},{8,9},{9,8},{10,11... | collective-permute-start | bytes 479240 | tf_op jit(solution)/shard_map/ppermute | solution.py:333
  36.4 0.0 collective-permute-done.13.refs_6_
  36.4 0.0 copy-start.2
  36.4 0.1 collective-permute-start.14
  36.5 0.0 collective-permute-done.8.refs_1_
  36.5 0.0 copy-start.3
  36.5 0.4 collective-permute-start.3
  37.0 0.0 collective-permute-done.10.refs_3_
  37.0 0.0 copy-start.4
  37.0 0.1 collective-permute-start.5
  37.1 0.0 collective-permute-done.12.refs_5_
  37.1 0.0 copy-start.5
  37.1 0.4 collective-permute-start.7
  37.5 0.3 collective-permute-done.14.refs_7_
  37.8 0.0 copy-done
  37.8 0.0 copy-done.1
  37.8 0.0 copy-done.2
  37.9 0.0 copy-done.3
  37.9 0.0 copy-done.4
  37.9 0.0 copy-done.5
  37.9 0.0 copy-start.6
  37.9 0.7 %copy-done.6 = f32[312,128]{1,0:T(8,128)} copy-done((f32[312,128]{1,0:T(8,128)}, f32[312,128]{1,0:T(8,128)S(1)}, u32[]{:S(2)}) %copy-start.6) | copy-done | bytes 159768
  38.6 4.9 %shard_map.18 = (f32[8,264,128]{2,1,0:T(8,128)}, bf16[3,8,128,128]{3,2,1,0:T(8,128)(2,1)}, f32[3,8,1,128]{3,2,1,0:T(1,128)}) custom-call(f32[312,128]{1,0:T(8,128)} %get-tuple-element.20.refs_0_, f32[312,128]{1,0:T(8,128)} %copy-done.3, f32[312,128]{1,0:T(8,128)} %copy-done, f32[312,128]{1,0:T(8,128)} %copy-done.4, f32[312,128]{1,0:T(8,128)} %copy-done.1, ...), custom_call_target="tpu_custom_call" | custom-call | tf_op jit(solution)/shard_map/pallas_call | solution.py:189
  43.5 0.0 collective-permute-done.1.refs_1_
  43.5 0.0 copy-start.11
  43.5 0.0 collective-permute-done.3.refs_3_
  43.5 0.0 copy-start.12
  43.5 0.0 collective-permute-done.5.refs_5_
  43.5 0.0 copy-start.13
  43.5 0.0 collective-permute-done.7.refs_7_
  43.5 0.0 copy-start.14
  43.5 0.0 copy-done.7
  43.6 0.0 copy-done.8
  43.6 0.0 copy-done.9
  43.6 0.0 copy-done.10
  43.6 0.6 %copy-done.11 = f32[312,128]{1,0:T(8,128)} copy-done((f32[312,128]{1,0:T(8,128)}, f32[312,128]{1,0:T(8,128)S(1)}, u32[]{:S(2)}) %copy-start.11) | copy-done | bytes 159768
  44.1 0.1 copy-done.12
  44.2 0.0 copy-done.13
  44.3 0.1 copy-done.14
  44.3 7.5 %shard_map.19 = bf16[3,8,256,256]{3,2,1,0:T(8,128)(2,1)} custom-call(f32[312,128]{1,0:T(8,128)} %copy-done.7, f32[312,128]{1,0:T(8,128)} %copy-done.11, f32[312,128]{1,0:T(8,128)} %copy-done.8, f32[312,128]{1,0:T(8,128)} %copy-done.12, f32[312,128]{1,0:T(8,128)} %copy-done.9, f32[312,128]{1,0:T(8,128)} %copy-done.13, f32[312,128]{1,0:T(8,128)} %copy-done.10, ...), custom_call_target="tpu_custom_call" | custom-call | tf_op jit(solution)/shard_map/pallas_call | solution.py:216
Async XLA Ops:
  3.0 16.7 %collective-permute-start = (f32[312,128]{1,0:T(8,128)}, f32[312,128]{1,0:T(8,128)S(1)}, u32[]{:S(2)}, u32[]{:S(2)}) collective-permute-start(f32[312,128]{1,0:T(8,128)} %get-tuple-element.16), channel_id=1, source_target_pairs={{0,8},{1,9},{2,10},{3,11},{4,12},{5,13},{6,14},{7,15},{8,0},{9,1},... | collective-permute-start | bytes 479240 | tf_op jit(solution)/shard_map/ppermute | solution.py:333
  5.4 17.7 %collective-permute-start.2 = (f32[312,128]{1,0:T(8,128)}, f32[312,128]{1,0:T(8,128)S(1)}, u32[]{:S(2)}, u32[]{:S(2)}) collective-permute-start(f32[312,128]{1,0:T(8,128)} %get-tuple-element.17), channel_id=1, source_target_pairs={{0,10},{1,11},{2,8},{3,9},{4,14},{5,15},{6,12},{7,13},{8,2},{9,3},... | collective-permute-start | bytes 479240 | tf_op jit(solution)/shard_map/ppermute | solution.py:333
  6.4 23.2 %collective-permute-start.4 = (f32[312,128]{1,0:T(8,128)}, f32[312,128]{1,0:T(8,128)S(1)}, u32[]{:S(2)}, u32[]{:S(2)}) collective-permute-start(f32[312,128]{1,0:T(8,128)} %get-tuple-element.18), channel_id=1, source_target_pairs={{0,12},{1,13},{2,14},{3,15},{4,8},{5,9},{6,10},{7,11},{8,4},{9,5},... | collective-permute-start | bytes 479240 | tf_op jit(solution)/shard_map/ppermute | solution.py:333
  7.7 23.4 %collective-permute-start.9 = (f32[312,128]{1,0:T(8,128)}, f32[312,128]{1,0:T(8,128)S(1)}, u32[]{:S(2)}, u32[]{:S(2)}) collective-permute-start(f32[312,128]{1,0:T(8,128)} %get-tuple-element.21), channel_id=1, source_target_pairs={{0,2},{1,3},{2,0},{3,1},{4,6},{5,7},{6,4},{7,5},{8,10},{9,11},{10,... | collective-permute-start | bytes 479240 | tf_op jit(solution)/shard_map/ppermute | solution.py:333
  7.9 23.3 %collective-permute-start.11 = (f32[312,128]{1,0:T(8,128)}, f32[312,128]{1,0:T(8,128)S(1)}, u32[]{:S(2)}, u32[]{:S(2)}) collective-permute-start(f32[312,128]{1,0:T(8,128)} %get-tuple-element.22), channel_id=1, source_target_pairs={{0,4},{1,5},{2,6},{3,7},{4,0},{5,1},{6,2},{7,3},{8,12},{9,13},{10,... | collective-permute-start | bytes 479240 | tf_op jit(solution)/shard_map/ppermute | solution.py:333
  19.7 23.8 %copy-start.7 = (f32[312,128]{1,0:T(8,128)}, f32[312,128]{1,0:T(8,128)S(1)}, u32[]{:S(2)}) copy-start(f32[312,128]{1,0:T(8,128)S(1)} %collective-permute-done.refs_0_) | copy-start | bytes 479236
  19.7 14.8 %collective-permute-start.6 = (f32[312,128]{1,0:T(8,128)}, f32[312,128]{1,0:T(8,128)S(1)}, u32[]{:S(2)}, u32[]{:S(2)}) collective-permute-start(f32[312,128]{1,0:T(8,128)} %get-tuple-element.19), channel_id=1, source_target_pairs={{0,14},{1,15},{2,12},{3,13},{4,10},{5,11},{6,8},{7,9},{8,6},{9,7},... | collective-permute-start | bytes 479240 | tf_op jit(solution)/shard_map/ppermute | solution.py:333
  23.1 20.4 %copy-start.8 = (f32[312,128]{1,0:T(8,128)}, f32[312,128]{1,0:T(8,128)S(1)}, u32[]{:S(2)}) copy-start(f32[312,128]{1,0:T(8,128)S(1)} %collective-permute-done.2.refs_2_) | copy-start | bytes 479236
  23.1 13.3 %collective-permute-start.13 = (f32[312,128]{1,0:T(8,128)}, f32[312,128]{1,0:T(8,128)S(1)}, u32[]{:S(2)}, u32[]{:S(2)}) collective-permute-start(f32[312,128]{1,0:T(8,128)} %get-tuple-element.23), channel_id=1, source_target_pairs={{0,6},{1,7},{2,4},{3,5},{4,2},{5,3},{6,0},{7,1},{8,14},{9,15},{10,... | collective-permute-start | bytes 479240 | tf_op jit(solution)/shard_map/ppermute | solution.py:333
  29.6 14.0 %copy-start.9 = (f32[312,128]{1,0:T(8,128)}, f32[312,128]{1,0:T(8,128)S(1)}, u32[]{:S(2)}) copy-start(f32[312,128]{1,0:T(8,128)S(1)} %collective-permute-done.4.refs_4_) | copy-start | bytes 479236
  29.6 6.9 %collective-permute-start.8 = (f32[312,128]{1,0:T(8,128)}, f32[312,128]{1,0:T(8,128)S(1)}, u32[]{:S(2)}, u32[]{:S(2)}) collective-permute-start(f32[312,128]{1,0:T(8,128)} %get-tuple-element.20.refs_0_), channel_id=1, source_target_pairs={{0,1},{1,0},{2,3},{3,2},{4,5},{5,4},{6,7},{7,6},{8,9},{9,8},{10,11... | collective-permute-start | bytes 479240 | tf_op jit(solution)/shard_map/ppermute | solution.py:333
  31.1 6.7 %copy-start = (f32[312,128]{1,0:T(8,128)}, f32[312,128]{1,0:T(8,128)S(1)}, u32[]{:S(2)}) copy-start(f32[312,128]{1,0:T(8,128)S(1)} %collective-permute-done.9.refs_2_) | copy-start | bytes 479236
  31.1 5.9 %collective-permute-start.10 = (f32[312,128]{1,0:T(8,128)S(1)}, f32[312,128]{1,0:T(8,128)S(1)}, u32[]{:S(2)}, u32[]{:S(2)}) collective-permute-start(f32[312,128]{1,0:T(8,128)S(1)} %collective-permute-done.9.refs_2_), channel_id=1, source_target_pairs={{0,1},{1,0},{2,3},{3,2},{4,5},{5,4},{6,7},{7,6},{8,9},{9,8},{10,11... | collective-permute-start | bytes 479240 | tf_op jit(solution)/shard_map/ppermute | solution.py:333
  31.2 6.7 %copy-start.1 = (f32[312,128]{1,0:T(8,128)}, f32[312,128]{1,0:T(8,128)S(1)}, u32[]{:S(2)}) copy-start(f32[312,128]{1,0:T(8,128)S(1)} %collective-permute-done.11.refs_4_) | copy-start | bytes 479236
  31.2 5.9 %collective-permute-start.12 = (f32[312,128]{1,0:T(8,128)S(1)}, f32[312,128]{1,0:T(8,128)S(1)}, u32[]{:S(2)}, u32[]{:S(2)}) collective-permute-start(f32[312,128]{1,0:T(8,128)S(1)} %collective-permute-done.11.refs_4_), channel_id=1, source_target_pairs={{0,1},{1,0},{2,3},{3,2},{4,5},{5,4},{6,7},{7,6},{8,9},{9,8},{10,11... | collective-permute-start | bytes 479240 | tf_op jit(solution)/shard_map/ppermute | solution.py:333
  34.5 9.1 %copy-start.10 = (f32[312,128]{1,0:T(8,128)}, f32[312,128]{1,0:T(8,128)S(1)}, u32[]{:S(2)}) copy-start(f32[312,128]{1,0:T(8,128)S(1)} %collective-permute-done.6.refs_6_) | copy-start | bytes 479236
  34.5 9.0 %collective-permute-start.1 = (f32[312,128]{1,0:T(8,128)S(1)}, f32[312,128]{1,0:T(8,128)S(1)}, u32[]{:S(2)}, u32[]{:S(2)}) collective-permute-start(f32[312,128]{1,0:T(8,128)S(1)} %collective-permute-done.refs_0_), channel_id=1, source_target_pairs={{0,1},{1,0},{2,3},{3,2},{4,5},{5,4},{6,7},{7,6},{8,9},{9,8},{10,11... | collective-permute-start | bytes 479240 | tf_op jit(solution)/shard_map/ppermute | solution.py:333
  36.4 1.4 %copy-start.2 = (f32[312,128]{1,0:T(8,128)}, f32[312,128]{1,0:T(8,128)S(1)}, u32[]{:S(2)}) copy-start(f32[312,128]{1,0:T(8,128)S(1)} %collective-permute-done.13.refs_6_) | copy-start | bytes 479236
  36.4 1.4 %collective-permute-start.14 = (f32[312,128]{1,0:T(8,128)S(1)}, f32[312,128]{1,0:T(8,128)S(1)}, u32[]{:S(2)}, u32[]{:S(2)}) collective-permute-start(f32[312,128]{1,0:T(8,128)S(1)} %collective-permute-done.13.refs_6_), channel_id=1, source_target_pairs={{0,1},{1,0},{2,3},{3,2},{4,5},{5,4},{6,7},{7,6},{8,9},{9,8},{10,11... | collective-permute-start | bytes 479240 | tf_op jit(solution)/shard_map/ppermute | solution.py:333
  36.5 1.3 %copy-start.3 = (f32[312,128]{1,0:T(8,128)}, f32[312,128]{1,0:T(8,128)S(1)}, u32[]{:S(2)}) copy-start(f32[312,128]{1,0:T(8,128)S(1)} %collective-permute-done.8.refs_1_) | copy-start | bytes 479236
  36.5 7.0 %collective-permute-start.3 = (f32[312,128]{1,0:T(8,128)S(1)}, f32[312,128]{1,0:T(8,128)S(1)}, u32[]{:S(2)}, u32[]{:S(2)}) collective-permute-start(f32[312,128]{1,0:T(8,128)S(1)} %collective-permute-done.2.refs_2_), channel_id=1, source_target_pairs={{0,1},{1,0},{2,3},{3,2},{4,5},{5,4},{6,7},{7,6},{8,9},{9,8},{10,11... | collective-permute-start | bytes 479240 | tf_op jit(solution)/shard_map/ppermute | solution.py:333
  37.0 0.9 %copy-start.4 = (f32[312,128]{1,0:T(8,128)}, f32[312,128]{1,0:T(8,128)S(1)}, u32[]{:S(2)}) copy-start(f32[312,128]{1,0:T(8,128)S(1)} %collective-permute-done.10.refs_3_) | copy-start | bytes 479236
  37.0 6.5 %collective-permute-start.5 = (f32[312,128]{1,0:T(8,128)S(1)}, f32[312,128]{1,0:T(8,128)S(1)}, u32[]{:S(2)}, u32[]{:S(2)}) collective-permute-start(f32[312,128]{1,0:T(8,128)S(1)} %collective-permute-done.4.refs_4_), channel_id=1, source_target_pairs={{0,1},{1,0},{2,3},{3,2},{4,5},{5,4},{6,7},{7,6},{8,9},{9,8},{10,11... | collective-permute-start | bytes 479240 | tf_op jit(solution)/shard_map/ppermute | solution.py:333
  37.1 0.8 %copy-start.5 = (f32[312,128]{1,0:T(8,128)}, f32[312,128]{1,0:T(8,128)S(1)}, u32[]{:S(2)}) copy-start(f32[312,128]{1,0:T(8,128)S(1)} %collective-permute-done.12.refs_5_) | copy-start | bytes 479236
  37.1 6.5 %collective-permute-start.7 = (f32[312,128]{1,0:T(8,128)S(1)}, f32[312,128]{1,0:T(8,128)S(1)}, u32[]{:S(2)}, u32[]{:S(2)}) collective-permute-start(f32[312,128]{1,0:T(8,128)S(1)} %collective-permute-done.6.refs_6_), channel_id=1, source_target_pairs={{0,1},{1,0},{2,3},{3,2},{4,5},{5,4},{6,7},{7,6},{8,9},{9,8},{10,11... | collective-permute-start | bytes 479240 | tf_op jit(solution)/shard_map/ppermute | solution.py:333
  37.9 0.7 %copy-start.6 = (f32[312,128]{1,0:T(8,128)}, f32[312,128]{1,0:T(8,128)S(1)}, u32[]{:S(2)}) copy-start(f32[312,128]{1,0:T(8,128)S(1)} %collective-permute-done.14.refs_7_) | copy-start | bytes 479236
  43.5 0.7 %copy-start.11 = (f32[312,128]{1,0:T(8,128)}, f32[312,128]{1,0:T(8,128)S(1)}, u32[]{:S(2)}) copy-start(f32[312,128]{1,0:T(8,128)S(1)} %collective-permute-done.1.refs_1_) | copy-start | bytes 479236
  43.5 0.7 %copy-start.12 = (f32[312,128]{1,0:T(8,128)}, f32[312,128]{1,0:T(8,128)S(1)}, u32[]{:S(2)}) copy-start(f32[312,128]{1,0:T(8,128)S(1)} %collective-permute-done.3.refs_3_) | copy-start | bytes 479236
  43.5 0.7 %copy-start.13 = (f32[312,128]{1,0:T(8,128)}, f32[312,128]{1,0:T(8,128)S(1)}, u32[]{:S(2)}) copy-start(f32[312,128]{1,0:T(8,128)S(1)} %collective-permute-done.5.refs_5_) | copy-start | bytes 479236
  43.5 0.8 %copy-start.14 = (f32[312,128]{1,0:T(8,128)}, f32[312,128]{1,0:T(8,128)S(1)}, u32[]{:S(2)}) copy-start(f32[312,128]{1,0:T(8,128)S(1)} %collective-permute-done.7.refs_7_) | copy-start | bytes 479236
where the time goes:
time: 52 us; the launch traced here: 51.8 us
  waiting for transfers between devices  21.1 us (41%)
  Pallas kernels  15.4 us (30%)
  starting transfers between devices  13.7 us (26%)
  local copies, waits for them, and re-layouts  1.44 us (3%)
    ppermute x15, waiting for transfers between devices, swap(): lax.ppermute(value, 'date', [(i, i ^ distance) for i in range(count)])  21.1 us
    ppermute x15, starting transfers between devices, swap(): lax.ppermute(value, 'date', [(i, i ^ distance) for i in range(count)])  13.7 us
    pallas_call x1, Pallas kernels, far_grams(): pl.pallas_call(body, grid=(out_rows,), in_specs=[whole_spec(block) for bl...  7.47 us
    pallas_call x1, Pallas kernels, near_grams(): pl.pallas_call(body, grid=(out_rows,), in_specs=[whole_spec(block) for bl...  4.91 us
    pallas_call x1, Pallas kernels, pack(): pl.pallas_call(functools.partial(pack_kernel, chips, groups, slab), grid=...  3.01 us
    unnamed x30, local copies, waits for them, and re-layouts  1.44 us
  transfers between devices with their start and end apart: 15, of which 5 were waited for; matrix products, arithmetic and copies ran while one was open for 0% of the time, Pallas kernels for 9%

commit v1 on v0

--- a/solution.py
+++ b/solution.py
@@ -23,14 +23,13 @@
     return high, low
 
 
-def windows(planes, group, first_row):
+def windows(planes, group, first):
     per_az = 2 * STEP_RG
     inside = lax.broadcasted_iota(jnp.int32, (PAD_AZ, LANES), 0) < BOX_AZ
     highs, lows = {}, {}
     for part in range(2):
         for col in range(STEP_RG):
-            start = first_row * per_az + part * STEP_RG + col
-            window = planes[group, pl.ds(start, PAD_AZ, stride=per_az), :]
+            window = planes[group, pl.ds(first + part * STEP_RG + col, PAD_AZ, stride=per_az), :]
             highs[part, col], lows[part, col] = split(jnp.where(inside, window, 0.0))
     return highs, lows
 
@@ -113,10 +112,10 @@
 
 
 def near_body(planes, out_ref, roots_ref, sums, groups):
-    first_row = pl.program_id(0) * STEP_AZ
+    first = pl.program_id(0) * (STEP_AZ * 2 * STEP_RG)
 
     def make(group):
-        pieces = windows(planes, group, first_row)
+        pieces = windows(planes, group, first)
         return products(pieces, [pieces])
 
     def finish(group, boxes):
@@ -127,15 +126,14 @@
     over_groups(groups, sums, make, finish)
 
 
-def far_body(far_half, planes, near_planes, near_ref, roots_ref, out_ref, sums, groups):
-    first_row = pl.program_id(0) * STEP_AZ
+def far_body(far_half, first, near_first, planes, near_planes, near_ref, roots_ref, out_ref, sums, groups):
     upper = far_half == 1
     far_rows = pl.ds(pl.multiple_of(far_half * LANES, LANES), LANES)
     near_rows = pl.ds(pl.multiple_of((1 - far_half) * LANES, LANES), LANES)
 
     def make(group):
-        pieces = windows(planes, group, first_row)
-        return products(pieces, [pieces, windows(near_planes, group, first_row)])
+        pieces = windows(planes, group, first)
+        return products(pieces, [pieces, windows(near_planes, group, near_first)])
 
     def finish(group, boxes):
         square, real, imag = boxes
@@ -163,16 +161,27 @@
     return [pltpu.VMEM((count, LANES, LANES), jnp.float32)] * 3
 
 
-def row_spec(*shape):
-    return pl.BlockSpec((1, *shape), lambda a: (a,) + (0,) * len(shape))
+def row_spec(*shape, row=lambda a, *_: a):
+    return pl.BlockSpec((1, *shape), lambda *at: (row(*at),) + (0,) * len(shape))
 
 
 def whole_spec(array):
-    return pl.BlockSpec(array.shape, lambda a: (0,) * len(array.shape))
+    return pl.BlockSpec(array.shape, lambda *_: (0,) * len(array.shape))
 
 
 def need_rows(out_rows):
     return (STEP_AZ * (out_rows - 1) + BOX_AZ) * 2 * STEP_RG
+
+
+def near_shapes(out_rows, groups):
+    return [
+        jax.ShapeDtypeStruct((out_rows, groups, LANES, LANES), jnp.bfloat16),
+        jax.ShapeDtypeStruct((out_rows, groups, 1, LANES), jnp.float32),
+    ]
+
+
+def near_specs(groups, **row):
+    return [row_spec(groups, LANES, LANES, **row), row_spec(groups, 1, LANES, **row)]
 
 
 def near_grams(blocks, out_rows, groups, slab):
@@ -181,7 +190,8 @@
 
         @pl.when(pl.program_id(0) == 0)
         def _():
-            assemble(block_refs, planes, groups, slab, need_rows(out_rows))
+            first = lax.rem(lax.axis_index("date"), CORES) * (slab * 2 * STEP_RG)
+            assemble(block_refs, [first] * len(blocks), planes, 0, groups, need_rows(out_rows))
 
         near_body(planes, out_ref, roots_ref, sums, groups)
 
@@ -190,38 +200,108 @@
         body,
         grid=(out_rows,),
         in_specs=[whole_spec(block) for block in blocks],
-        out_specs=[whole_spec(planes), row_spec(groups, LANES, LANES), row_spec(groups, 1, LANES)],
-        out_shape=[
-            planes,
-            jax.ShapeDtypeStruct((out_rows, groups, LANES, LANES), jnp.bfloat16),
-            jax.ShapeDtypeStruct((out_rows, groups, 1, LANES), jnp.float32),
-        ],
+        out_specs=[whole_spec(planes)] + near_specs(groups),
+        out_shape=[planes] + near_shapes(out_rows, groups),
         scratch_shapes=sums_scratch(1),
     )(*blocks)
 
 
-def far_grams(blocks, near, out_rows, groups, slab):
-    def body(*refs):
-        block_refs, (near_planes, near_ref, roots_ref, out_ref, planes, *sums) = refs[: len(blocks)], refs[len(blocks) :]
+PAD_ROWS = 4
+EDGE_AZ = STEP_AZ
+
+
+def far_sizes(slab):
+    per_az = 2 * STEP_RG
+    bulk = (slab + MARGIN - EDGE_AZ) * per_az
+    return EDGE_AZ * per_az, bulk, PAD_ROWS + (slab + MARGIN - BOX_AZ + EDGE_AZ + PAD_AZ) * per_az
+
+
+def place_of_device():
+    me = lax.axis_index("date")
+    return lax.rem(me // CORES, 2), lax.rem(me, CORES)
+
+
+def far_bulk(core_index, wide, tall, near, out_rows, groups, slab):
+    near_planes, _, _ = near
+    edge, bulk, rows = far_sizes(slab)
+    dates = 2 * LANES
+    per_az = 2 * STEP_RG
+    blocks = wide + tall
+
+    def row(a, core):
+        return a + 1 - core[0]
+
+    def body(core_ref, *refs):
+        block_refs, (near_planes_ref, near_ref, roots_ref, out_ref, planes, *sums) = refs[: len(blocks)], refs[len(blocks) :]
+        lane, core = place_of_device()
 
         @pl.when(pl.program_id(0) == 0)
         def _():
-            assemble(block_refs, planes, groups, slab, need_rows(out_rows))
-
+            inner = core * ((slab - EDGE_AZ) * per_az)
+            outer = lane * (CORES * slab * per_az) + edge + inner
+            firsts = [outer] * len(wide) + [inner] * len(tall)
+            assemble(block_refs, firsts, planes, PAD_ROWS + edge, groups, bulk)
+
+        a = pl.program_id(0)
         far_half = 1 - lax.axis_index("date") // groups
-        far_body(far_half, planes, near_planes, near_ref, roots_ref, out_ref, sums, groups)
-
-    near_planes, _, _ = near
-    dates = 2 * LANES
+        first = PAD_ROWS + edge + a * (STEP_AZ * per_az)
+        near_first = (a + 1 - core) * (STEP_AZ * per_az)
+        far_body(far_half, first, near_first, planes, near_planes_ref, near_ref, roots_ref, out_ref, sums, groups)
+
+    planes = jax.ShapeDtypeStruct((groups, rows, LANES), jnp.float32)
     return pl.pallas_call(
         body,
-        grid=(out_rows,),
-        in_specs=[whole_spec(block) for block in blocks]
-        + [whole_spec(near_planes), row_spec(groups, LANES, LANES), row_spec(groups, 1, LANES)],
-        out_specs=row_spec(groups, dates, dates),
-        out_shape=jax.ShapeDtypeStruct((out_rows, groups, dates, dates), jnp.bfloat16),
-        scratch_shapes=[pltpu.VMEM(near_planes.shape, jnp.float32)] + sums_scratch(3),
-    )(*blocks, *near)
+        grid_spec=pltpu.PrefetchScalarGridSpec(
+            num_scalar_prefetch=1,
+            grid=(out_rows - 1,),
+            in_specs=[whole_spec(block) for block in blocks] + [whole_spec(near_planes)] + near_specs(groups, row=row),
+            out_specs=[row_spec(groups, dates, dates, row=row), whole_spec(planes)],
+            scratch_shapes=sums_scratch(3),
+        ),
+        out_shape=[jax.ShapeDtypeStruct((out_rows, groups, dates, dates), jnp.bfloat16), planes],
+    )(core_index, *blocks, *near)
+
+
+def far_edge(core_index, wide, edges, bulk_made, near, out_rows, groups, slab):
+    near_planes, near_out, roots = near
+    out, planes = bulk_made
+    edge, bulk, _ = far_sizes(slab)
+    dates = 2 * LANES
+    per_az = 2 * STEP_RG
+    blocks = wide + edges
+
+    def row(a, core):
+        return (out_rows - 1) * core[0]
+
+    def body(core_ref, *refs):
+        block_refs = refs[: len(blocks)]
+        planes_ref, near_planes_ref, near_ref, roots_ref, _, out_ref, held, *sums = refs[len(blocks) :]
+        lane, core = place_of_device()
+        held[...] = planes_ref[...]
+        skipped = core * (edges[0].shape[0] - edge)
+        outer = lane * (CORES * slab * per_az) + core * ((CORES * slab + MARGIN - EDGE_AZ) * per_az)
+        firsts = [outer] * len(wide) + [skipped] * len(edges)
+        assemble(block_refs, firsts, held, PAD_ROWS + core * (edge + bulk), groups, edge)
+        far_half = 1 - lax.axis_index("date") // groups
+        first = PAD_ROWS + core * ((EDGE_AZ + slab + MARGIN - BOX_AZ) * per_az)
+        near_first = core * ((out_rows - 1) * STEP_AZ * per_az)
+        far_body(far_half, first, near_first, held, near_planes_ref, near_ref, roots_ref, out_ref, sums, groups)
+
+    return pl.pallas_call(
+        body,
+        grid_spec=pltpu.PrefetchScalarGridSpec(
+            num_scalar_prefetch=1,
+            grid=(1,),
+            in_specs=[whole_spec(block) for block in blocks]
+            + [whole_spec(planes), whole_spec(near_planes)]
+            + near_specs(groups, row=row)
+            + [pl.BlockSpec(memory_space=pl.ANY)],
+            out_specs=row_spec(groups, dates, dates, row=row),
+            scratch_shapes=[pltpu.VMEM(planes.shape, jnp.float32)] + sums_scratch(3),
+        ),
+        out_shape=jax.ShapeDtypeStruct(out.shape, out.dtype),
+        input_output_aliases={1 + len(blocks) + 4: 0},
+    )(core_index, *blocks, planes, near_planes, near_out, roots, out)
 
 
 def grams_of_planes(planes, out_rows):
@@ -232,34 +312,31 @@
         near_body(planes_ref, out_ref, roots_ref, sums, groups)
 
     def far(planes_ref, near_planes, near_ref, roots_ref, out_ref, *sums):
-        far_body(jnp.int32(1), planes_ref, near_planes, near_ref, roots_ref, out_ref, sums, groups)
-
-    kept = [row_spec(groups, LANES, LANES), row_spec(groups, 1, LANES)]
+        first = pl.program_id(0) * (STEP_AZ * 2 * STEP_RG)
+        far_body(jnp.int32(1), first, first, planes_ref, near_planes, near_ref, roots_ref, out_ref, sums, groups)
+
     near_out = pl.pallas_call(
         near,
         grid=(out_rows,),
         in_specs=[whole_spec(planes[0])],
-        out_specs=kept,
-        out_shape=[
-            jax.ShapeDtypeStruct((out_rows, groups, LANES, LANES), jnp.bfloat16),
-            jax.ShapeDtypeStruct((out_rows, groups, 1, LANES), jnp.float32),
-        ],
+        out_specs=near_specs(groups),
+        out_shape=near_shapes(out_rows, groups),
         scratch_shapes=sums_scratch(1),
     )(planes[0])
     return pl.pallas_call(
         far,
         grid=(out_rows,),
-        in_specs=[whole_spec(planes[1]), whole_spec(planes[0])] + kept,
+        in_specs=[whole_spec(planes[1]), whole_spec(planes[0])] + near_specs(groups),
         out_specs=row_spec(groups, dates, dates),
         out_shape=jax.ShapeDtypeStruct((out_rows, groups, dates, dates), jnp.bfloat16),
         scratch_shapes=sums_scratch(3),
     )(planes[1], planes[0], *near_out)
 
 
-def pack_kernel(chips, groups, slab, x0_ref, x1_ref, *rest):
-    out_refs, (rows_ref, sems) = rest[:chips], rest[chips:]
+def pack_kernel(chips, groups, slab, x0_ref, x1_ref, *refs):
+    (*out_refs, rows_ref, stage_ref, sems) = refs
     me = lax.axis_index("date")
-    chip, slot = me // CORES, lax.rem(me, groups)
+    chip, core, slot = me // CORES, lax.rem(me, CORES), lax.rem(me, groups)
     width = groups * STEP_RG
     dates = LANES // groups
     per_az = 2 * STEP_RG
@@ -278,14 +355,32 @@
                 turned = jnp.concatenate(pieces, axis=0).T
                 rows_ref[pl.ds(first * per_az + at, count, stride=per_az), :] = turned[:count]
     chip_rows = CORES * slab * per_az
+    edge_rows = out_refs[-1].shape[0]
+    bulk_rows = stage_ref.shape[1]
     copies = []
-    for step in range(chips):
-        start = pl.multiple_of(jnp.bitwise_xor(chip, step) * chip_rows, 8)
-        copy = pltpu.make_async_copy(
-            rows_ref.at[pl.ds(start, chip_rows + MARGIN * per_az), :], out_refs[step], sems.at[step]
-        )
+
+    def send(source, target):
+        copy = pltpu.make_async_copy(source, target, sems.at[len(copies)])
         copy.start()
         copies.append(copy)
+
+    def rows_of(start, target):
+        return rows_ref.at[pl.ds(pl.multiple_of(start, 8), target.shape[0]), :]
+
+    plane = chips // 2
+    near_refs = out_refs[1 : 1 + plane]
+    plane_ref, bulk_refs, edge_refs = out_refs[0], out_refs[1 + plane : 3 + plane], out_refs[3 + plane :]
+    send(rows_of(jnp.bitwise_xor(chip, plane) // 2 * (2 * chip_rows), plane_ref), plane_ref)
+    for step, out_ref in enumerate(near_refs):
+        send(rows_of(jnp.bitwise_xor(chip, step) * chip_rows, out_ref), out_ref)
+    for i, out_ref in enumerate(bulk_refs):
+        start = jnp.bitwise_xor(chip, chips - 2 + i) * chip_rows
+        stage_ref[i] = rows_ref[pl.ds(start + EDGE_AZ * per_az, bulk_rows), :]
+        send(stage_ref.at[i], out_ref)
+        for crossed in range(CORES):
+            target = edge_refs[CORES * i + crossed]
+            far_end = jnp.bitwise_xor(core, crossed) * (chip_rows + MARGIN * per_az - edge_rows)
+            send(rows_of(start + far_end, target), target)
     for copy in copies:
         copy.wait()
 
@@ -293,39 +388,42 @@
 def pack(flat, chips, groups, slab):
     per_az = 2 * STEP_RG
     azimuths = chips * CORES * slab
-    rows = (CORES * slab + MARGIN) * per_az
+    chip_az = CORES * slab
+    edge = EDGE_AZ * per_az + PAD_ROWS
+    bulk = (chip_az + MARGIN - 2 * EDGE_AZ) * per_az
+    counts = [(2 * chip_az + MARGIN) * per_az] + [(chip_az + MARGIN) * per_az] * (chips // 2) + [bulk] * 2 + [edge] * 4
     spec0 = pl.BlockSpec((flat.shape[0], LANES), lambda i: (0, 0))
     spec1 = pl.BlockSpec((flat.shape[0], LANES), lambda i: (0, 1))
-    return pl.pallas_call(
+    made = pl.pallas_call(
         functools.partial(pack_kernel, chips, groups, slab),
         grid=(1,),
         in_specs=[spec0, spec1],
-        out_specs=[pl.BlockSpec(memory_space=pl.ANY)] * chips,
-        out_shape=[jax.ShapeDtypeStruct((rows, LANES), jnp.float32)] * chips,
+        out_specs=[pl.BlockSpec(memory_space=pl.ANY)] * len(counts),
+        out_shape=[jax.ShapeDtypeStruct((count, LANES), jnp.float32) for count in counts],
         scratch_shapes=[
             pltpu.VMEM(((azimuths + MARGIN) * per_az, LANES), jnp.float32),
-            pltpu.SemaphoreType.DMA((chips,)),
+            pltpu.VMEM((2, bulk, LANES), jnp.float32),
+            pltpu.SemaphoreType.DMA((len(counts),)),
         ],
     )(flat, flat)
-
-
-def assemble(blocks, planes, groups, slab, need):
-    me = lax.axis_index("date")
-    slot = lax.rem(me, groups)
+    return made[0], made[1 : 1 + chips // 2], made[1 + chips // 2 : 3 + chips // 2], made[3 + chips // 2 :]
+
+
+def assemble(blocks, firsts, planes, at, groups, need):
+    slot = lax.rem(lax.axis_index("date"), groups)
     width = LANES // groups
     place = lax.broadcasted_iota(jnp.int32, (8, LANES), 1) // width
     held = [lax.rem(place - jnp.bitwise_xor(slot, source) + groups, groups) for source in range(groups)]
-    first = lax.rem(me, CORES) * (slab * 2 * STEP_RG)
     starts = [8 * i for i in range(need // 8)] + ([need - 8] if need % 8 else [])
     for start in starts:
-        loaded = [block[pl.ds(first + start, 8), :] for block in blocks]
+        loaded = [block[pl.ds(first + start, 8), :] for block, first in zip(blocks, firsts)]
         for group in range(groups):
             merged = loaded[0]
             for source in range(1, groups):
                 merged = jnp.where(held[source] == group, loaded[source], merged)
             if group:
                 merged = pltpu.roll(merged, LANES - width * group, 1)
-            planes[group, pl.ds(start, 8), :] = merged
+            planes[group, pl.ds(at + start, 8), :] = merged
 
 
 def swap(value, distance):
@@ -333,25 +431,32 @@
     return lax.ppermute(value, "date", [(i, i ^ distance) for i in range(count)])
 
 
-def legs_in_order(chips):
-    far = [step for step in range(chips // 2, chips) if step % 2 == 0]
-    rest = [step for step in range(chips // 2, chips) if step % 2]
-    near = list(range(2, chips // 2)) + [1]
-    return far + near + rest
-
-
 def by_chips(slc, slab, out_rows, groups):
     chips = lax.axis_size("date") // CORES
+    plane = chips // 2
+
+    core_index = lax.rem(lax.axis_index("date"), CORES).reshape(1)
     flat = jnp.swapaxes(slc, 2, 3).reshape(-1, slc.shape[2])
-    sent = pack(flat, chips, groups, slab)
-    arrived = {0: sent[0]}
-    for step in legs_in_order(chips):
-        arrived[step] = swap(sent[step], CORES * step)
-    blocks = []
-    for step in range(chips):
-        blocks += [arrived[step], swap(arrived[step], 1)]
-    near = near_grams(blocks[:groups], out_rows, groups, slab)
-    return far_grams(blocks[groups:], near, out_rows, groups, slab)
+    wide_sent, near_sent, bulk_sent, edge_sent = pack(flat, chips, groups, slab)
+    wide = swap(wide_sent, CORES * plane)
+    near_legs = [near_sent[0]] + [swap(near_sent[i], CORES * i) for i in range(1, plane)]
+    bulks = [swap(bulk_sent[i], CORES * (chips - 2 + i)) for i in range(2)]
+    edges = []
+    for i in range(2):
+        for crossed in range(CORES):
+            distance = CORES * (chips - 2 + i) + crossed
+            edges.append(swap(edge_sent[CORES * i + crossed], distance))
+    passed = swap(wide, CORES)
+
+    def paired(value):
+        return [value, swap(value, 1)]
+
+    near_blocks = [block for i in range(plane) for block in paired(near_legs[i])]
+    wides = paired(wide) + paired(passed)
+    talls = paired(bulks[0]) + paired(bulks[1])
+    near = near_grams(near_blocks, out_rows, groups, slab)
+    made = far_bulk(core_index, wides, talls, near, out_rows, groups, slab)
+    return far_edge(core_index, wides, edges, made, near, out_rows, groups, slab)
 
 
 def by_slabs(slc, slab, out_rows, groups):

time: 52 us -> 68.6 us (1.32)
  the two profiles are of different devices: /device:TPU:9 before, /device:TPU:1 now
where the time goes in v1:
time: 68.6 us; the launch traced here: 68.2 us
  starting transfers between devices  33.2 us (48%)
  Pallas kernels  18.9 us (28%)
  waiting for transfers between devices  14.6 us (21%)
  local copies, waits for them, and re-layouts  1.29 us (2%)
    ppermute x19, starting transfers between devices, swap(): lax.ppermute(value, 'date', [(i, i ^ distance) for i in range(count)])  33.2 us
    ppermute x19, waiting for transfers between devices, swap(): lax.ppermute(value, 'date', [(i, i ^ distance) for i in range(count)])  14.6 us
    pallas_call x1, Pallas kernels, far_bulk(): pl.pallas_call(body, grid_spec=pltpu.PrefetchScalarGridSpec(num_scalar_pr...  6.32 us
    pallas_call x1, Pallas kernels, near_grams(): pl.pallas_call(body, grid=(out_rows,), in_specs=[whole_spec(block) for bl...  4.91 us
    pallas_call x1, Pallas kernels, far_edge(): pl.pallas_call(body, grid_spec=pltpu.PrefetchScalarGridSpec(num_scalar_pr...  4.69 us
    pallas_call x1, Pallas kernels, pack(): pl.pallas_call(functools.partial(pack_kernel, chips, groups, slab), grid=...  3.02 us
  transfers between devices with their start and end apart: 19, of which 2 were waited for; matrix products, arithmetic and copies ran while one was open for 0% of the time, Pallas kernels for 16%

profile of v1, /device:TPU:1, one launch (start us, length us, event | category | flops | bytes accessed | tf_op | source)
XLA Modules:
  0.0 68.2 jit_solution(10957403120065623064)
XLA Ops:
  0.0 3.0 %shard_map.17 = (f32[528,128]{1,0:T(8,128)}, f32[312,128]{1,0:T(8,128)}, f32[312,128]{1,0:T(8,128)}, f32[312,128]{1,0:T(8,128)}, f32[312,128]{1,0:T(8,128)}, /*i...) custom-call(f32[1536,144]{1,0:T(8,128)} %bitcast.4, ...), custom_call_target="tpu_custom_call" | custom-call | tf_op jit(solution)/shard_map/pallas_call | solution.py:397
  3.0 3.2 %collective-permute-start = (f32[528,128]{1,0:T(8,128)}, f32[528,128]{1,0:T(8,128)S(1)}, u32[]{:S(2)}, u32[]{:S(2)}) collective-permute-start(f32[528,128]{1,0:T(8,128)} %get-tuple-element.21), channel_id=1, source_target_pairs={{0,8},{1,9},{2,10},{3,11},{4,12},{5,13},{6,14},{7,15},{8,0},{9,1},... | collective-permute-start | bytes 811016 | tf_op jit(solution)/shard_map/ppermute | solution.py:431
  6.2 1.1 %collective-permute-start.8 = (f32[240,128]{1,0:T(8,128)}, f32[240,128]{1,0:T(8,128)S(1)}, u32[]{:S(2)}, u32[]{:S(2)}) collective-permute-start(f32[240,128]{1,0:T(8,128)} %get-tuple-element.26), channel_id=1, source_target_pairs={{0,12},{1,13},{2,14},{3,15},{4,8},{5,9},{6,10},{7,11},{8,4},{9,5},... | collective-permute-start | bytes 368648 | tf_op jit(solution)/shard_map/ppermute | solution.py:431
  7.3 13.7 %collective-permute-done.refs_0_ = f32[528,128]{1,0:T(8,128)S(1)} collective-permute-done((f32[528,128]{1,0:T(8,128)}, f32[528,128]{1,0:T(8,128)S(1)}, u32[]{:S(2)}, u32[]{:S(2)}) %collective-permute-start) | collective-permute-done | bytes 270368 | tf_op jit(solution)/shard_map/ppermute | solution.py:431
  21.0 1.0 %collective-permute-start.2 = (f32[528,128]{1,0:T(8,128)S(1)}, f32[528,128]{1,0:T(8,128)S(1)}, u32[]{:S(2)}, u32[]{:S(2)}) collective-permute-start(f32[528,128]{1,0:T(8,128)S(1)} %collective-permute-done.refs_0_), channel_id=1, source_target_pairs={{0,2},{1,3},{2,0},{3,1},{4,6},{5,7},{6,4},{7,5},{8,10},{9,11},{10,... | collective-permute-start | bytes 811016 | tf_op jit(solution)/shard_map/ppermute | solution.py:431
  22.1 4.2 %collective-permute-start.10 = (f32[240,128]{1,0:T(8,128)}, f32[240,128]{1,0:T(8,128)S(1)}, u32[]{:S(2)}, u32[]{:S(2)}) collective-permute-start(f32[240,128]{1,0:T(8,128)} %get-tuple-element.27), channel_id=1, source_target_pairs={{0,14},{1,15},{2,12},{3,13},{4,10},{5,11},{6,8},{7,9},{8,6},{9,7},... | collective-permute-start | bytes 368648 | tf_op jit(solution)/shard_map/ppermute | solution.py:431
  26.2 1.2 %collective-permute-start.13 = (f32[312,128]{1,0:T(8,128)}, f32[312,128]{1,0:T(8,128)S(1)}, u32[]{:S(2)}, u32[]{:S(2)}) collective-permute-start(f32[312,128]{1,0:T(8,128)} %get-tuple-element.29), channel_id=1, source_target_pairs={{0,2},{1,3},{2,0},{3,1},{4,6},{5,7},{6,4},{7,5},{8,10},{9,11},{10,... | collective-permute-start | bytes 479240 | tf_op jit(solution)/shard_map/ppermute | solution.py:431
  27.5 0.0 collective-permute-start.15
  27.5 0.0 collective-permute-done.8.refs_4_
  27.5 1.4 %collective-permute-start.17 = (f32[312,128]{1,0:T(8,128)}, f32[312,128]{1,0:T(8,128)S(1)}, u32[]{:S(2)}, u32[]{:S(2)}) collective-permute-start(f32[312,128]{1,0:T(8,128)} %get-tuple-element.31), channel_id=1, source_target_pairs={{0,6},{1,7},{2,4},{3,5},{4,2},{5,3},{6,0},{7,1},{8,14},{9,15},{10,... | collective-permute-start | bytes 479240 | tf_op jit(solution)/shard_map/ppermute | solution.py:431
  28.9 0.0 collective-permute-done.10.refs_6_
  28.9 5.2 %collective-permute-start.12 = (f32[312,128]{1,0:T(8,128)}, f32[312,128]{1,0:T(8,128)S(1)}, u32[]{:S(2)}, u32[]{:S(2)}) collective-permute-start(f32[312,128]{1,0:T(8,128)} %get-tuple-element.28.refs_0_), channel_id=1, source_target_pairs={{0,1},{1,0},{2,3},{3,2},{4,5},{5,4},{6,7},{7,6},{8,9},{9,8},{10,11... | collective-permute-start | bytes 479240 | tf_op jit(solution)/shard_map/ppermute | solution.py:431
  34.1 0.0 collective-permute-done.13.refs_2_
  34.1 5.3 %collective-permute-start.9 = (f32[240,128]{1,0:T(8,128)S(1)}, f32[240,128]{1,0:T(8,128)S(1)}, u32[]{:S(2)}, u32[]{:S(2)}) collective-permute-start(f32[240,128]{1,0:T(8,128)S(1)} %collective-permute-done.8.refs_4_), channel_id=1, source_target_pairs={{0,1},{1,0},{2,3},{3,2},{4,5},{5,4},{6,7},{7,6},{8,9},{9,8},{10,11... | collective-permute-start | bytes 368648 | tf_op jit(solution)/shard_map/ppermute | solution.py:431
  39.4 0.0 collective-permute-done.15.refs_4_
  39.4 0.1 collective-permute-start.11
  39.5 0.0 collective-permute-done.17.refs_6_
  39.5 0.4 collective-permute-start.1
  40.0 0.0 collective-permute-done.2.refs_2_
  40.0 0.1 collective-permute-start.3
  40.0 0.0 collective-permute-done.12.refs_1_
  40.0 0.4 collective-permute-start.14
  40.5 0.0 collective-permute-done.9.refs_5_
  40.5 0.3 collective-permute-start.16
  40.8 0.0 collective-permute-done.11.refs_7_
  40.8 0.2 collective-permute-start.18
  41.0 0.8 %collective-permute-done.14.refs_3_ = f32[312,128]{1,0:T(8,128)S(1)} collective-permute-done((f32[312,128]{1,0:T(8,128)S(1)}, f32[312,128]{1,0:T(8,128)S(1)}, u32[]{:S(2)}, u32[]{:S(2)}) %collective-permute-start.14) | collective-permute-done | bytes 159776 | tf_op jit(solution)/shard_map/ppermute | solution.py:431
  41.8 4.0 %collective-permute-start.4 = (f32[40,128]{1,0:T(8,128)}, f32[40,128]{1,0:T(8,128)S(1)}, u32[]{:S(2)}, u32[]{:S(2)}) collective-permute-start(f32[40,128]{1,0:T(8,128)} %get-tuple-element.22), channel_id=1, source_target_pairs={{0,12},{1,13},{2,14},{3,15},{4,8},{5,9},{6,10},{7,11},{8,4},{9,5},... | collective-permute-start | bytes 61448 | tf_op jit(solution)/shard_map/ppermute | solution.py:431
  45.8 0.0 collective-permute-done.16.refs_5_
  45.8 0.4 collective-permute-start.5
  46.2 0.0 collective-permute-done.18.refs_7_
  46.2 4.3 %collective-permute-start.6 = (f32[40,128]{1,0:T(8,128)}, f32[40,128]{1,0:T(8,128)S(1)}, u32[]{:S(2)}, u32[]{:S(2)}) collective-permute-start(f32[40,128]{1,0:T(8,128)} %get-tuple-element.24), channel_id=1, source_target_pairs={{0,14},{1,15},{2,12},{3,13},{4,10},{5,11},{6,8},{7,9},{8,6},{9,7},... | collective-permute-start | bytes 61448 | tf_op jit(solution)/shard_map/ppermute | solution.py:431
  50.5 0.0 collective-permute-done.1.refs_1_
  50.5 0.3 collective-permute-start.7
  50.8 0.0 copy-done.4
  50.8 0.0 copy-done.5
  50.8 0.0 copy-done.6
  50.8 0.0 copy-done.7
  50.9 0.0 copy-done.8
  50.9 0.0 copy-done.9
  50.9 0.0 copy-done.10
  50.9 4.9 %shard_map.18 = (f32[8,264,128]{2,1,0:T(8,128)}, bf16[3,8,128,128]{3,2,1,0:T(8,128)(2,1)}, f32[3,8,1,128]{3,2,1,0:T(1,128)}) custom-call(f32[312,128]{1,0:T(8,128)} %get-tuple-element.28.refs_0_, f32[312,128]{1,0:T(8,128)} %copy-done.7, f32[312,128]{1,0:T(8,128)} %copy-done.4, f32[312,128]{1,0:T(8,128)} %copy-done.8, f32[312,128]{1,0:T(8,128)} %copy-done.5, ...), custom_call_target="tpu_custom_call" | custom-call | tf_op jit(solution)/shard_map/pallas_call | solution.py:199
  55.8 0.0 collective-permute-done.3.refs_3_
  55.8 0.0 copy-start.3
  55.8 0.0 copy-done
  55.8 0.0 copy-done.11
  55.8 0.0 copy-done.12
  55.8 0.0 copy-done.1
  55.9 0.0 copy-done.13
  55.9 0.0 copy-done.14
  55.9 0.0 copy-done.2
  55.9 0.6 copy-done.3
  56.5 6.3 %shard_map.19 = (bf16[3,8,256,256]{3,2,1,0:T(8,128)(2,1)}, f32[8,304,128]{2,1,0:T(8,128)}) custom-call(s32[1]{0:T(128)} %bitcast.core_ref, f32[528,128]{1,0:T(8,128)} %copy-done, f32[528,128]{1,0:T(8,128)} %copy-done.2, f32[528,128]{1,0:T(8,128)} %copy-done.1, f32[528,128]{1,0:T(8,128)} %copy-done.3, f32[240,128]{1,0:T(8,128)} %copy-done.11, ...), custom_call_target="tpu_custom_call" | custom-call | tf_op jit(solution)/shard_map/pallas_call | solution.py:252
  62.8 0.0 collective-permute-done.4.refs_4_
  62.8 0.0 copy-start.15
  62.9 0.0 collective-permute-done.5.refs_5_
  62.9 0.0 copy-start.16
  62.9 0.0 collective-permute-done.6.refs_6_
  62.9 0.0 collective-permute-done.7.refs_7_
  62.9 0.5 copy-done.15
  63.5 0.0 copy-done.16
  63.5 0.0 copy-done.17
  63.5 0.0 copy-done.18
  63.5 4.7 %shard_map.20 = bf16[3,8,256,256]{3,2,1,0:T(8,128)(2,1)} custom-call(s32[1]{0:T(128)} %bitcast.core_ref, f32[528,128]{1,0:T(8,128)} %copy-done, f32[528,128]{1,0:T(8,128)} %copy-done.2, f32[528,128]{1,0:T(8,128)} %copy-done.1, f32[528,128]{1,0:T(8,128)} %copy-done.3, f32[40,128]{1,0:T(8,128)} %copy-done.15, ...), custom_call_target="tpu_custom_call", output_to_operand_aliasing={{}: (13, {})} | custom-call | tf_op jit(solution)/shard_map/pallas_call | solution.py:290
  (16 shorter events, 0.0 us)
Async XLA Ops:
  3.0 18.0 %collective-permute-start = (f32[528,128]{1,0:T(8,128)}, f32[528,128]{1,0:T(8,128)S(1)}, u32[]{:S(2)}, u32[]{:S(2)}) collective-permute-start(f32[528,128]{1,0:T(8,128)} %get-tuple-element.21), channel_id=1, source_target_pairs={{0,8},{1,9},{2,10},{3,11},{4,12},{5,13},{6,14},{7,15},{8,0},{9,1},... | collective-permute-start | bytes 811016 | tf_op jit(solution)/shard_map/ppermute | solution.py:431
  6.2 21.3 %collective-permute-start.8 = (f32[240,128]{1,0:T(8,128)}, f32[240,128]{1,0:T(8,128)S(1)}, u32[]{:S(2)}, u32[]{:S(2)}) collective-permute-start(f32[240,128]{1,0:T(8,128)} %get-tuple-element.26), channel_id=1, source_target_pairs={{0,12},{1,13},{2,14},{3,15},{4,8},{5,9},{6,10},{7,11},{8,4},{9,5},... | collective-permute-start | bytes 368648 | tf_op jit(solution)/shard_map/ppermute | solution.py:431
  21.0 34.8 %copy-start = (f32[528,128]{1,0:T(8,128)}, f32[528,128]{1,0:T(8,128)S(1)}, u32[]{:S(2)}) copy-start(f32[528,128]{1,0:T(8,128)S(1)} %collective-permute-done.refs_0_) | copy-start | bytes 811012
  21.0 18.9 %collective-permute-start.2 = (f32[528,128]{1,0:T(8,128)S(1)}, f32[528,128]{1,0:T(8,128)S(1)}, u32[]{:S(2)}, u32[]{:S(2)}) collective-permute-start(f32[528,128]{1,0:T(8,128)S(1)} %collective-permute-done.refs_0_), channel_id=1, source_target_pairs={{0,2},{1,3},{2,0},{3,1},{4,6},{5,7},{6,4},{7,5},{8,10},{9,11},{10,... | collective-permute-start | bytes 811016 | tf_op jit(solution)/shard_map/ppermute | solution.py:431
  22.1 6.8 %collective-permute-start.10 = (f32[240,128]{1,0:T(8,128)}, f32[240,128]{1,0:T(8,128)S(1)}, u32[]{:S(2)}, u32[]{:S(2)}) collective-permute-start(f32[240,128]{1,0:T(8,128)} %get-tuple-element.27), channel_id=1, source_target_pairs={{0,14},{1,15},{2,12},{3,13},{4,10},{5,11},{6,8},{7,9},{8,6},{9,7},... | collective-permute-start | bytes 368648 | tf_op jit(solution)/shard_map/ppermute | solution.py:431
  26.2 7.8 %collective-permute-start.13 = (f32[312,128]{1,0:T(8,128)}, f32[312,128]{1,0:T(8,128)S(1)}, u32[]{:S(2)}, u32[]{:S(2)}) collective-permute-start(f32[312,128]{1,0:T(8,128)} %get-tuple-element.29), channel_id=1, source_target_pairs={{0,2},{1,3},{2,0},{3,1},{4,6},{5,7},{6,4},{7,5},{8,10},{9,11},{10,... | collective-permute-start | bytes 479240 | tf_op jit(solution)/shard_map/ppermute | solution.py:431
  27.5 11.9 %collective-permute-start.15 = (f32[312,128]{1,0:T(8,128)}, f32[312,128]{1,0:T(8,128)S(1)}, u32[]{:S(2)}, u32[]{:S(2)}) collective-permute-start(f32[312,128]{1,0:T(8,128)} %get-tuple-element.30), channel_id=1, source_target_pairs={{0,4},{1,5},{2,6},{3,7},{4,0},{5,1},{6,2},{7,3},{8,12},{9,13},{10,... | collective-permute-start | bytes 479240 | tf_op jit(solution)/shard_map/ppermute | solution.py:431
  27.5 28.3 %copy-start.11 = (f32[240,128]{1,0:T(8,128)}, f32[240,128]{1,0:T(8,128)S(1)}, u32[]{:S(2)}) copy-start(f32[240,128]{1,0:T(8,128)S(1)} %collective-permute-done.8.refs_4_) | copy-start | bytes 368644
  27.5 12.0 %collective-permute-start.17 = (f32[312,128]{1,0:T(8,128)}, f32[312,128]{1,0:T(8,128)S(1)}, u32[]{:S(2)}, u32[]{:S(2)}) collective-permute-start(f32[312,128]{1,0:T(8,128)} %get-tuple-element.31), channel_id=1, source_target_pairs={{0,6},{1,7},{2,4},{3,5},{4,2},{5,3},{6,0},{7,1},{8,14},{9,15},{10,... | collective-permute-start | bytes 479240 | tf_op jit(solution)/shard_map/ppermute | solution.py:431
  28.9 26.9 %copy-start.12 = (f32[240,128]{1,0:T(8,128)}, f32[240,128]{1,0:T(8,128)S(1)}, u32[]{:S(2)}) copy-start(f32[240,128]{1,0:T(8,128)S(1)} %collective-permute-done.10.refs_6_) | copy-start | bytes 368644
  28.9 11.1 %collective-permute-start.12 = (f32[312,128]{1,0:T(8,128)}, f32[312,128]{1,0:T(8,128)S(1)}, u32[]{:S(2)}, u32[]{:S(2)}) collective-permute-start(f32[312,128]{1,0:T(8,128)} %get-tuple-element.28.refs_0_), channel_id=1, source_target_pairs={{0,1},{1,0},{2,3},{3,2},{4,5},{5,4},{6,7},{7,6},{8,9},{9,8},{10,11... | collective-permute-start | bytes 479240 | tf_op jit(solution)/shard_map/ppermute | solution.py:431
  34.1 16.8 %copy-start.4 = (f32[312,128]{1,0:T(8,128)}, f32[312,128]{1,0:T(8,128)S(1)}, u32[]{:S(2)}) copy-start(f32[312,128]{1,0:T(8,128)S(1)} %collective-permute-done.13.refs_2_) | copy-start | bytes 479236
  34.1 6.4 %collective-permute-start.9 = (f32[240,128]{1,0:T(8,128)S(1)}, f32[240,128]{1,0:T(8,128)S(1)}, u32[]{:S(2)}, u32[]{:S(2)}) collective-permute-start(f32[240,128]{1,0:T(8,128)S(1)} %collective-permute-done.8.refs_4_), channel_id=1, source_target_pairs={{0,1},{1,0},{2,3},{3,2},{4,5},{5,4},{6,7},{7,6},{8,9},{9,8},{10,11... | collective-permute-start | bytes 368648 | tf_op jit(solution)/shard_map/ppermute | solution.py:431
  39.4 11.4 %copy-start.5 = (f32[312,128]{1,0:T(8,128)}, f32[312,128]{1,0:T(8,128)S(1)}, u32[]{:S(2)}) copy-start(f32[312,128]{1,0:T(8,128)S(1)} %collective-permute-done.15.refs_4_) | copy-start | bytes 479236
  39.4 1.3 %collective-permute-start.11 = (f32[240,128]{1,0:T(8,128)S(1)}, f32[240,128]{1,0:T(8,128)S(1)}, u32[]{:S(2)}, u32[]{:S(2)}) collective-permute-start(f32[240,128]{1,0:T(8,128)S(1)} %collective-permute-done.10.refs_6_), channel_id=1, source_target_pairs={{0,1},{1,0},{2,3},{3,2},{4,5},{5,4},{6,7},{7,6},{8,9},{9,8},{10,11... | collective-permute-start | bytes 368648 | tf_op jit(solution)/shard_map/ppermute | solution.py:431
  39.5 11.3 %copy-start.6 = (f32[312,128]{1,0:T(8,128)}, f32[312,128]{1,0:T(8,128)S(1)}, u32[]{:S(2)}) copy-start(f32[312,128]{1,0:T(8,128)S(1)} %collective-permute-done.17.refs_6_) | copy-start | bytes 479236
  39.5 11.0 %collective-permute-start.1 = (f32[528,128]{1,0:T(8,128)S(1)}, f32[528,128]{1,0:T(8,128)S(1)}, u32[]{:S(2)}, u32[]{:S(2)}) collective-permute-start(f32[528,128]{1,0:T(8,128)S(1)} %collective-permute-done.refs_0_), channel_id=1, source_target_pairs={{0,1},{1,0},{2,3},{3,2},{4,5},{5,4},{6,7},{7,6},{8,9},{9,8},{10,11... | collective-permute-start | bytes 811016 | tf_op jit(solution)/shard_map/ppermute | solution.py:431
  40.0 15.9 %copy-start.1 = (f32[528,128]{1,0:T(8,128)}, f32[528,128]{1,0:T(8,128)S(1)}, u32[]{:S(2)}) copy-start(f32[528,128]{1,0:T(8,128)S(1)} %collective-permute-done.2.refs_2_) | copy-start | bytes 811012
  40.0 15.8 %collective-permute-start.3 = (f32[528,128]{1,0:T(8,128)S(1)}, f32[528,128]{1,0:T(8,128)S(1)}, u32[]{:S(2)}, u32[]{:S(2)}) collective-permute-start(f32[528,128]{1,0:T(8,128)S(1)} %collective-permute-done.2.refs_2_), channel_id=1, source_target_pairs={{0,1},{1,0},{2,3},{3,2},{4,5},{5,4},{6,7},{7,6},{8,9},{9,8},{10,11... | collective-permute-start | bytes 811016 | tf_op jit(solution)/shard_map/ppermute | solution.py:431
  40.0 10.8 %copy-start.7 = (f32[312,128]{1,0:T(8,128)}, f32[312,128]{1,0:T(8,128)S(1)}, u32[]{:S(2)}) copy-start(f32[312,128]{1,0:T(8,128)S(1)} %collective-permute-done.12.refs_1_) | copy-start | bytes 479236
  40.0 1.7 %collective-permute-start.14 = (f32[312,128]{1,0:T(8,128)S(1)}, f32[312,128]{1,0:T(8,128)S(1)}, u32[]{:S(2)}, u32[]{:S(2)}) collective-permute-start(f32[312,128]{1,0:T(8,128)S(1)} %collective-permute-done.13.refs_2_), channel_id=1, source_target_pairs={{0,1},{1,0},{2,3},{3,2},{4,5},{5,4},{6,7},{7,6},{8,9},{9,8},{10,11... | collective-permute-start | bytes 479240 | tf_op jit(solution)/shard_map/ppermute | solution.py:431
  40.5 15.4 %copy-start.13 = (f32[240,128]{1,0:T(8,128)}, f32[240,128]{1,0:T(8,128)S(1)}, u32[]{:S(2)}) copy-start(f32[240,128]{1,0:T(8,128)S(1)} %collective-permute-done.9.refs_5_) | copy-start | bytes 368644
  40.5 5.3 %collective-permute-start.16 = (f32[312,128]{1,0:T(8,128)S(1)}, f32[312,128]{1,0:T(8,128)S(1)}, u32[]{:S(2)}, u32[]{:S(2)}) collective-permute-start(f32[312,128]{1,0:T(8,128)S(1)} %collective-permute-done.15.refs_4_), channel_id=1, source_target_pairs={{0,1},{1,0},{2,3},{3,2},{4,5},{5,4},{6,7},{7,6},{8,9},{9,8},{10,11... | collective-permute-start | bytes 479240 | tf_op jit(solution)/shard_map/ppermute | solution.py:431
  40.8 15.1 %copy-start.14 = (f32[240,128]{1,0:T(8,128)}, f32[240,128]{1,0:T(8,128)S(1)}, u32[]{:S(2)}) copy-start(f32[240,128]{1,0:T(8,128)S(1)} %collective-permute-done.11.refs_7_) | copy-start | bytes 368644
  40.8 5.5 %collective-permute-start.18 = (f32[312,128]{1,0:T(8,128)S(1)}, f32[312,128]{1,0:T(8,128)S(1)}, u32[]{:S(2)}, u32[]{:S(2)}) collective-permute-start(f32[312,128]{1,0:T(8,128)S(1)} %collective-permute-done.17.refs_6_), channel_id=1, source_target_pairs={{0,1},{1,0},{2,3},{3,2},{4,5},{5,4},{6,7},{7,6},{8,9},{9,8},{10,11... | collective-permute-start | bytes 479240 | tf_op jit(solution)/shard_map/ppermute | solution.py:431
  41.8 9.1 %copy-start.8 = (f32[312,128]{1,0:T(8,128)}, f32[312,128]{1,0:T(8,128)S(1)}, u32[]{:S(2)}) copy-start(f32[312,128]{1,0:T(8,128)S(1)} %collective-permute-done.14.refs_3_) | copy-start | bytes 479236
  41.8 21.1 %collective-permute-start.4 = (f32[40,128]{1,0:T(8,128)}, f32[40,128]{1,0:T(8,128)S(1)}, u32[]{:S(2)}, u32[]{:S(2)}) collective-permute-start(f32[40,128]{1,0:T(8,128)} %get-tuple-element.22), channel_id=1, source_target_pairs={{0,12},{1,13},{2,14},{3,15},{4,8},{5,9},{6,10},{7,11},{8,4},{9,5},... | collective-permute-start | bytes 61448 | tf_op jit(solution)/shard_map/ppermute | solution.py:431
  45.8 5.1 %copy-start.9 = (f32[312,128]{1,0:T(8,128)}, f32[312,128]{1,0:T(8,128)S(1)}, u32[]{:S(2)}) copy-start(f32[312,128]{1,0:T(8,128)S(1)} %collective-permute-done.16.refs_5_) | copy-start | bytes 479236
  45.8 17.1 %collective-permute-start.5 = (f32[40,128]{1,0:T(8,128)}, f32[40,128]{1,0:T(8,128)S(1)}, u32[]{:S(2)}, u32[]{:S(2)}) collective-permute-start(f32[40,128]{1,0:T(8,128)} %get-tuple-element.23), channel_id=1, source_target_pairs={{0,13},{1,12},{2,15},{3,14},{4,9},{5,8},{6,11},{7,10},{8,5},{9,4},... | collective-permute-start | bytes 61448 | tf_op jit(solution)/shard_map/ppermute | solution.py:431
  46.2 4.6 %copy-start.10 = (f32[312,128]{1,0:T(8,128)}, f32[312,128]{1,0:T(8,128)S(1)}, u32[]{:S(2)}) copy-start(f32[312,128]{1,0:T(8,128)S(1)} %collective-permute-done.18.refs_7_) | copy-start | bytes 479236
  46.2 16.6 %collective-permute-start.6 = (f32[40,128]{1,0:T(8,128)}, f32[40,128]{1,0:T(8,128)S(1)}, u32[]{:S(2)}, u32[]{:S(2)}) collective-permute-start(f32[40,128]{1,0:T(8,128)} %get-tuple-element.24), channel_id=1, source_target_pairs={{0,14},{1,15},{2,12},{3,13},{4,10},{5,11},{6,8},{7,9},{8,6},{9,7},... | collective-permute-start | bytes 61448 | tf_op jit(solution)/shard_map/ppermute | solution.py:431
  50.5 5.3 %copy-start.2 = (f32[528,128]{1,0:T(8,128)}, f32[528,128]{1,0:T(8,128)S(1)}, u32[]{:S(2)}) copy-start(f32[528,128]{1,0:T(8,128)S(1)} %collective-permute-done.1.refs_1_) | copy-start | bytes 811012
  50.5 12.4 %collective-permute-start.7 = (f32[40,128]{1,0:T(8,128)}, f32[40,128]{1,0:T(8,128)S(1)}, u32[]{:S(2)}, u32[]{:S(2)}) collective-permute-start(f32[40,128]{1,0:T(8,128)} %get-tuple-element.25), channel_id=1, source_target_pairs={{0,15},{1,14},{2,13},{3,12},{4,11},{5,10},{6,9},{7,8},{8,7},{9,6},... | collective-permute-start | bytes 61448 | tf_op jit(solution)/shard_map/ppermute | solution.py:431
  55.8 0.7 %copy-start.3 = (f32[528,128]{1,0:T(8,128)}, f32[528,128]{1,0:T(8,128)S(1)}, u32[]{:S(2)}) copy-start(f32[528,128]{1,0:T(8,128)S(1)} %collective-permute-done.3.refs_3_) | copy-start | bytes 811012
  62.8 0.6 copy-start.15
  62.9 0.6 copy-start.16
  62.9 0.6 copy-start.17
  62.9 0.6 copy-start.18

commit v2 on v1

--- a/solution.py
+++ b/solution.py
@@ -206,102 +206,35 @@
     )(*blocks)
 
 
-PAD_ROWS = 4
-EDGE_AZ = STEP_AZ
-
-
-def far_sizes(slab):
-    per_az = 2 * STEP_RG
-    bulk = (slab + MARGIN - EDGE_AZ) * per_az
-    return EDGE_AZ * per_az, bulk, PAD_ROWS + (slab + MARGIN - BOX_AZ + EDGE_AZ + PAD_AZ) * per_az
-
-
-def place_of_device():
-    me = lax.axis_index("date")
-    return lax.rem(me // CORES, 2), lax.rem(me, CORES)
-
-
-def far_bulk(core_index, wide, tall, near, out_rows, groups, slab):
-    near_planes, _, _ = near
-    edge, bulk, rows = far_sizes(slab)
+def far_grams(wide, tall, near, out_rows, groups, slab):
+    near_planes = near[0]
+    blocks = wide + tall
     dates = 2 * LANES
     per_az = 2 * STEP_RG
-    blocks = wide + tall
-
-    def row(a, core):
-        return a + 1 - core[0]
-
-    def body(core_ref, *refs):
+
+    def body(*refs):
         block_refs, (near_planes_ref, near_ref, roots_ref, out_ref, planes, *sums) = refs[: len(blocks)], refs[len(blocks) :]
-        lane, core = place_of_device()
+        me = lax.axis_index("date")
 
         @pl.when(pl.program_id(0) == 0)
         def _():
-            inner = core * ((slab - EDGE_AZ) * per_az)
-            outer = lane * (CORES * slab * per_az) + edge + inner
+            inner = lax.rem(me, CORES) * (slab * per_az)
+            outer = lax.rem(me // CORES, 2) * (CORES * slab * per_az) + inner
             firsts = [outer] * len(wide) + [inner] * len(tall)
-            assemble(block_refs, firsts, planes, PAD_ROWS + edge, groups, bulk)
-
-        a = pl.program_id(0)
-        far_half = 1 - lax.axis_index("date") // groups
-        first = PAD_ROWS + edge + a * (STEP_AZ * per_az)
-        near_first = (a + 1 - core) * (STEP_AZ * per_az)
-        far_body(far_half, first, near_first, planes, near_planes_ref, near_ref, roots_ref, out_ref, sums, groups)
-
-    planes = jax.ShapeDtypeStruct((groups, rows, LANES), jnp.float32)
+            assemble(block_refs, firsts, planes, 0, groups, need_rows(out_rows))
+
+        first = pl.program_id(0) * (STEP_AZ * per_az)
+        far_half = 1 - me // groups
+        far_body(far_half, first, first, planes, near_planes_ref, near_ref, roots_ref, out_ref, sums, groups)
+
     return pl.pallas_call(
         body,
-        grid_spec=pltpu.PrefetchScalarGridSpec(
-            num_scalar_prefetch=1,
-            grid=(out_rows - 1,),
-            in_specs=[whole_spec(block) for block in blocks] + [whole_spec(near_planes)] + near_specs(groups, row=row),
-            out_specs=[row_spec(groups, dates, dates, row=row), whole_spec(planes)],
-            scratch_shapes=sums_scratch(3),
-        ),
-        out_shape=[jax.ShapeDtypeStruct((out_rows, groups, dates, dates), jnp.bfloat16), planes],
-    )(core_index, *blocks, *near)
-
-
-def far_edge(core_index, wide, edges, bulk_made, near, out_rows, groups, slab):
-    near_planes, near_out, roots = near
-    out, planes = bulk_made
-    edge, bulk, _ = far_sizes(slab)
-    dates = 2 * LANES
-    per_az = 2 * STEP_RG
-    blocks = wide + edges
-
-    def row(a, core):
-        return (out_rows - 1) * core[0]
-
-    def body(core_ref, *refs):
-        block_refs = refs[: len(blocks)]
-        planes_ref, near_planes_ref, near_ref, roots_ref, _, out_ref, held, *sums = refs[len(blocks) :]
-        lane, core = place_of_device()
-        held[...] = planes_ref[...]
-        skipped = core * (edges[0].shape[0] - edge)
-        outer = lane * (CORES * slab * per_az) + core * ((CORES * slab + MARGIN - EDGE_AZ) * per_az)
-        firsts = [outer] * len(wide) + [skipped] * len(edges)
-        assemble(block_refs, firsts, held, PAD_ROWS + core * (edge + bulk), groups, edge)
-        far_half = 1 - lax.axis_index("date") // groups
-        first = PAD_ROWS + core * ((EDGE_AZ + slab + MARGIN - BOX_AZ) * per_az)
-        near_first = core * ((out_rows - 1) * STEP_AZ * per_az)
-        far_body(far_half, first, near_first, held, near_planes_ref, near_ref, roots_ref, out_ref, sums, groups)
-
-    return pl.pallas_call(
-        body,
-        grid_spec=pltpu.PrefetchScalarGridSpec(
-            num_scalar_prefetch=1,
-            grid=(1,),
-            in_specs=[whole_spec(block) for block in blocks]
-            + [whole_spec(planes), whole_spec(near_planes)]
-            + near_specs(groups, row=row)
-            + [pl.BlockSpec(memory_space=pl.ANY)],
-            out_specs=row_spec(groups, dates, dates, row=row),
-            scratch_shapes=[pltpu.VMEM(planes.shape, jnp.float32)] + sums_scratch(3),
-        ),
-        out_shape=jax.ShapeDtypeStruct(out.shape, out.dtype),
-        input_output_aliases={1 + len(blocks) + 4: 0},
-    )(core_index, *blocks, planes, near_planes, near_out, roots, out)
+        grid=(out_rows,),
+        in_specs=[whole_spec(block) for block in blocks] + [whole_spec(near_planes)] + near_specs(groups),
+        out_specs=row_spec(groups, dates, dates),
+        out_shape=jax.ShapeDtypeStruct((out_rows, groups, dates, dates), jnp.bfloat16),
+        scratch_shapes=[pltpu.VMEM(near_planes.shape, jnp.float32)] + sums_scratch(3),
+    )(*blocks, *near)
 
 
 def grams_of_planes(planes, out_rows):
@@ -334,7 +267,7 @@
 
 
 def pack_kernel(chips, groups, slab, x0_ref, x1_ref, *refs):
-    (*out_refs, rows_ref, stage_ref, sems) = refs
+    (*out_refs, rows_ref, sems) = refs
     me = lax.axis_index("date")
     chip, core, slot = me // CORES, lax.rem(me, CORES), lax.rem(me, groups)
     width = groups * STEP_RG
@@ -355,8 +288,6 @@
                 turned = jnp.concatenate(pieces, axis=0).T
                 rows_ref[pl.ds(first * per_az + at, count, stride=per_az), :] = turned[:count]
     chip_rows = CORES * slab * per_az
-    edge_rows = out_refs[-1].shape[0]
-    bulk_rows = stage_ref.shape[1]
     copies = []
 
     def send(source, target):
@@ -368,19 +299,9 @@
         return rows_ref.at[pl.ds(pl.multiple_of(start, 8), target.shape[0]), :]
 
     plane = chips // 2
-    near_refs = out_refs[1 : 1 + plane]
-    plane_ref, bulk_refs, edge_refs = out_refs[0], out_refs[1 + plane : 3 + plane], out_refs[3 + plane :]
-    send(rows_of(jnp.bitwise_xor(chip, plane) // 2 * (2 * chip_rows), plane_ref), plane_ref)
-    for step, out_ref in enumerate(near_refs):
+    send(rows_of(jnp.bitwise_xor(chip, plane) // 2 * (2 * chip_rows), out_refs[0]), out_refs[0])
+    for step, out_ref in zip([*range(plane), *range(plane + 2, chips)], out_refs[1:]):
         send(rows_of(jnp.bitwise_xor(chip, step) * chip_rows, out_ref), out_ref)
-    for i, out_ref in enumerate(bulk_refs):
-        start = jnp.bitwise_xor(chip, chips - 2 + i) * chip_rows
-        stage_ref[i] = rows_ref[pl.ds(start + EDGE_AZ * per_az, bulk_rows), :]
-        send(stage_ref.at[i], out_ref)
-        for crossed in range(CORES):
-            target = edge_refs[CORES * i + crossed]
-            far_end = jnp.bitwise_xor(core, crossed) * (chip_rows + MARGIN * per_az - edge_rows)
-            send(rows_of(start + far_end, target), target)
     for copy in copies:
         copy.wait()
 
@@ -389,12 +310,10 @@
     per_az = 2 * STEP_RG
     azimuths = chips * CORES * slab
     chip_az = CORES * slab
-    edge = EDGE_AZ * per_az + PAD_ROWS
-    bulk = (chip_az + MARGIN - 2 * EDGE_AZ) * per_az
-    counts = [(2 * chip_az + MARGIN) * per_az] + [(chip_az + MARGIN) * per_az] * (chips // 2) + [bulk] * 2 + [edge] * 4
+    counts = [(2 * chip_az + MARGIN) * per_az] + [(chip_az + MARGIN) * per_az] * (chips - 2)
     spec0 = pl.BlockSpec((flat.shape[0], LANES), lambda i: (0, 0))
     spec1 = pl.BlockSpec((flat.shape[0], LANES), lambda i: (0, 1))
-    made = pl.pallas_call(
+    return pl.pallas_call(
         functools.partial(pack_kernel, chips, groups, slab),
         grid=(1,),
         in_specs=[spec0, spec1],
@@ -402,11 +321,9 @@
         out_shape=[jax.ShapeDtypeStruct((count, LANES), jnp.float32) for count in counts],
         scratch_shapes=[
             pltpu.VMEM(((azimuths + MARGIN) * per_az, LANES), jnp.float32),
-            pltpu.VMEM((2, bulk, LANES), jnp.float32),
             pltpu.SemaphoreType.DMA((len(counts),)),
         ],
     )(flat, flat)
-    return made[0], made[1 : 1 + chips // 2], made[1 + chips // 2 : 3 + chips // 2], made[3 + chips // 2 :]
 
 
 def assemble(blocks, firsts, planes, at, groups, need):
@@ -435,28 +352,21 @@
     chips = lax.axis_size("date") // CORES
     plane = chips // 2
 
-    core_index = lax.rem(lax.axis_index("date"), CORES).reshape(1)
     flat = jnp.swapaxes(slc, 2, 3).reshape(-1, slc.shape[2])
-    wide_sent, near_sent, bulk_sent, edge_sent = pack(flat, chips, groups, slab)
+    wide_sent, *sent = pack(flat, chips, groups, slab)
     wide = swap(wide_sent, CORES * plane)
-    near_legs = [near_sent[0]] + [swap(near_sent[i], CORES * i) for i in range(1, plane)]
-    bulks = [swap(bulk_sent[i], CORES * (chips - 2 + i)) for i in range(2)]
-    edges = []
-    for i in range(2):
-        for crossed in range(CORES):
-            distance = CORES * (chips - 2 + i) + crossed
-            edges.append(swap(edge_sent[CORES * i + crossed], distance))
+    near_legs = [sent[0]] + [swap(sent[step], CORES * step) for step in range(1, plane)]
+    far_legs = [swap(sent[step - 2], CORES * step) for step in range(plane + 2, chips)]
     passed = swap(wide, CORES)
 
     def paired(value):
         return [value, swap(value, 1)]
 
-    near_blocks = [block for i in range(plane) for block in paired(near_legs[i])]
+    near_blocks = [block for step in range(plane) for block in paired(near_legs[step])]
     wides = paired(wide) + paired(passed)
-    talls = paired(bulks[0]) + paired(bulks[1])
+    talls = [block for leg in far_legs for block in paired(leg)]
     near = near_grams(near_blocks, out_rows, groups, slab)
-    made = far_bulk(core_index, wides, talls, near, out_rows, groups, slab)
-    return far_edge(core_index, wides, edges, made, near, out_rows, groups, slab)
+    return far_grams(wides, talls, near, out_rows, groups, slab)
 
 
 def by_slabs(slc, slab, out_rows, groups):

time: 68.6 us -> 57.9 us (0.84)
  starting transfers between devices: 33.2 us -> 24.4 us
  Pallas kernels: 18.9 us -> 15.4 us
  waiting for transfers between devices: 14.6 us -> 15.9 us
    ppermute x19 -> x15, starting transfers between devices: 33.2 us -> 24.4 us  [swap(): lax.ppermute(value, 'date', [(i, i ^ distance) for i in range(count)])]
    pallas_call x2 -> x1, Pallas kernels: 11 us -> 7.56 us  [far_grams(): pl.pallas_call(body, grid=(out_rows,), in_specs=[whole_spec(block) for bl...]
    ppermute x19 -> x15, waiting for transfers between devices: 14.6 us -> 15.9 us  [swap(): lax.ppermute(value, 'date', [(i, i ^ distance) for i in range(count)])]
    unnamed x38 -> x30, local copies, waits for them, and re-layouts: 1.29 us -> 1.51 us
  transfers between devices with their start and end apart: 19 -> 15, of which waited for: 2 -> 4; matrix products, arithmetic and copies ran while one was open for 0% -> 0% of each run, Pallas kernels for 16% -> 8%
where the time goes in v2:
time: 57.9 us; the launch traced here: 57.4 us
  starting transfers between devices  24.4 us (42%)
  waiting for transfers between devices  15.9 us (27%)
  Pallas kernels  15.4 us (27%)
  local copies, waits for them, and re-layouts  1.51 us (3%)
    ppermute x15, starting transfers between devices, swap(): lax.ppermute(value, 'date', [(i, i ^ distance) for i in range(count)])  24.4 us
    ppermute x15, waiting for transfers between devices, swap(): lax.ppermute(value, 'date', [(i, i ^ distance) for i in range(count)])  15.9 us
    pallas_call x1, Pallas kernels, far_grams(): pl.pallas_call(body, grid=(out_rows,), in_specs=[whole_spec(block) for bl...  7.56 us
    pallas_call x1, Pallas kernels, near_grams(): pl.pallas_call(body, grid=(out_rows,), in_specs=[whole_spec(block) for bl...  4.88 us
    pallas_call x1, Pallas kernels, pack(): pl.pallas_call(functools.partial(pack_kernel, chips, groups, slab), grid=...  3 us
    unnamed x30, local copies, waits for them, and re-layouts  1.51 us
  transfers between devices with their start and end apart: 15, of which 4 were waited for; matrix products, arithmetic and copies ran while one was open for 0% of the time, Pallas kernels for 8%

profile of v2, /device:TPU:1, one launch (start us, length us, event | category | flops | bytes accessed | tf_op | source)
XLA Modules:
  0.0 57.4 jit_solution(12205317130416827113)
XLA Ops:
  0.0 3.0 %shard_map.17 = (f32[528,128]{1,0:T(8,128)}, f32[312,128]{1,0:T(8,128)}, f32[312,128]{1,0:T(8,128)}, f32[312,128]{1,0:T(8,128)}, f32[312,128]{1,0:T(8,128)}, /*index=5*/f32[312,128]{1,0:T(8,128)}, f32[312,128]{1,0:T(8,128)}) custom-call(f32[1536,144]{1,0:T(8,128)} %bitcast.3, f32[1536,144]{1,0:T(8,128)} %bitcast.4), custom_call_target="tpu_custom_call" | custom-call | tf_op jit(solution)/shard_map/pallas_call | solution.py:316
  3.0 3.2 %collective-permute-start = (f32[528,128]{1,0:T(8,128)}, f32[528,128]{1,0:T(8,128)S(1)}, u32[]{:S(2)}, u32[]{:S(2)}) collective-permute-start(f32[528,128]{1,0:T(8,128)} %get-tuple-element.15), channel_id=1, source_target_pairs={{0,8},{1,9},{2,10},{3,11},{4,12},{5,13},{6,14},{7,15},{8,0},{9,1},... | collective-permute-start | bytes 811016 | tf_op jit(solution)/shard_map/ppermute | solution.py:348
  6.2 1.1 %collective-permute-start.4 = (f32[312,128]{1,0:T(8,128)}, f32[312,128]{1,0:T(8,128)S(1)}, u32[]{:S(2)}, u32[]{:S(2)}) collective-permute-start(f32[312,128]{1,0:T(8,128)} %get-tuple-element.16), channel_id=1, source_target_pairs={{0,12},{1,13},{2,14},{3,15},{4,8},{5,9},{6,10},{7,11},{8,4},{9,5},... | collective-permute-start | bytes 479240 | tf_op jit(solution)/shard_map/ppermute | solution.py:348
  7.3 14.5 %collective-permute-done.refs_0_ = f32[528,128]{1,0:T(8,128)S(1)} collective-permute-done((f32[528,128]{1,0:T(8,128)}, f32[528,128]{1,0:T(8,128)S(1)}, u32[]{:S(2)}, u32[]{:S(2)}) %collective-permute-start) | collective-permute-done | bytes 270368 | tf_op jit(solution)/shard_map/ppermute | solution.py:348
  21.8 0.0 copy-start
  21.8 1.0 %collective-permute-start.2 = (f32[528,128]{1,0:T(8,128)S(1)}, f32[528,128]{1,0:T(8,128)S(1)}, u32[]{:S(2)}, u32[]{:S(2)}) collective-permute-start(f32[528,128]{1,0:T(8,128)S(1)} %collective-permute-done.refs_0_), channel_id=1, source_target_pairs={{0,2},{1,3},{2,0},{3,1},{4,6},{5,7},{6,4},{7,5},{8,10},{9,11},{10,... | collective-permute-start | bytes 811016 | tf_op jit(solution)/shard_map/ppermute | solution.py:348
  22.8 4.2 %collective-permute-start.6 = (f32[312,128]{1,0:T(8,128)}, f32[312,128]{1,0:T(8,128)S(1)}, u32[]{:S(2)}, u32[]{:S(2)}) collective-permute-start(f32[312,128]{1,0:T(8,128)} %get-tuple-element.17), channel_id=1, source_target_pairs={{0,14},{1,15},{2,12},{3,13},{4,10},{5,11},{6,8},{7,9},{8,6},{9,7},... | collective-permute-start | bytes 479240 | tf_op jit(solution)/shard_map/ppermute | solution.py:348
  27.0 1.2 %collective-permute-start.9 = (f32[312,128]{1,0:T(8,128)}, f32[312,128]{1,0:T(8,128)S(1)}, u32[]{:S(2)}, u32[]{:S(2)}) collective-permute-start(f32[312,128]{1,0:T(8,128)} %get-tuple-element.19), channel_id=1, source_target_pairs={{0,2},{1,3},{2,0},{3,1},{4,6},{5,7},{6,4},{7,5},{8,10},{9,11},{10,... | collective-permute-start | bytes 479240 | tf_op jit(solution)/shard_map/ppermute | solution.py:348
  28.3 0.0 collective-permute-start.11
  28.3 0.0 collective-permute-done.4.refs_4_
  28.3 0.0 copy-start.11
  28.3 1.4 %collective-permute-start.13 = (f32[312,128]{1,0:T(8,128)}, f32[312,128]{1,0:T(8,128)S(1)}, u32[]{:S(2)}, u32[]{:S(2)}) collective-permute-start(f32[312,128]{1,0:T(8,128)} %get-tuple-element.21), channel_id=1, source_target_pairs={{0,6},{1,7},{2,4},{3,5},{4,2},{5,3},{6,0},{7,1},{8,14},{9,15},{10,... | collective-permute-start | bytes 479240 | tf_op jit(solution)/shard_map/ppermute | solution.py:348
  29.7 0.4 collective-permute-done.6.refs_6_
  30.0 0.0 copy-start.12
  30.0 5.6 %collective-permute-start.8 = (f32[312,128]{1,0:T(8,128)}, f32[312,128]{1,0:T(8,128)S(1)}, u32[]{:S(2)}, u32[]{:S(2)}) collective-permute-start(f32[312,128]{1,0:T(8,128)} %get-tuple-element.18.refs_0_), channel_id=1, source_target_pairs={{0,1},{1,0},{2,3},{3,2},{4,5},{5,4},{6,7},{7,6},{8,9},{9,8},{10,11... | collective-permute-start | bytes 479240 | tf_op jit(solution)/shard_map/ppermute | solution.py:348
  35.6 0.2 collective-permute-done.9.refs_2_
  35.9 0.0 copy-start.4
  35.9 5.1 %collective-permute-start.10 = (f32[312,128]{1,0:T(8,128)S(1)}, f32[312,128]{1,0:T(8,128)S(1)}, u32[]{:S(2)}, u32[]{:S(2)}) collective-permute-start(f32[312,128]{1,0:T(8,128)S(1)} %collective-permute-done.9.refs_2_), channel_id=1, source_target_pairs={{0,1},{1,0},{2,3},{3,2},{4,5},{5,4},{6,7},{7,6},{8,9},{9,8},{10,11... | collective-permute-start | bytes 479240 | tf_op jit(solution)/shard_map/ppermute | solution.py:348
  41.0 0.0 collective-permute-done.11.refs_4_
  41.0 0.0 copy-start.5
  41.0 0.1 collective-permute-start.12
  41.1 0.0 collective-permute-done.13.refs_6_
  41.1 0.0 copy-start.6
  41.1 0.4 collective-permute-start.1
  41.5 0.0 collective-permute-done.2.refs_2_
  41.5 0.0 copy-start.1
  41.5 0.1 collective-permute-start.3
  41.6 0.0 collective-permute-done.8.refs_1_
  41.6 0.0 copy-start.7
  41.6 0.4 collective-permute-start.14
  42.0 0.0 collective-permute-done.10.refs_3_
  42.0 0.0 copy-start.8
  42.0 0.3 collective-permute-start.5
  42.4 0.0 collective-permute-done.12.refs_5_
  42.4 0.0 copy-start.9
  42.4 0.2 collective-permute-start.7
  42.6 0.8 %collective-permute-done.14.refs_7_ = f32[312,128]{1,0:T(8,128)S(1)} collective-permute-done((f32[312,128]{1,0:T(8,128)S(1)}, f32[312,128]{1,0:T(8,128)S(1)}, u32[]{:S(2)}, u32[]{:S(2)}) %collective-permute-start.14) | collective-permute-done | bytes 159776 | tf_op jit(solution)/shard_map/ppermute | solution.py:348
  43.4 0.0 copy-done.4
  43.4 0.0 copy-done.5
  43.4 0.0 copy-done.6
  43.4 0.0 copy-done.7
  43.4 0.0 copy-done.8
  43.4 0.0 copy-done.9
  43.4 0.0 copy-start.10
  43.4 0.6 %copy-done.10 = f32[312,128]{1,0:T(8,128)} copy-done((f32[312,128]{1,0:T(8,128)}, f32[312,128]{1,0:T(8,128)S(1)}, u32[]{:S(2)}) %copy-start.10) | copy-done | bytes 159768
  44.1 4.9 %shard_map.18 = (f32[8,264,128]{2,1,0:T(8,128)}, bf16[3,8,128,128]{3,2,1,0:T(8,128)(2,1)}, f32[3,8,1,128]{3,2,1,0:T(1,128)}) custom-call(f32[312,128]{1,0:T(8,128)} %get-tuple-element.18.refs_0_, f32[312,128]{1,0:T(8,128)} %copy-done.7, f32[312,128]{1,0:T(8,128)} %copy-done.4, f32[312,128]{1,0:T(8,128)} %copy-done.8, f32[312,128]{1,0:T(8,128)} %copy-done.5, ...), custom_call_target="tpu_custom_call" | custom-call | tf_op jit(solution)/shard_map/pallas_call | solution.py:199
  48.9 0.0 collective-permute-done.5.refs_5_
  49.0 0.0 copy-start.13
  49.0 0.0 collective-permute-done.7.refs_7_
  49.0 0.0 copy-start.14
  49.0 0.0 collective-permute-done.1.refs_1_
  49.0 0.0 copy-start.2
  49.0 0.0 collective-permute-done.3.refs_3_
  49.0 0.0 copy-start.3
  49.0 0.0 copy-done
  49.0 0.0 copy-done.11
  49.0 0.0 copy-done.12
  49.1 0.0 copy-done.1
  49.1 0.6 copy-done.13
  49.6 0.1 copy-done.14
  49.7 0.1 copy-done.2
  49.8 0.1 copy-done.3
  49.9 7.6 %shard_map.19 = bf16[3,8,256,256]{3,2,1,0:T(8,128)(2,1)} custom-call(f32[528,128]{1,0:T(8,128)} %copy-done, f32[528,128]{1,0:T(8,128)} %copy-done.2, f32[528,128]{1,0:T(8,128)} %copy-done.1, f32[528,128]{1,0:T(8,128)} %copy-done.3, f32[312,128]{1,0:T(8,128)} %copy-done.11, f32[312,128]{1,0:T(8,128)} %copy-done.13, f32[312,128]{1,0:T(8,128)} %copy-done.12, ...), custom_call_target="tpu_custom_call" | custom-call | tf_op jit(solution)/shard_map/pallas_call | solution.py:230
Async XLA Ops:
  3.0 18.8 %collective-permute-start = (f32[528,128]{1,0:T(8,128)}, f32[528,128]{1,0:T(8,128)S(1)}, u32[]{:S(2)}, u32[]{:S(2)}) collective-permute-start(f32[528,128]{1,0:T(8,128)} %get-tuple-element.15), channel_id=1, source_target_pairs={{0,8},{1,9},{2,10},{3,11},{4,12},{5,13},{6,14},{7,15},{8,0},{9,1},... | collective-permute-start | bytes 811016 | tf_op jit(solution)/shard_map/ppermute | solution.py:348
  6.2 22.1 %collective-permute-start.4 = (f32[312,128]{1,0:T(8,128)}, f32[312,128]{1,0:T(8,128)S(1)}, u32[]{:S(2)}, u32[]{:S(2)}) collective-permute-start(f32[312,128]{1,0:T(8,128)} %get-tuple-element.16), channel_id=1, source_target_pairs={{0,12},{1,13},{2,14},{3,15},{4,8},{5,9},{6,10},{7,11},{8,4},{9,5},... | collective-permute-start | bytes 479240 | tf_op jit(solution)/shard_map/ppermute | solution.py:348
  21.8 27.2 %copy-start = (f32[528,128]{1,0:T(8,128)}, f32[528,128]{1,0:T(8,128)S(1)}, u32[]{:S(2)}) copy-start(f32[528,128]{1,0:T(8,128)S(1)} %collective-permute-done.refs_0_) | copy-start | bytes 811012
  21.8 19.7 %collective-permute-start.2 = (f32[528,128]{1,0:T(8,128)S(1)}, f32[528,128]{1,0:T(8,128)S(1)}, u32[]{:S(2)}, u32[]{:S(2)}) collective-permute-start(f32[528,128]{1,0:T(8,128)S(1)} %collective-permute-done.refs_0_), channel_id=1, source_target_pairs={{0,2},{1,3},{2,0},{3,1},{4,6},{5,7},{6,4},{7,5},{8,10},{9,11},{10,... | collective-permute-start | bytes 811016 | tf_op jit(solution)/shard_map/ppermute | solution.py:348
  22.8 7.2 %collective-permute-start.6 = (f32[312,128]{1,0:T(8,128)}, f32[312,128]{1,0:T(8,128)S(1)}, u32[]{:S(2)}, u32[]{:S(2)}) collective-permute-start(f32[312,128]{1,0:T(8,128)} %get-tuple-element.17), channel_id=1, source_target_pairs={{0,14},{1,15},{2,12},{3,13},{4,10},{5,11},{6,8},{7,9},{8,6},{9,7},... | collective-permute-start | bytes 479240 | tf_op jit(solution)/shard_map/ppermute | solution.py:348
  27.0 8.9 %collective-permute-start.9 = (f32[312,128]{1,0:T(8,128)}, f32[312,128]{1,0:T(8,128)S(1)}, u32[]{:S(2)}, u32[]{:S(2)}) collective-permute-start(f32[312,128]{1,0:T(8,128)} %get-tuple-element.19), channel_id=1, source_target_pairs={{0,2},{1,3},{2,0},{3,1},{4,6},{5,7},{6,4},{7,5},{8,10},{9,11},{10,... | collective-permute-start | bytes 479240 | tf_op jit(solution)/shard_map/ppermute | solution.py:348
  28.3 12.7 %collective-permute-start.11 = (f32[312,128]{1,0:T(8,128)}, f32[312,128]{1,0:T(8,128)S(1)}, u32[]{:S(2)}, u32[]{:S(2)}) collective-permute-start(f32[312,128]{1,0:T(8,128)} %get-tuple-element.20), channel_id=1, source_target_pairs={{0,4},{1,5},{2,6},{3,7},{4,0},{5,1},{6,2},{7,3},{8,12},{9,13},{10,... | collective-permute-start | bytes 479240 | tf_op jit(solution)/shard_map/ppermute | solution.py:348
  28.3 20.8 %copy-start.11 = (f32[312,128]{1,0:T(8,128)}, f32[312,128]{1,0:T(8,128)S(1)}, u32[]{:S(2)}) copy-start(f32[312,128]{1,0:T(8,128)S(1)} %collective-permute-done.4.refs_4_) | copy-start | bytes 479236
  28.3 12.8 %collective-permute-start.13 = (f32[312,128]{1,0:T(8,128)}, f32[312,128]{1,0:T(8,128)S(1)}, u32[]{:S(2)}, u32[]{:S(2)}) collective-permute-start(f32[312,128]{1,0:T(8,128)} %get-tuple-element.21), channel_id=1, source_target_pairs={{0,6},{1,7},{2,4},{3,5},{4,2},{5,3},{6,0},{7,1},{8,14},{9,15},{10,... | collective-permute-start | bytes 479240 | tf_op jit(solution)/shard_map/ppermute | solution.py:348
  30.0 19.0 %copy-start.12 = (f32[312,128]{1,0:T(8,128)}, f32[312,128]{1,0:T(8,128)S(1)}, u32[]{:S(2)}) copy-start(f32[312,128]{1,0:T(8,128)S(1)} %collective-permute-done.6.refs_6_) | copy-start | bytes 479236
  30.0 11.6 %collective-permute-start.8 = (f32[312,128]{1,0:T(8,128)}, f32[312,128]{1,0:T(8,128)S(1)}, u32[]{:S(2)}, u32[]{:S(2)}) collective-permute-start(f32[312,128]{1,0:T(8,128)} %get-tuple-element.18.refs_0_), channel_id=1, source_target_pairs={{0,1},{1,0},{2,3},{3,2},{4,5},{5,4},{6,7},{7,6},{8,9},{9,8},{10,11... | collective-permute-start | bytes 479240 | tf_op jit(solution)/shard_map/ppermute | solution.py:348
  35.9 7.5 %copy-start.4 = (f32[312,128]{1,0:T(8,128)}, f32[312,128]{1,0:T(8,128)S(1)}, u32[]{:S(2)}) copy-start(f32[312,128]{1,0:T(8,128)S(1)} %collective-permute-done.9.refs_2_) | copy-start | bytes 479236
  35.9 6.2 %collective-permute-start.10 = (f32[312,128]{1,0:T(8,128)S(1)}, f32[312,128]{1,0:T(8,128)S(1)}, u32[]{:S(2)}, u32[]{:S(2)}) collective-permute-start(f32[312,128]{1,0:T(8,128)S(1)} %collective-permute-done.9.refs_2_), channel_id=1, source_target_pairs={{0,1},{1,0},{2,3},{3,2},{4,5},{5,4},{6,7},{7,6},{8,9},{9,8},{10,11... | collective-permute-start | bytes 479240 | tf_op jit(solution)/shard_map/ppermute | solution.py:348
  41.0 2.4 %copy-start.5 = (f32[312,128]{1,0:T(8,128)}, f32[312,128]{1,0:T(8,128)S(1)}, u32[]{:S(2)}) copy-start(f32[312,128]{1,0:T(8,128)S(1)} %collective-permute-done.11.refs_4_) | copy-start | bytes 479236
  41.0 1.4 %collective-permute-start.12 = (f32[312,128]{1,0:T(8,128)S(1)}, f32[312,128]{1,0:T(8,128)S(1)}, u32[]{:S(2)}, u32[]{:S(2)}) collective-permute-start(f32[312,128]{1,0:T(8,128)S(1)} %collective-permute-done.11.refs_4_), channel_id=1, source_target_pairs={{0,1},{1,0},{2,3},{3,2},{4,5},{5,4},{6,7},{7,6},{8,9},{9,8},{10,11... | collective-permute-start | bytes 479240 | tf_op jit(solution)/shard_map/ppermute | solution.py:348
  41.1 2.3 %copy-start.6 = (f32[312,128]{1,0:T(8,128)}, f32[312,128]{1,0:T(8,128)S(1)}, u32[]{:S(2)}) copy-start(f32[312,128]{1,0:T(8,128)S(1)} %collective-permute-done.13.refs_6_) | copy-start | bytes 479236
  41.1 7.9 %collective-permute-start.1 = (f32[528,128]{1,0:T(8,128)S(1)}, f32[528,128]{1,0:T(8,128)S(1)}, u32[]{:S(2)}, u32[]{:S(2)}) collective-permute-start(f32[528,128]{1,0:T(8,128)S(1)} %collective-permute-done.refs_0_), channel_id=1, source_target_pairs={{0,1},{1,0},{2,3},{3,2},{4,5},{5,4},{6,7},{7,6},{8,9},{9,8},{10,11... | collective-permute-start | bytes 811016 | tf_op jit(solution)/shard_map/ppermute | solution.py:348
  41.5 7.5 %copy-start.1 = (f32[528,128]{1,0:T(8,128)}, f32[528,128]{1,0:T(8,128)S(1)}, u32[]{:S(2)}) copy-start(f32[528,128]{1,0:T(8,128)S(1)} %collective-permute-done.2.refs_2_) | copy-start | bytes 811012
  41.5 7.5 %collective-permute-start.3 = (f32[528,128]{1,0:T(8,128)S(1)}, f32[528,128]{1,0:T(8,128)S(1)}, u32[]{:S(2)}, u32[]{:S(2)}) collective-permute-start(f32[528,128]{1,0:T(8,128)S(1)} %collective-permute-done.2.refs_2_), channel_id=1, source_target_pairs={{0,1},{1,0},{2,3},{3,2},{4,5},{5,4},{6,7},{7,6},{8,9},{9,8},{10,11... | collective-permute-start | bytes 811016 | tf_op jit(solution)/shard_map/ppermute | solution.py:348
  41.6 1.8 %copy-start.7 = (f32[312,128]{1,0:T(8,128)}, f32[312,128]{1,0:T(8,128)S(1)}, u32[]{:S(2)}) copy-start(f32[312,128]{1,0:T(8,128)S(1)} %collective-permute-done.8.refs_1_) | copy-start | bytes 479236
  41.6 1.8 %collective-permute-start.14 = (f32[312,128]{1,0:T(8,128)S(1)}, f32[312,128]{1,0:T(8,128)S(1)}, u32[]{:S(2)}, u32[]{:S(2)}) collective-permute-start(f32[312,128]{1,0:T(8,128)S(1)} %collective-permute-done.13.refs_6_), channel_id=1, source_target_pairs={{0,1},{1,0},{2,3},{3,2},{4,5},{5,4},{6,7},{7,6},{8,9},{9,8},{10,11... | collective-permute-start | bytes 479240 | tf_op jit(solution)/shard_map/ppermute | solution.py:348
  42.0 1.4 %copy-start.8 = (f32[312,128]{1,0:T(8,128)}, f32[312,128]{1,0:T(8,128)S(1)}, u32[]{:S(2)}) copy-start(f32[312,128]{1,0:T(8,128)S(1)} %collective-permute-done.10.refs_3_) | copy-start | bytes 479236
  42.0 6.9 %collective-permute-start.5 = (f32[312,128]{1,0:T(8,128)S(1)}, f32[312,128]{1,0:T(8,128)S(1)}, u32[]{:S(2)}, u32[]{:S(2)}) collective-permute-start(f32[312,128]{1,0:T(8,128)S(1)} %collective-permute-done.4.refs_4_), channel_id=1, source_target_pairs={{0,1},{1,0},{2,3},{3,2},{4,5},{5,4},{6,7},{7,6},{8,9},{9,8},{10,11... | collective-permute-start | bytes 479240 | tf_op jit(solution)/shard_map/ppermute | solution.py:348
  42.4 1.0 %copy-start.9 = (f32[312,128]{1,0:T(8,128)}, f32[312,128]{1,0:T(8,128)S(1)}, u32[]{:S(2)}) copy-start(f32[312,128]{1,0:T(8,128)S(1)} %collective-permute-done.12.refs_5_) | copy-start | bytes 479236
  42.4 6.6 %collective-permute-start.7 = (f32[312,128]{1,0:T(8,128)S(1)}, f32[312,128]{1,0:T(8,128)S(1)}, u32[]{:S(2)}, u32[]{:S(2)}) collective-permute-start(f32[312,128]{1,0:T(8,128)S(1)} %collective-permute-done.6.refs_6_), channel_id=1, source_target_pairs={{0,1},{1,0},{2,3},{3,2},{4,5},{5,4},{6,7},{7,6},{8,9},{9,8},{10,11... | collective-permute-start | bytes 479240 | tf_op jit(solution)/shard_map/ppermute | solution.py:348
  43.4 0.7 %copy-start.10 = (f32[312,128]{1,0:T(8,128)}, f32[312,128]{1,0:T(8,128)S(1)}, u32[]{:S(2)}) copy-start(f32[312,128]{1,0:T(8,128)S(1)} %collective-permute-done.14.refs_7_) | copy-start | bytes 479236
  49.0 0.7 %copy-start.13 = (f32[312,128]{1,0:T(8,128)}, f32[312,128]{1,0:T(8,128)S(1)}, u32[]{:S(2)}) copy-start(f32[312,128]{1,0:T(8,128)S(1)} %collective-permute-done.5.refs_5_) | copy-start | bytes 479236
  49.0 0.7 %copy-start.14 = (f32[312,128]{1,0:T(8,128)}, f32[312,128]{1,0:T(8,128)S(1)}, u32[]{:S(2)}) copy-start(f32[312,128]{1,0:T(8,128)S(1)} %collective-permute-done.7.refs_7_) | copy-start | bytes 479236
  49.0 0.8 %copy-start.2 = (f32[528,128]{1,0:T(8,128)}, f32[528,128]{1,0:T(8,128)S(1)}, u32[]{:S(2)}) copy-start(f32[528,128]{1,0:T(8,128)S(1)} %collective-permute-done.1.refs_1_) | copy-start | bytes 811012
  49.0 0.9 %copy-start.3 = (f32[528,128]{1,0:T(8,128)}, f32[528,128]{1,0:T(8,128)S(1)}, u32[]{:S(2)}) copy-start(f32[528,128]{1,0:T(8,128)S(1)} %collective-permute-done.3.refs_3_) | copy-start | bytes 811012

commit v3 on v2

--- a/solution.py
+++ b/solution.py
@@ -79,13 +79,13 @@
     return [jnp.where(up >= low, cut[0], cut[1])] + cut[2:]
 
 
-def box_sums(made, last_partial, pending, pair):
+def box_sums(made, fresh, last_partial, pending, pair):
     boxes = []
     for i, (partial, last) in enumerate(zip(blocks_of(made[0]), blocks_of(made[1]))):
         full = partial + last
-        boxes.append(full + pending[i])
-        pending[i] = full + pair[i]
-        pair[i] = full + last_partial[i]
+        boxes.append(full if fresh else full + pending[i])
+        pending[i] = full if fresh else full + pair[i]
+        pair[i] = full if fresh else full + last_partial[i]
         last_partial[i] = partial
     return boxes
 
@@ -99,58 +99,67 @@
     return jnp.broadcast_to(row, (LANES, LANES))
 
 
-def over_groups(groups, sums, make, finish):
-    for ref in sums:
-        ref[...] = jnp.zeros_like(ref)
+def over_rows(out_rows, groups, sums, prepare, make, finish):
     ready = None
-    for group in reversed(range(groups)):
-        made = make(group)
-        if ready is not None:
-            finish(group + 1, box_sums(ready, *sums))
-        ready = made
-    finish(0, box_sums(ready, *sums))
-
-
-def near_body(planes, out_ref, roots_ref, sums, groups):
-    first = pl.program_id(0) * (STEP_AZ * 2 * STEP_RG)
-
-    def make(group):
+    for row in range(out_rows):
+        for group in reversed(range(groups)):
+            if row == 0:
+                prepare(group)
+            made = make(row * (STEP_AZ * 2 * STEP_RG), group)
+            if ready is not None:
+                finish(*ready[:2], box_sums(ready[2], ready[1] == groups - 1, *sums))
+            ready = (row, group, made)
+    finish(*ready[:2], box_sums(ready[2], groups == 1, *sums))
+
+
+def near_body(prepare, planes, out_ref, roots_ref, sums, out_rows, groups):
+    def make(first, group):
         pieces = windows(planes, group, first)
         return products(pieces, [pieces])
 
-    def finish(group, boxes):
+    def finish(row, group, boxes):
         roots = inverse_roots(boxes[0])
-        roots_ref[0, group] = roots
-        out_ref[0, group] = (boxes[0] * (spread(roots).T * spread(roots))).astype(jnp.bfloat16)
-
-    over_groups(groups, sums, make, finish)
-
-
-def far_body(far_half, first, near_first, planes, near_planes, near_ref, roots_ref, out_ref, sums, groups):
+        roots_ref[row, group] = roots
+        out_ref[row, group] = (boxes[0] * (spread(roots).T * spread(roots))).astype(jnp.bfloat16)
+
+    over_rows(out_rows, groups, sums, prepare, make, finish)
+
+
+def far_body(far_half, prepare, planes, near_refs, out_hbm, out_ref, sems, sums, out_rows, groups):
+    near_planes, near_ref, roots_ref = near_refs
     upper = far_half == 1
     far_rows = pl.ds(pl.multiple_of(far_half * LANES, LANES), LANES)
     near_rows = pl.ds(pl.multiple_of((1 - far_half) * LANES, LANES), LANES)
-
-    def make(group):
+    batch = groups // 2
+    copies = []
+
+    def make(first, group):
         pieces = windows(planes, group, first)
-        return products(pieces, [pieces, windows(near_planes, group, near_first)])
-
-    def finish(group, boxes):
+        return products(pieces, [pieces, windows(near_planes, group, first)])
+
+    def finish(row, group, boxes):
         square, real, imag = boxes
         far_across = spread(inverse_roots(square))
         far_down = far_across.T
-        near_across = spread(roots_ref[0, group])
+        near_across = spread(roots_ref[row, group])
         square = square * (far_down * far_across)
         scale = far_down * near_across
         real, imag = real * scale, imag * scale
         straight = jnp.where(upper, imag, real).astype(jnp.bfloat16)
         turned = jnp.where(upper, real, -imag).T.astype(jnp.bfloat16)
-        out_ref[0, group, near_rows, near_rows] = near_ref[0, group]
-        out_ref[0, group, far_rows, far_rows] = square.astype(jnp.bfloat16)
-        out_ref[0, group, far_rows, near_rows] = straight
-        out_ref[0, group, near_rows, far_rows] = turned
-
-    over_groups(groups, sums, make, finish)
+        out_ref[row, group, near_rows, near_rows] = near_ref[row, group]
+        out_ref[row, group, far_rows, far_rows] = square.astype(jnp.bfloat16)
+        out_ref[row, group, far_rows, near_rows] = straight
+        out_ref[row, group, near_rows, far_rows] = turned
+        if group % batch == 0:
+            part = (row, pl.ds(group, batch))
+            copy = pltpu.make_async_copy(out_ref.at[part], out_hbm.at[part], sems.at[len(copies)])
+            copy.start()
+            copies.append(copy)
+
+    over_rows(out_rows, groups, sums, prepare, make, finish)
+    for copy in copies:
+        copy.wait()
 
 
 def plane_rows(out_rows):
@@ -161,10 +170,6 @@
     return [pltpu.VMEM((count, LANES, LANES), jnp.float32)] * 3
 
 
-def row_spec(*shape, row=lambda a, *_: a):
-    return pl.BlockSpec((1, *shape), lambda *at: (row(*at),) + (0,) * len(shape))
-
-
 def whole_spec(array):
     return pl.BlockSpec(array.shape, lambda *_: (0,) * len(array.shape))
 
@@ -173,97 +178,80 @@
     return (STEP_AZ * (out_rows - 1) + BOX_AZ) * 2 * STEP_RG
 
 
-def near_shapes(out_rows, groups):
-    return [
+def nothing(group):
+    pass
+
+
+def near_call(body, operands, made, out_rows, groups):
+    shapes = made + [
         jax.ShapeDtypeStruct((out_rows, groups, LANES, LANES), jnp.bfloat16),
         jax.ShapeDtypeStruct((out_rows, groups, 1, LANES), jnp.float32),
     ]
-
-
-def near_specs(groups, **row):
-    return [row_spec(groups, LANES, LANES, **row), row_spec(groups, 1, LANES, **row)]
+    return pl.pallas_call(
+        body,
+        grid=(1,),
+        in_specs=[whole_spec(operand) for operand in operands],
+        out_specs=[whole_spec(shape) for shape in shapes],
+        out_shape=shapes,
+        scratch_shapes=sums_scratch(1),
+    )(*operands)
+
+
+def far_call(body, operands, held, out_rows, groups):
+    dates = 2 * LANES
+    shape = (out_rows, groups, dates, dates)
+    return pl.pallas_call(
+        body,
+        grid=(1,),
+        in_specs=[whole_spec(operand) for operand in operands],
+        out_specs=pl.BlockSpec(memory_space=pl.ANY),
+        out_shape=jax.ShapeDtypeStruct(shape, jnp.bfloat16),
+        scratch_shapes=held
+        + [pltpu.VMEM(shape, jnp.bfloat16), pltpu.SemaphoreType.DMA((2 * out_rows,))]
+        + sums_scratch(3),
+    )(*operands)
 
 
 def near_grams(blocks, out_rows, groups, slab):
     def body(*refs):
         block_refs, (planes, out_ref, roots_ref, *sums) = refs[: len(blocks)], refs[len(blocks) :]
-
-        @pl.when(pl.program_id(0) == 0)
-        def _():
-            first = lax.rem(lax.axis_index("date"), CORES) * (slab * 2 * STEP_RG)
-            assemble(block_refs, [first] * len(blocks), planes, 0, groups, need_rows(out_rows))
-
-        near_body(planes, out_ref, roots_ref, sums, groups)
+        first = lax.rem(lax.axis_index("date"), CORES) * (slab * 2 * STEP_RG)
+        prepare = assembler(block_refs, [first] * len(blocks), planes, groups, need_rows(out_rows))
+        near_body(prepare, planes, out_ref, roots_ref, sums, out_rows, groups)
 
     planes = jax.ShapeDtypeStruct((groups, plane_rows(out_rows), LANES), jnp.float32)
-    return pl.pallas_call(
-        body,
-        grid=(out_rows,),
-        in_specs=[whole_spec(block) for block in blocks],
-        out_specs=[whole_spec(planes)] + near_specs(groups),
-        out_shape=[planes] + near_shapes(out_rows, groups),
-        scratch_shapes=sums_scratch(1),
-    )(*blocks)
+    return near_call(body, blocks, [planes], out_rows, groups)
 
 
 def far_grams(wide, tall, near, out_rows, groups, slab):
-    near_planes = near[0]
     blocks = wide + tall
-    dates = 2 * LANES
     per_az = 2 * STEP_RG
 
     def body(*refs):
-        block_refs, (near_planes_ref, near_ref, roots_ref, out_ref, planes, *sums) = refs[: len(blocks)], refs[len(blocks) :]
+        block_refs, near_refs = refs[: len(blocks)], refs[len(blocks) : len(blocks) + len(near)]
+        out_hbm, planes, out_ref, sems, *sums = refs[len(blocks) + len(near) :]
         me = lax.axis_index("date")
-
-        @pl.when(pl.program_id(0) == 0)
-        def _():
-            inner = lax.rem(me, CORES) * (slab * per_az)
-            outer = lax.rem(me // CORES, 2) * (CORES * slab * per_az) + inner
-            firsts = [outer] * len(wide) + [inner] * len(tall)
-            assemble(block_refs, firsts, planes, 0, groups, need_rows(out_rows))
-
-        first = pl.program_id(0) * (STEP_AZ * per_az)
-        far_half = 1 - me // groups
-        far_body(far_half, first, first, planes, near_planes_ref, near_ref, roots_ref, out_ref, sums, groups)
-
-    return pl.pallas_call(
-        body,
-        grid=(out_rows,),
-        in_specs=[whole_spec(block) for block in blocks] + [whole_spec(near_planes)] + near_specs(groups),
-        out_specs=row_spec(groups, dates, dates),
-        out_shape=jax.ShapeDtypeStruct((out_rows, groups, dates, dates), jnp.bfloat16),
-        scratch_shapes=[pltpu.VMEM(near_planes.shape, jnp.float32)] + sums_scratch(3),
-    )(*blocks, *near)
+        inner = lax.rem(me, CORES) * (slab * per_az)
+        outer = lax.rem(me // CORES, 2) * (CORES * slab * per_az) + inner
+        firsts = [outer] * len(wide) + [inner] * len(tall)
+        prepare = assembler(block_refs, firsts, planes, groups, need_rows(out_rows))
+        far_body(1 - me // groups, prepare, planes, near_refs, out_hbm, out_ref, sems, sums, out_rows, groups)
+
+    return far_call(body, [*blocks, *near], [pltpu.VMEM(near[0].shape, jnp.float32)], out_rows, groups)
 
 
 def grams_of_planes(planes, out_rows):
     groups = planes.shape[1]
-    dates = 2 * LANES
 
     def near(planes_ref, out_ref, roots_ref, *sums):
-        near_body(planes_ref, out_ref, roots_ref, sums, groups)
-
-    def far(planes_ref, near_planes, near_ref, roots_ref, out_ref, *sums):
-        first = pl.program_id(0) * (STEP_AZ * 2 * STEP_RG)
-        far_body(jnp.int32(1), first, first, planes_ref, near_planes, near_ref, roots_ref, out_ref, sums, groups)
-
-    near_out = pl.pallas_call(
-        near,
-        grid=(out_rows,),
-        in_specs=[whole_spec(planes[0])],
-        out_specs=near_specs(groups),
-        out_shape=near_shapes(out_rows, groups),
-        scratch_shapes=sums_scratch(1),
-    )(planes[0])
-    return pl.pallas_call(
-        far,
-        grid=(out_rows,),
-        in_specs=[whole_spec(planes[1]), whole_spec(planes[0])] + near_specs(groups),
-        out_specs=row_spec(groups, dates, dates),
-        out_shape=jax.ShapeDtypeStruct((out_rows, groups, dates, dates), jnp.bfloat16),
-        scratch_shapes=sums_scratch(3),
-    )(planes[1], planes[0], *near_out)
+        near_body(nothing, planes_ref, out_ref, roots_ref, sums, out_rows, groups)
+
+    def far(planes_ref, near_planes, near_ref, roots_ref, out_hbm, out_ref, sems, *sums):
+        near_refs = near_planes, near_ref, roots_ref
+        far_body(jnp.int32(1), nothing, planes_ref, near_refs, out_hbm, out_ref, sems, sums, out_rows, groups)
+
+    near_out = near_call(near, [planes[0]], [], out_rows, groups)
+    return far_call(far, [planes[1], planes[0], *near_out], [], out_rows, groups)
 
 
 def pack_kernel(chips, groups, slab, x0_ref, x1_ref, *refs):
@@ -326,21 +314,23 @@
     )(flat, flat)
 
 
-def assemble(blocks, firsts, planes, at, groups, need):
+def assembler(blocks, firsts, planes, groups, need):
     slot = lax.rem(lax.axis_index("date"), groups)
     width = LANES // groups
     place = lax.broadcasted_iota(jnp.int32, (8, LANES), 1) // width
     held = [lax.rem(place - jnp.bitwise_xor(slot, source) + groups, groups) for source in range(groups)]
     starts = [8 * i for i in range(need // 8)] + ([need - 8] if need % 8 else [])
-    for start in starts:
-        loaded = [block[pl.ds(first + start, 8), :] for block, first in zip(blocks, firsts)]
-        for group in range(groups):
-            merged = loaded[0]
+
+    def prepare(group):
+        for start in starts:
+            merged = blocks[0][pl.ds(firsts[0] + start, 8), :]
             for source in range(1, groups):
-                merged = jnp.where(held[source] == group, loaded[source], merged)
+                merged = jnp.where(held[source] == group, blocks[source][pl.ds(firsts[source] + start, 8), :], merged)
             if group:
                 merged = pltpu.roll(merged, LANES - width * group, 1)
-            planes[group, pl.ds(at + start, 8), :] = merged
+            planes[group, pl.ds(start, 8), :] = merged
+
+    return prepare
 
 
 def swap(value, distance):

time: 57.9 us -> 57.6 us (level)
  no operation moved by 1% of the time
where the time goes in v3:
time: 57.6 us; the launch traced here: 57.2 us
  starting transfers between devices  24.4 us (42%)
  waiting for transfers between devices  15.9 us (28%)
  Pallas kernels  15.2 us (26%)
  local copies, waits for them, and re-layouts  1.51 us (3%)
    ppermute x15, starting transfers between devices, swap(): lax.ppermute(value, 'date', [(i, i ^ distance) for i in range(count)])  24.4 us
    ppermute x15, waiting for transfers between devices, swap(): lax.ppermute(value, 'date', [(i, i ^ distance) for i in range(count)])  15.9 us
    pallas_call x1, Pallas kernels, far_call(): pl.pallas_call(body, grid=(1,), in_specs=[whole_spec(operand) for operand...  7.51 us
    pallas_call x1, Pallas kernels, near_call(): pl.pallas_call(body, grid=(1,), in_specs=[whole_spec(operand) for operand...  4.67 us
    pallas_call x1, Pallas kernels, pack(): pl.pallas_call(functools.partial(pack_kernel, chips, groups, slab), grid=...  3 us
    unnamed x30, local copies, waits for them, and re-layouts  1.51 us
  transfers between devices with their start and end apart: 15, of which 4 were waited for; matrix products, arithmetic and copies ran while one was open for 0% of the time, Pallas kernels for 8%

profile of v3, /device:TPU:1, one launch (start us, length us, event | category | flops | bytes accessed | tf_op | source)
XLA Modules:
  0.0 57.2 jit_solution(13910650416334846272)
XLA Ops:
  0.0 3.0 %shard_map.17 = (f32[528,128]{1,0:T(8,128)}, f32[312,128]{1,0:T(8,128)}, f32[312,128]{1,0:T(8,128)}, f32[312,128]{1,0:T(8,128)}, f32[312,128]{1,0:T(8,128)}, /*index=5*/f32[312,128]{1,0:T(8,128)}, f32[312,128]{1,0:T(8,128)}) custom-call(f32[1536,144]{1,0:T(8,128)} %bitcast.3, f32[1536,144]{1,0:T(8,128)} %bitcast.4), custom_call_target="tpu_custom_call" | custom-call | tf_op jit(solution)/shard_map/pallas_call | solution.py:304
  3.0 3.2 %collective-permute-start = (f32[528,128]{1,0:T(8,128)}, f32[528,128]{1,0:T(8,128)S(1)}, u32[]{:S(2)}, u32[]{:S(2)}) collective-permute-start(f32[528,128]{1,0:T(8,128)} %get-tuple-element.15), channel_id=1, source_target_pairs={{0,8},{1,9},{2,10},{3,11},{4,12},{5,13},{6,14},{7,15},{8,0},{9,1},... | collective-permute-start | bytes 811016 | tf_op jit(solution)/shard_map/ppermute | solution.py:338
  6.2 1.1 %collective-permute-start.4 = (f32[312,128]{1,0:T(8,128)}, f32[312,128]{1,0:T(8,128)S(1)}, u32[]{:S(2)}, u32[]{:S(2)}) collective-permute-start(f32[312,128]{1,0:T(8,128)} %get-tuple-element.16), channel_id=1, source_target_pairs={{0,12},{1,13},{2,14},{3,15},{4,8},{5,9},{6,10},{7,11},{8,4},{9,5},... | collective-permute-start | bytes 479240 | tf_op jit(solution)/shard_map/ppermute | solution.py:338
  7.3 14.5 %collective-permute-done.refs_0_ = f32[528,128]{1,0:T(8,128)S(1)} collective-permute-done((f32[528,128]{1,0:T(8,128)}, f32[528,128]{1,0:T(8,128)S(1)}, u32[]{:S(2)}, u32[]{:S(2)}) %collective-permute-start) | collective-permute-done | bytes 270368 | tf_op jit(solution)/shard_map/ppermute | solution.py:338
  21.8 0.0 copy-start
  21.8 1.0 %collective-permute-start.2 = (f32[528,128]{1,0:T(8,128)S(1)}, f32[528,128]{1,0:T(8,128)S(1)}, u32[]{:S(2)}, u32[]{:S(2)}) collective-permute-start(f32[528,128]{1,0:T(8,128)S(1)} %collective-permute-done.refs_0_), channel_id=1, source_target_pairs={{0,2},{1,3},{2,0},{3,1},{4,6},{5,7},{6,4},{7,5},{8,10},{9,11},{10,... | collective-permute-start | bytes 811016 | tf_op jit(solution)/shard_map/ppermute | solution.py:338
  22.8 4.2 %collective-permute-start.6 = (f32[312,128]{1,0:T(8,128)}, f32[312,128]{1,0:T(8,128)S(1)}, u32[]{:S(2)}, u32[]{:S(2)}) collective-permute-start(f32[312,128]{1,0:T(8,128)} %get-tuple-element.17), channel_id=1, source_target_pairs={{0,14},{1,15},{2,12},{3,13},{4,10},{5,11},{6,8},{7,9},{8,6},{9,7},... | collective-permute-start | bytes 479240 | tf_op jit(solution)/shard_map/ppermute | solution.py:338
  27.0 1.2 %collective-permute-start.9 = (f32[312,128]{1,0:T(8,128)}, f32[312,128]{1,0:T(8,128)S(1)}, u32[]{:S(2)}, u32[]{:S(2)}) collective-permute-start(f32[312,128]{1,0:T(8,128)} %get-tuple-element.19), channel_id=1, source_target_pairs={{0,2},{1,3},{2,0},{3,1},{4,6},{5,7},{6,4},{7,5},{8,10},{9,11},{10,... | collective-permute-start | bytes 479240 | tf_op jit(solution)/shard_map/ppermute | solution.py:338
  28.3 0.0 collective-permute-start.11
  28.3 0.0 collective-permute-done.4.refs_4_
  28.3 0.0 copy-start.11
  28.3 1.4 %collective-permute-start.13 = (f32[312,128]{1,0:T(8,128)}, f32[312,128]{1,0:T(8,128)S(1)}, u32[]{:S(2)}, u32[]{:S(2)}) collective-permute-start(f32[312,128]{1,0:T(8,128)} %get-tuple-element.21), channel_id=1, source_target_pairs={{0,6},{1,7},{2,4},{3,5},{4,2},{5,3},{6,0},{7,1},{8,14},{9,15},{10,... | collective-permute-start | bytes 479240 | tf_op jit(solution)/shard_map/ppermute | solution.py:338
  29.7 0.4 collective-permute-done.6.refs_6_
  30.0 0.0 copy-start.12
  30.0 5.6 %collective-permute-start.8 = (f32[312,128]{1,0:T(8,128)}, f32[312,128]{1,0:T(8,128)S(1)}, u32[]{:S(2)}, u32[]{:S(2)}) collective-permute-start(f32[312,128]{1,0:T(8,128)} %get-tuple-element.18.refs_0_), channel_id=1, source_target_pairs={{0,1},{1,0},{2,3},{3,2},{4,5},{5,4},{6,7},{7,6},{8,9},{9,8},{10,11... | collective-permute-start | bytes 479240 | tf_op jit(solution)/shard_map/ppermute | solution.py:338
  35.6 0.2 collective-permute-done.9.refs_2_
  35.9 0.0 copy-start.4
  35.9 5.1 %collective-permute-start.10 = (f32[312,128]{1,0:T(8,128)S(1)}, f32[312,128]{1,0:T(8,128)S(1)}, u32[]{:S(2)}, u32[]{:S(2)}) collective-permute-start(f32[312,128]{1,0:T(8,128)S(1)} %collective-permute-done.9.refs_2_), channel_id=1, source_target_pairs={{0,1},{1,0},{2,3},{3,2},{4,5},{5,4},{6,7},{7,6},{8,9},{9,8},{10,11... | collective-permute-start | bytes 479240 | tf_op jit(solution)/shard_map/ppermute | solution.py:338
  41.0 0.0 collective-permute-done.11.refs_4_
  41.0 0.0 copy-start.5
  41.0 0.1 collective-permute-start.12
  41.1 0.0 collective-permute-done.13.refs_6_
  41.1 0.0 copy-start.6
  41.1 0.4 collective-permute-start.1
  41.5 0.0 collective-permute-done.2.refs_2_
  41.5 0.0 copy-start.1
  41.5 0.1 collective-permute-start.3
  41.6 0.0 collective-permute-done.8.refs_1_
  41.6 0.0 copy-start.7
  41.6 0.4 collective-permute-start.14
  42.0 0.0 collective-permute-done.10.refs_3_
  42.0 0.0 copy-start.8
  42.0 0.3 collective-permute-start.5
  42.4 0.0 collective-permute-done.12.refs_5_
  42.4 0.0 copy-start.9
  42.4 0.2 collective-permute-start.7
  42.6 0.8 %collective-permute-done.14.refs_7_ = f32[312,128]{1,0:T(8,128)S(1)} collective-permute-done((f32[312,128]{1,0:T(8,128)S(1)}, f32[312,128]{1,0:T(8,128)S(1)}, u32[]{:S(2)}, u32[]{:S(2)}) %collective-permute-start.14) | collective-permute-done | bytes 159776 | tf_op jit(solution)/shard_map/ppermute | solution.py:338
  43.4 0.0 copy-done.4
  43.4 0.0 copy-done.5
  43.4 0.0 copy-done.6
  43.4 0.0 copy-done.7
  43.4 0.0 copy-done.8
  43.4 0.0 copy-done.9
  43.4 0.0 copy-start.10
  43.4 0.6 %copy-done.10 = f32[312,128]{1,0:T(8,128)} copy-done((f32[312,128]{1,0:T(8,128)}, f32[312,128]{1,0:T(8,128)S(1)}, u32[]{:S(2)}) %copy-start.10) | copy-done | bytes 159768
  44.1 4.7 %shard_map.18 = (f32[8,264,128]{2,1,0:T(8,128)}, bf16[3,8,128,128]{3,2,1,0:T(8,128)(2,1)}, f32[3,8,1,128]{3,2,1,0:T(1,128)}) custom-call(f32[312,128]{1,0:T(8,128)} %get-tuple-element.18.refs_0_, f32[312,128]{1,0:T(8,128)} %copy-done.7, f32[312,128]{1,0:T(8,128)} %copy-done.4, f32[312,128]{1,0:T(8,128)} %copy-done.8, f32[312,128]{1,0:T(8,128)} %copy-done.5, ...), custom_call_target="tpu_custom_call" | custom-call | tf_op jit(solution)/shard_map/pallas_call | solution.py:190
  48.7 0.0 collective-permute-done.5.refs_5_
  48.8 0.0 copy-start.13
  48.8 0.0 collective-permute-done.7.refs_7_
  48.8 0.0 copy-start.14
  48.8 0.0 collective-permute-done.1.refs_1_
  48.8 0.0 copy-start.2
  48.8 0.0 collective-permute-done.3.refs_3_
  48.8 0.0 copy-start.3
  48.8 0.0 copy-done
  48.8 0.0 copy-done.11
  48.8 0.0 copy-done.12
  48.8 0.0 copy-done.1
  48.9 0.6 copy-done.13
  49.4 0.1 copy-done.14
  49.5 0.1 copy-done.2
  49.6 0.1 copy-done.3
  49.7 7.5 %shard_map.19 = bf16[3,8,256,256]{3,2,1,0:T(8,128)(2,1)} custom-call(f32[528,128]{1,0:T(8,128)} %copy-done, f32[528,128]{1,0:T(8,128)} %copy-done.2, f32[528,128]{1,0:T(8,128)} %copy-done.1, f32[528,128]{1,0:T(8,128)} %copy-done.3, f32[312,128]{1,0:T(8,128)} %copy-done.11, f32[312,128]{1,0:T(8,128)} %copy-done.13, f32[312,128]{1,0:T(8,128)} %copy-done.12, ...), custom_call_target="tpu_custom_call" | custom-call | tf_op jit(solution)/shard_map/pallas_call | solution.py:203
Async XLA Ops:
  3.0 18.8 %collective-permute-start = (f32[528,128]{1,0:T(8,128)}, f32[528,128]{1,0:T(8,128)S(1)}, u32[]{:S(2)}, u32[]{:S(2)}) collective-permute-start(f32[528,128]{1,0:T(8,128)} %get-tuple-element.15), channel_id=1, source_target_pairs={{0,8},{1,9},{2,10},{3,11},{4,12},{5,13},{6,14},{7,15},{8,0},{9,1},... | collective-permute-start | bytes 811016 | tf_op jit(solution)/shard_map/ppermute | solution.py:338
  6.2 22.1 %collective-permute-start.4 = (f32[312,128]{1,0:T(8,128)}, f32[312,128]{1,0:T(8,128)S(1)}, u32[]{:S(2)}, u32[]{:S(2)}) collective-permute-start(f32[312,128]{1,0:T(8,128)} %get-tuple-element.16), channel_id=1, source_target_pairs={{0,12},{1,13},{2,14},{3,15},{4,8},{5,9},{6,10},{7,11},{8,4},{9,5},... | collective-permute-start | bytes 479240 | tf_op jit(solution)/shard_map/ppermute | solution.py:338
  21.8 27.0 %copy-start = (f32[528,128]{1,0:T(8,128)}, f32[528,128]{1,0:T(8,128)S(1)}, u32[]{:S(2)}) copy-start(f32[528,128]{1,0:T(8,128)S(1)} %collective-permute-done.refs_0_) | copy-start | bytes 811012
  21.8 19.7 %collective-permute-start.2 = (f32[528,128]{1,0:T(8,128)S(1)}, f32[528,128]{1,0:T(8,128)S(1)}, u32[]{:S(2)}, u32[]{:S(2)}) collective-permute-start(f32[528,128]{1,0:T(8,128)S(1)} %collective-permute-done.refs_0_), channel_id=1, source_target_pairs={{0,2},{1,3},{2,0},{3,1},{4,6},{5,7},{6,4},{7,5},{8,10},{9,11},{10,... | collective-permute-start | bytes 811016 | tf_op jit(solution)/shard_map/ppermute | solution.py:338
  22.8 7.2 %collective-permute-start.6 = (f32[312,128]{1,0:T(8,128)}, f32[312,128]{1,0:T(8,128)S(1)}, u32[]{:S(2)}, u32[]{:S(2)}) collective-permute-start(f32[312,128]{1,0:T(8,128)} %get-tuple-element.17), channel_id=1, source_target_pairs={{0,14},{1,15},{2,12},{3,13},{4,10},{5,11},{6,8},{7,9},{8,6},{9,7},... | collective-permute-start | bytes 479240 | tf_op jit(solution)/shard_map/ppermute | solution.py:338
  27.0 8.9 %collective-permute-start.9 = (f32[312,128]{1,0:T(8,128)}, f32[312,128]{1,0:T(8,128)S(1)}, u32[]{:S(2)}, u32[]{:S(2)}) collective-permute-start(f32[312,128]{1,0:T(8,128)} %get-tuple-element.19), channel_id=1, source_target_pairs={{0,2},{1,3},{2,0},{3,1},{4,6},{5,7},{6,4},{7,5},{8,10},{9,11},{10,... | collective-permute-start | bytes 479240 | tf_op jit(solution)/shard_map/ppermute | solution.py:338
  28.3 12.7 %collective-permute-start.11 = (f32[312,128]{1,0:T(8,128)}, f32[312,128]{1,0:T(8,128)S(1)}, u32[]{:S(2)}, u32[]{:S(2)}) collective-permute-start(f32[312,128]{1,0:T(8,128)} %get-tuple-element.20), channel_id=1, source_target_pairs={{0,4},{1,5},{2,6},{3,7},{4,0},{5,1},{6,2},{7,3},{8,12},{9,13},{10,... | collective-permute-start | bytes 479240 | tf_op jit(solution)/shard_map/ppermute | solution.py:338
  28.3 20.6 %copy-start.11 = (f32[312,128]{1,0:T(8,128)}, f32[312,128]{1,0:T(8,128)S(1)}, u32[]{:S(2)}) copy-start(f32[312,128]{1,0:T(8,128)S(1)} %collective-permute-done.4.refs_4_) | copy-start | bytes 479236
  28.3 12.8 %collective-permute-start.13 = (f32[312,128]{1,0:T(8,128)}, f32[312,128]{1,0:T(8,128)S(1)}, u32[]{:S(2)}, u32[]{:S(2)}) collective-permute-start(f32[312,128]{1,0:T(8,128)} %get-tuple-element.21), channel_id=1, source_target_pairs={{0,6},{1,7},{2,4},{3,5},{4,2},{5,3},{6,0},{7,1},{8,14},{9,15},{10,... | collective-permute-start | bytes 479240 | tf_op jit(solution)/shard_map/ppermute | solution.py:338
  30.0 18.8 %copy-start.12 = (f32[312,128]{1,0:T(8,128)}, f32[312,128]{1,0:T(8,128)S(1)}, u32[]{:S(2)}) copy-start(f32[312,128]{1,0:T(8,128)S(1)} %collective-permute-done.6.refs_6_) | copy-start | bytes 479236
  30.0 11.6 %collective-permute-start.8 = (f32[312,128]{1,0:T(8,128)}, f32[312,128]{1,0:T(8,128)S(1)}, u32[]{:S(2)}, u32[]{:S(2)}) collective-permute-start(f32[312,128]{1,0:T(8,128)} %get-tuple-element.18.refs_0_), channel_id=1, source_target_pairs={{0,1},{1,0},{2,3},{3,2},{4,5},{5,4},{6,7},{7,6},{8,9},{9,8},{10,11... | collective-permute-start | bytes 479240 | tf_op jit(solution)/shard_map/ppermute | solution.py:338
  35.9 7.5 %copy-start.4 = (f32[312,128]{1,0:T(8,128)}, f32[312,128]{1,0:T(8,128)S(1)}, u32[]{:S(2)}) copy-start(f32[312,128]{1,0:T(8,128)S(1)} %collective-permute-done.9.refs_2_) | copy-start | bytes 479236
  35.9 6.2 %collective-permute-start.10 = (f32[312,128]{1,0:T(8,128)S(1)}, f32[312,128]{1,0:T(8,128)S(1)}, u32[]{:S(2)}, u32[]{:S(2)}) collective-permute-start(f32[312,128]{1,0:T(8,128)S(1)} %collective-permute-done.9.refs_2_), channel_id=1, source_target_pairs={{0,1},{1,0},{2,3},{3,2},{4,5},{5,4},{6,7},{7,6},{8,9},{9,8},{10,11... | collective-permute-start | bytes 479240 | tf_op jit(solution)/shard_map/ppermute | solution.py:338
  41.0 2.4 %copy-start.5 = (f32[312,128]{1,0:T(8,128)}, f32[312,128]{1,0:T(8,128)S(1)}, u32[]{:S(2)}) copy-start(f32[312,128]{1,0:T(8,128)S(1)} %collective-permute-done.11.refs_4_) | copy-start | bytes 479236
  41.0 1.4 %collective-permute-start.12 = (f32[312,128]{1,0:T(8,128)S(1)}, f32[312,128]{1,0:T(8,128)S(1)}, u32[]{:S(2)}, u32[]{:S(2)}) collective-permute-start(f32[312,128]{1,0:T(8,128)S(1)} %collective-permute-done.11.refs_4_), channel_id=1, source_target_pairs={{0,1},{1,0},{2,3},{3,2},{4,5},{5,4},{6,7},{7,6},{8,9},{9,8},{10,11... | collective-permute-start | bytes 479240 | tf_op jit(solution)/shard_map/ppermute | solution.py:338
  41.1 2.3 %copy-start.6 = (f32[312,128]{1,0:T(8,128)}, f32[312,128]{1,0:T(8,128)S(1)}, u32[]{:S(2)}) copy-start(f32[312,128]{1,0:T(8,128)S(1)} %collective-permute-done.13.refs_6_) | copy-start | bytes 479236
  41.1 7.7 %collective-permute-start.1 = (f32[528,128]{1,0:T(8,128)S(1)}, f32[528,128]{1,0:T(8,128)S(1)}, u32[]{:S(2)}, u32[]{:S(2)}) collective-permute-start(f32[528,128]{1,0:T(8,128)S(1)} %collective-permute-done.refs_0_), channel_id=1, source_target_pairs={{0,1},{1,0},{2,3},{3,2},{4,5},{5,4},{6,7},{7,6},{8,9},{9,8},{10,11... | collective-permute-start | bytes 811016 | tf_op jit(solution)/shard_map/ppermute | solution.py:338
  41.5 7.3 %copy-start.1 = (f32[528,128]{1,0:T(8,128)}, f32[528,128]{1,0:T(8,128)S(1)}, u32[]{:S(2)}) copy-start(f32[528,128]{1,0:T(8,128)S(1)} %collective-permute-done.2.refs_2_) | copy-start | bytes 811012
  41.5 7.3 %collective-permute-start.3 = (f32[528,128]{1,0:T(8,128)S(1)}, f32[528,128]{1,0:T(8,128)S(1)}, u32[]{:S(2)}, u32[]{:S(2)}) collective-permute-start(f32[528,128]{1,0:T(8,128)S(1)} %collective-permute-done.2.refs_2_), channel_id=1, source_target_pairs={{0,1},{1,0},{2,3},{3,2},{4,5},{5,4},{6,7},{7,6},{8,9},{9,8},{10,11... | collective-permute-start | bytes 811016 | tf_op jit(solution)/shard_map/ppermute | solution.py:338
  41.6 1.8 %copy-start.7 = (f32[312,128]{1,0:T(8,128)}, f32[312,128]{1,0:T(8,128)S(1)}, u32[]{:S(2)}) copy-start(f32[312,128]{1,0:T(8,128)S(1)} %collective-permute-done.8.refs_1_) | copy-start | bytes 479236
  41.6 1.8 %collective-permute-start.14 = (f32[312,128]{1,0:T(8,128)S(1)}, f32[312,128]{1,0:T(8,128)S(1)}, u32[]{:S(2)}, u32[]{:S(2)}) collective-permute-start(f32[312,128]{1,0:T(8,128)S(1)} %collective-permute-done.13.refs_6_), channel_id=1, source_target_pairs={{0,1},{1,0},{2,3},{3,2},{4,5},{5,4},{6,7},{7,6},{8,9},{9,8},{10,11... | collective-permute-start | bytes 479240 | tf_op jit(solution)/shard_map/ppermute | solution.py:338
  42.0 1.4 %copy-start.8 = (f32[312,128]{1,0:T(8,128)}, f32[312,128]{1,0:T(8,128)S(1)}, u32[]{:S(2)}) copy-start(f32[312,128]{1,0:T(8,128)S(1)} %collective-permute-done.10.refs_3_) | copy-start | bytes 479236
  42.0 6.7 %collective-permute-start.5 = (f32[312,128]{1,0:T(8,128)S(1)}, f32[312,128]{1,0:T(8,128)S(1)}, u32[]{:S(2)}, u32[]{:S(2)}) collective-permute-start(f32[312,128]{1,0:T(8,128)S(1)} %collective-permute-done.4.refs_4_), channel_id=1, source_target_pairs={{0,1},{1,0},{2,3},{3,2},{4,5},{5,4},{6,7},{7,6},{8,9},{9,8},{10,11... | collective-permute-start | bytes 479240 | tf_op jit(solution)/shard_map/ppermute | solution.py:338
  42.4 1.0 %copy-start.9 = (f32[312,128]{1,0:T(8,128)}, f32[312,128]{1,0:T(8,128)S(1)}, u32[]{:S(2)}) copy-start(f32[312,128]{1,0:T(8,128)S(1)} %collective-permute-done.12.refs_5_) | copy-start | bytes 479236
  42.4 6.4 %collective-permute-start.7 = (f32[312,128]{1,0:T(8,128)S(1)}, f32[312,128]{1,0:T(8,128)S(1)}, u32[]{:S(2)}, u32[]{:S(2)}) collective-permute-start(f32[312,128]{1,0:T(8,128)S(1)} %collective-permute-done.6.refs_6_), channel_id=1, source_target_pairs={{0,1},{1,0},{2,3},{3,2},{4,5},{5,4},{6,7},{7,6},{8,9},{9,8},{10,11... | collective-permute-start | bytes 479240 | tf_op jit(solution)/shard_map/ppermute | solution.py:338
  43.4 0.7 %copy-start.10 = (f32[312,128]{1,0:T(8,128)}, f32[312,128]{1,0:T(8,128)S(1)}, u32[]{:S(2)}) copy-start(f32[312,128]{1,0:T(8,128)S(1)} %collective-permute-done.14.refs_7_) | copy-start | bytes 479236
  48.8 0.7 %copy-start.13 = (f32[312,128]{1,0:T(8,128)}, f32[312,128]{1,0:T(8,128)S(1)}, u32[]{:S(2)}) copy-start(f32[312,128]{1,0:T(8,128)S(1)} %collective-permute-done.5.refs_5_) | copy-start | bytes 479236
  48.8 0.7 %copy-start.14 = (f32[312,128]{1,0:T(8,128)}, f32[312,128]{1,0:T(8,128)S(1)}, u32[]{:S(2)}) copy-start(f32[312,128]{1,0:T(8,128)S(1)} %collective-permute-done.7.refs_7_) | copy-start | bytes 479236
  48.8 0.8 %copy-start.2 = (f32[528,128]{1,0:T(8,128)}, f32[528,128]{1,0:T(8,128)S(1)}, u32[]{:S(2)}) copy-start(f32[528,128]{1,0:T(8,128)S(1)} %collective-permute-done.1.refs_1_) | copy-start | bytes 811012
  48.8 0.9 %copy-start.3 = (f32[528,128]{1,0:T(8,128)}, f32[528,128]{1,0:T(8,128)S(1)}, u32[]{:S(2)}) copy-start(f32[528,128]{1,0:T(8,128)S(1)} %collective-permute-done.3.refs_3_) | copy-start | bytes 811012

commit v4 on v3

--- a/solution.py
+++ b/solution.py
@@ -23,14 +23,20 @@
     return high, low
 
 
-def windows(planes, group, first):
+def windows(planes, group, first, parts=(0, 1), sign=None):
     per_az = 2 * STEP_RG
-    inside = lax.broadcasted_iota(jnp.int32, (PAD_AZ, LANES), 0) < BOX_AZ
+    rows = PAD_AZ // 2
+    inside = lax.broadcasted_iota(jnp.int32, (rows, LANES), 0) < BOX_AZ - rows
     highs, lows = {}, {}
-    for part in range(2):
+    for place, part in enumerate(parts):
         for col in range(STEP_RG):
-            window = planes[group, pl.ds(first + part * STEP_RG + col, PAD_AZ, stride=per_az), :]
-            highs[part, col], lows[part, col] = split(jnp.where(inside, window, 0.0))
+            start = first + part * STEP_RG + col
+            top = planes[group, pl.ds(start, rows, stride=per_az), :]
+            bottom = planes[group, pl.ds(start + rows * per_az, rows, stride=per_az), :]
+            window = jnp.concatenate([top, jnp.where(inside, bottom, 0.0)], axis=0)
+            if place == 0 and sign is not None:
+                window = window * sign
+            highs[place, col], lows[place, col] = split(window)
     return highs, lows
 
 
@@ -48,6 +54,10 @@
     return [(which, 1 - part, col, 1 if part else -1) for which in thirds for part in range(2) for col in cols]
 
 
+def turned_keys(thirds, cols):
+    return [(which, 1 - part, col, -1 if part else 1) for which in thirds for part in range(2) for col in cols]
+
+
 BULK, REST, LAST = range(STEP_RG - 2), [STEP_RG - 2], [STEP_RG - 1]
 LEFT, RIGHT = (0, 0, 1), (0, 1, 0)
 
@@ -57,7 +67,7 @@
         return stacked(left, real_keys(thirds, cols)).T
 
     def rhs_of(cols):
-        sides = [stacked(right, keys(RIGHT, cols)) for right in rights for keys in (real_keys, imag_keys)]
+        sides = [stacked(right, keys(RIGHT, cols)) for right, kinds in rights for keys in kinds]
         return jnp.concatenate(sides, axis=1)
 
     dot = functools.partial(
@@ -115,7 +125,7 @@
 def near_body(prepare, planes, out_ref, roots_ref, sums, out_rows, groups):
     def make(first, group):
         pieces = windows(planes, group, first)
-        return products(pieces, [pieces])
+        return products(pieces, [(pieces, (real_keys, imag_keys))])
 
     def finish(row, group, boxes):
         roots = inverse_roots(boxes[0])
@@ -127,7 +137,7 @@
 
 def far_body(far_half, prepare, planes, near_refs, out_hbm, out_ref, sems, sums, out_rows, groups):
     near_planes, near_ref, roots_ref = near_refs
-    upper = far_half == 1
+    sign = jnp.where(far_half == 1, -1.0, 1.0)
     far_rows = pl.ds(pl.multiple_of(far_half * LANES, LANES), LANES)
     near_rows = pl.ds(pl.multiple_of((1 - far_half) * LANES, LANES), LANES)
     batch = groups // 2
@@ -135,22 +145,20 @@
 
     def make(first, group):
         pieces = windows(planes, group, first)
-        return products(pieces, [pieces, windows(near_planes, group, first)])
+        crossed = windows(near_planes, group, first, (far_half, 1 - far_half), sign)
+        return products(pieces, [(pieces, (real_keys, imag_keys)), (crossed, (real_keys, turned_keys))])
 
     def finish(row, group, boxes):
-        square, real, imag = boxes
+        square, straight, turned = boxes
         far_across = spread(inverse_roots(square))
         far_down = far_across.T
         near_across = spread(roots_ref[row, group])
         square = square * (far_down * far_across)
         scale = far_down * near_across
-        real, imag = real * scale, imag * scale
-        straight = jnp.where(upper, imag, real).astype(jnp.bfloat16)
-        turned = jnp.where(upper, real, -imag).T.astype(jnp.bfloat16)
         out_ref[row, group, near_rows, near_rows] = near_ref[row, group]
         out_ref[row, group, far_rows, far_rows] = square.astype(jnp.bfloat16)
-        out_ref[row, group, far_rows, near_rows] = straight
-        out_ref[row, group, near_rows, far_rows] = turned
+        out_ref[row, group, far_rows, near_rows] = (straight * scale).astype(jnp.bfloat16)
+        out_ref[row, group, near_rows, far_rows] = (turned * scale).astype(jnp.bfloat16).T
         if group % batch == 0:
             part = (row, pl.ds(group, batch))
             copy = pltpu.make_async_copy(out_ref.at[part], out_hbm.at[part], sems.at[len(copies)])

time: 57.6 us -> 57.6 us (level)
  no operation moved by 1% of the time
where the time goes in v4:
time: 57.6 us; the launch traced here: 57.1 us
  starting transfers between devices  24.4 us (42%)
  waiting for transfers between devices  15.9 us (28%)
  Pallas kernels  15.1 us (26%)
  local copies, waits for them, and re-layouts  1.51 us (3%)
    ppermute x15, starting transfers between devices, swap(): lax.ppermute(value, 'date', [(i, i ^ distance) for i in range(count)])  24.4 us
    ppermute x15, waiting for transfers between devices, swap(): lax.ppermute(value, 'date', [(i, i ^ distance) for i in range(count)])  15.9 us
    pallas_call x1, Pallas kernels, far_call(): pl.pallas_call(body, grid=(1,), in_specs=[whole_spec(operand) for operand...  7.44 us
    pallas_call x1, Pallas kernels, near_call(): pl.pallas_call(body, grid=(1,), in_specs=[whole_spec(operand) for operand...  4.68 us
    pallas_call x1, Pallas kernels, pack(): pl.pallas_call(functools.partial(pack_kernel, chips, groups, slab), grid=...  3 us
    unnamed x30, local copies, waits for them, and re-layouts  1.51 us
  transfers between devices with their start and end apart: 15, of which 4 were waited for; matrix products, arithmetic and copies ran while one was open for 0% of the time, Pallas kernels for 8%

profile of v4, /device:TPU:1, one launch (start us, length us, event | category | flops | bytes accessed | tf_op | source)
XLA Modules:
  0.0 57.1 jit_solution(11722642518570386318)
XLA Ops:
  0.0 3.0 %shard_map.17 = (f32[528,128]{1,0:T(8,128)}, f32[312,128]{1,0:T(8,128)}, f32[312,128]{1,0:T(8,128)}, f32[312,128]{1,0:T(8,128)}, f32[312,128]{1,0:T(8,128)}, /*index=5*/f32[312,128]{1,0:T(8,128)}, f32[312,128]{1,0:T(8,128)}) custom-call(f32[1536,144]{1,0:T(8,128)} %bitcast.3, f32[1536,144]{1,0:T(8,128)} %bitcast.4), custom_call_target="tpu_custom_call" | custom-call | tf_op jit(solution)/shard_map/pallas_call | solution.py:312
  3.0 3.2 %collective-permute-start = (f32[528,128]{1,0:T(8,128)}, f32[528,128]{1,0:T(8,128)S(1)}, u32[]{:S(2)}, u32[]{:S(2)}) collective-permute-start(f32[528,128]{1,0:T(8,128)} %get-tuple-element.15), channel_id=1, source_target_pairs={{0,8},{1,9},{2,10},{3,11},{4,12},{5,13},{6,14},{7,15},{8,0},{9,1},... | collective-permute-start | bytes 811016 | tf_op jit(solution)/shard_map/ppermute | solution.py:346
  6.2 1.1 %collective-permute-start.4 = (f32[312,128]{1,0:T(8,128)}, f32[312,128]{1,0:T(8,128)S(1)}, u32[]{:S(2)}, u32[]{:S(2)}) collective-permute-start(f32[312,128]{1,0:T(8,128)} %get-tuple-element.16), channel_id=1, source_target_pairs={{0,12},{1,13},{2,14},{3,15},{4,8},{5,9},{6,10},{7,11},{8,4},{9,5},... | collective-permute-start | bytes 479240 | tf_op jit(solution)/shard_map/ppermute | solution.py:346
  7.3 14.5 %collective-permute-done.refs_0_ = f32[528,128]{1,0:T(8,128)S(1)} collective-permute-done((f32[528,128]{1,0:T(8,128)}, f32[528,128]{1,0:T(8,128)S(1)}, u32[]{:S(2)}, u32[]{:S(2)}) %collective-permute-start) | collective-permute-done | bytes 270368 | tf_op jit(solution)/shard_map/ppermute | solution.py:346
  21.8 0.0 copy-start
  21.8 1.0 %collective-permute-start.2 = (f32[528,128]{1,0:T(8,128)S(1)}, f32[528,128]{1,0:T(8,128)S(1)}, u32[]{:S(2)}, u32[]{:S(2)}) collective-permute-start(f32[528,128]{1,0:T(8,128)S(1)} %collective-permute-done.refs_0_), channel_id=1, source_target_pairs={{0,2},{1,3},{2,0},{3,1},{4,6},{5,7},{6,4},{7,5},{8,10},{9,11},{10,... | collective-permute-start | bytes 811016 | tf_op jit(solution)/shard_map/ppermute | solution.py:346
  22.8 4.2 %collective-permute-start.6 = (f32[312,128]{1,0:T(8,128)}, f32[312,128]{1,0:T(8,128)S(1)}, u32[]{:S(2)}, u32[]{:S(2)}) collective-permute-start(f32[312,128]{1,0:T(8,128)} %get-tuple-element.17), channel_id=1, source_target_pairs={{0,14},{1,15},{2,12},{3,13},{4,10},{5,11},{6,8},{7,9},{8,6},{9,7},... | collective-permute-start | bytes 479240 | tf_op jit(solution)/shard_map/ppermute | solution.py:346
  27.0 1.2 %collective-permute-start.9 = (f32[312,128]{1,0:T(8,128)}, f32[312,128]{1,0:T(8,128)S(1)}, u32[]{:S(2)}, u32[]{:S(2)}) collective-permute-start(f32[312,128]{1,0:T(8,128)} %get-tuple-element.19), channel_id=1, source_target_pairs={{0,2},{1,3},{2,0},{3,1},{4,6},{5,7},{6,4},{7,5},{8,10},{9,11},{10,... | collective-permute-start | bytes 479240 | tf_op jit(solution)/shard_map/ppermute | solution.py:346
  28.3 0.0 collective-permute-start.11
  28.3 0.0 collective-permute-done.4.refs_4_
  28.3 0.0 copy-start.11
  28.3 1.4 %collective-permute-start.13 = (f32[312,128]{1,0:T(8,128)}, f32[312,128]{1,0:T(8,128)S(1)}, u32[]{:S(2)}, u32[]{:S(2)}) collective-permute-start(f32[312,128]{1,0:T(8,128)} %get-tuple-element.21), channel_id=1, source_target_pairs={{0,6},{1,7},{2,4},{3,5},{4,2},{5,3},{6,0},{7,1},{8,14},{9,15},{10,... | collective-permute-start | bytes 479240 | tf_op jit(solution)/shard_map/ppermute | solution.py:346
  29.7 0.4 collective-permute-done.6.refs_6_
  30.0 0.0 copy-start.12
  30.0 5.6 %collective-permute-start.8 = (f32[312,128]{1,0:T(8,128)}, f32[312,128]{1,0:T(8,128)S(1)}, u32[]{:S(2)}, u32[]{:S(2)}) collective-permute-start(f32[312,128]{1,0:T(8,128)} %get-tuple-element.18.refs_0_), channel_id=1, source_target_pairs={{0,1},{1,0},{2,3},{3,2},{4,5},{5,4},{6,7},{7,6},{8,9},{9,8},{10,11... | collective-permute-start | bytes 479240 | tf_op jit(solution)/shard_map/ppermute | solution.py:346
  35.6 0.2 collective-permute-done.9.refs_2_
  35.9 0.0 copy-start.4
  35.9 5.1 %collective-permute-start.10 = (f32[312,128]{1,0:T(8,128)S(1)}, f32[312,128]{1,0:T(8,128)S(1)}, u32[]{:S(2)}, u32[]{:S(2)}) collective-permute-start(f32[312,128]{1,0:T(8,128)S(1)} %collective-permute-done.9.refs_2_), channel_id=1, source_target_pairs={{0,1},{1,0},{2,3},{3,2},{4,5},{5,4},{6,7},{7,6},{8,9},{9,8},{10,11... | collective-permute-start | bytes 479240 | tf_op jit(solution)/shard_map/ppermute | solution.py:346
  41.0 0.0 collective-permute-done.11.refs_4_
  41.0 0.0 copy-start.5
  41.0 0.1 collective-permute-start.12
  41.1 0.0 collective-permute-done.13.refs_6_
  41.1 0.0 copy-start.6
  41.1 0.4 collective-permute-start.1
  41.5 0.0 collective-permute-done.2.refs_2_
  41.5 0.0 copy-start.1
  41.5 0.1 collective-permute-start.3
  41.6 0.0 collective-permute-done.8.refs_1_
  41.6 0.0 copy-start.7
  41.6 0.4 collective-permute-start.14
  42.0 0.0 collective-permute-done.10.refs_3_
  42.0 0.0 copy-start.8
  42.0 0.3 collective-permute-start.5
  42.4 0.0 collective-permute-done.12.refs_5_
  42.4 0.0 copy-start.9
  42.4 0.2 collective-permute-start.7
  42.6 0.8 %collective-permute-done.14.refs_7_ = f32[312,128]{1,0:T(8,128)S(1)} collective-permute-done((f32[312,128]{1,0:T(8,128)S(1)}, f32[312,128]{1,0:T(8,128)S(1)}, u32[]{:S(2)}, u32[]{:S(2)}) %collective-permute-start.14) | collective-permute-done | bytes 159776 | tf_op jit(solution)/shard_map/ppermute | solution.py:346
  43.4 0.0 copy-done.4
  43.4 0.0 copy-done.5
  43.4 0.0 copy-done.6
  43.4 0.0 copy-done.7
  43.4 0.0 copy-done.8
  43.4 0.0 copy-done.9
  43.4 0.0 copy-start.10
  43.4 0.6 %copy-done.10 = f32[312,128]{1,0:T(8,128)} copy-done((f32[312,128]{1,0:T(8,128)}, f32[312,128]{1,0:T(8,128)S(1)}, u32[]{:S(2)}) %copy-start.10) | copy-done | bytes 159768
  44.1 4.7 %shard_map.18 = (f32[8,264,128]{2,1,0:T(8,128)}, bf16[3,8,128,128]{3,2,1,0:T(8,128)(2,1)}, f32[3,8,1,128]{3,2,1,0:T(1,128)}) custom-call(f32[312,128]{1,0:T(8,128)} %get-tuple-element.18.refs_0_, f32[312,128]{1,0:T(8,128)} %copy-done.7, f32[312,128]{1,0:T(8,128)} %copy-done.4, f32[312,128]{1,0:T(8,128)} %copy-done.8, f32[312,128]{1,0:T(8,128)} %copy-done.5, ...), custom_call_target="tpu_custom_call" | custom-call | tf_op jit(solution)/shard_map/pallas_call | solution.py:198
  48.8 0.0 collective-permute-done.5.refs_5_
  48.8 0.0 copy-start.13
  48.8 0.0 collective-permute-done.7.refs_7_
  48.8 0.0 copy-start.14
  48.8 0.0 collective-permute-done.1.refs_1_
  48.8 0.0 copy-start.2
  48.8 0.0 collective-permute-done.3.refs_3_
  48.8 0.0 copy-start.3
  48.8 0.0 copy-done
  48.8 0.0 copy-done.11
  48.8 0.0 copy-done.12
  48.9 0.0 copy-done.1
  48.9 0.6 copy-done.13
  49.4 0.1 copy-done.14
  49.5 0.1 copy-done.2
  49.6 0.1 copy-done.3
  49.7 7.4 %shard_map.19 = bf16[3,8,256,256]{3,2,1,0:T(8,128)(2,1)} custom-call(f32[528,128]{1,0:T(8,128)} %copy-done, f32[528,128]{1,0:T(8,128)} %copy-done.2, f32[528,128]{1,0:T(8,128)} %copy-done.1, f32[528,128]{1,0:T(8,128)} %copy-done.3, f32[312,128]{1,0:T(8,128)} %copy-done.11, f32[312,128]{1,0:T(8,128)} %copy-done.13, f32[312,128]{1,0:T(8,128)} %copy-done.12, ...), custom_call_target="tpu_custom_call" | custom-call | tf_op jit(solution)/shard_map/pallas_call | solution.py:211
Async XLA Ops:
  3.0 18.8 %collective-permute-start = (f32[528,128]{1,0:T(8,128)}, f32[528,128]{1,0:T(8,128)S(1)}, u32[]{:S(2)}, u32[]{:S(2)}) collective-permute-start(f32[528,128]{1,0:T(8,128)} %get-tuple-element.15), channel_id=1, source_target_pairs={{0,8},{1,9},{2,10},{3,11},{4,12},{5,13},{6,14},{7,15},{8,0},{9,1},... | collective-permute-start | bytes 811016 | tf_op jit(solution)/shard_map/ppermute | solution.py:346
  6.2 22.1 %collective-permute-start.4 = (f32[312,128]{1,0:T(8,128)}, f32[312,128]{1,0:T(8,128)S(1)}, u32[]{:S(2)}, u32[]{:S(2)}) collective-permute-start(f32[312,128]{1,0:T(8,128)} %get-tuple-element.16), channel_id=1, source_target_pairs={{0,12},{1,13},{2,14},{3,15},{4,8},{5,9},{6,10},{7,11},{8,4},{9,5},... | collective-permute-start | bytes 479240 | tf_op jit(solution)/shard_map/ppermute | solution.py:346
  21.8 27.0 %copy-start = (f32[528,128]{1,0:T(8,128)}, f32[528,128]{1,0:T(8,128)S(1)}, u32[]{:S(2)}) copy-start(f32[528,128]{1,0:T(8,128)S(1)} %collective-permute-done.refs_0_) | copy-start | bytes 811012
  21.8 19.7 %collective-permute-start.2 = (f32[528,128]{1,0:T(8,128)S(1)}, f32[528,128]{1,0:T(8,128)S(1)}, u32[]{:S(2)}, u32[]{:S(2)}) collective-permute-start(f32[528,128]{1,0:T(8,128)S(1)} %collective-permute-done.refs_0_), channel_id=1, source_target_pairs={{0,2},{1,3},{2,0},{3,1},{4,6},{5,7},{6,4},{7,5},{8,10},{9,11},{10,... | collective-permute-start | bytes 811016 | tf_op jit(solution)/shard_map/ppermute | solution.py:346
  22.8 7.2 %collective-permute-start.6 = (f32[312,128]{1,0:T(8,128)}, f32[312,128]{1,0:T(8,128)S(1)}, u32[]{:S(2)}, u32[]{:S(2)}) collective-permute-start(f32[312,128]{1,0:T(8,128)} %get-tuple-element.17), channel_id=1, source_target_pairs={{0,14},{1,15},{2,12},{3,13},{4,10},{5,11},{6,8},{7,9},{8,6},{9,7},... | collective-permute-start | bytes 479240 | tf_op jit(solution)/shard_map/ppermute | solution.py:346
  27.0 8.9 %collective-permute-start.9 = (f32[312,128]{1,0:T(8,128)}, f32[312,128]{1,0:T(8,128)S(1)}, u32[]{:S(2)}, u32[]{:S(2)}) collective-permute-start(f32[312,128]{1,0:T(8,128)} %get-tuple-element.19), channel_id=1, source_target_pairs={{0,2},{1,3},{2,0},{3,1},{4,6},{5,7},{6,4},{7,5},{8,10},{9,11},{10,... | collective-permute-start | bytes 479240 | tf_op jit(solution)/shard_map/ppermute | solution.py:346
  28.3 12.7 %collective-permute-start.11 = (f32[312,128]{1,0:T(8,128)}, f32[312,128]{1,0:T(8,128)S(1)}, u32[]{:S(2)}, u32[]{:S(2)}) collective-permute-start(f32[312,128]{1,0:T(8,128)} %get-tuple-element.20), channel_id=1, source_target_pairs={{0,4},{1,5},{2,6},{3,7},{4,0},{5,1},{6,2},{7,3},{8,12},{9,13},{10,... | collective-permute-start | bytes 479240 | tf_op jit(solution)/shard_map/ppermute | solution.py:346
  28.3 20.6 %copy-start.11 = (f32[312,128]{1,0:T(8,128)}, f32[312,128]{1,0:T(8,128)S(1)}, u32[]{:S(2)}) copy-start(f32[312,128]{1,0:T(8,128)S(1)} %collective-permute-done.4.refs_4_) | copy-start | bytes 479236
  28.3 12.8 %collective-permute-start.13 = (f32[312,128]{1,0:T(8,128)}, f32[312,128]{1,0:T(8,128)S(1)}, u32[]{:S(2)}, u32[]{:S(2)}) collective-permute-start(f32[312,128]{1,0:T(8,128)} %get-tuple-element.21), channel_id=1, source_target_pairs={{0,6},{1,7},{2,4},{3,5},{4,2},{5,3},{6,0},{7,1},{8,14},{9,15},{10,... | collective-permute-start | bytes 479240 | tf_op jit(solution)/shard_map/ppermute | solution.py:346
  30.0 18.8 %copy-start.12 = (f32[312,128]{1,0:T(8,128)}, f32[312,128]{1,0:T(8,128)S(1)}, u32[]{:S(2)}) copy-start(f32[312,128]{1,0:T(8,128)S(1)} %collective-permute-done.6.refs_6_) | copy-start | bytes 479236
  30.0 11.6 %collective-permute-start.8 = (f32[312,128]{1,0:T(8,128)}, f32[312,128]{1,0:T(8,128)S(1)}, u32[]{:S(2)}, u32[]{:S(2)}) collective-permute-start(f32[312,128]{1,0:T(8,128)} %get-tuple-element.18.refs_0_), channel_id=1, source_target_pairs={{0,1},{1,0},{2,3},{3,2},{4,5},{5,4},{6,7},{7,6},{8,9},{9,8},{10,11... | collective-permute-start | bytes 479240 | tf_op jit(solution)/shard_map/ppermute | solution.py:346
  35.9 7.5 %copy-start.4 = (f32[312,128]{1,0:T(8,128)}, f32[312,128]{1,0:T(8,128)S(1)}, u32[]{:S(2)}) copy-start(f32[312,128]{1,0:T(8,128)S(1)} %collective-permute-done.9.refs_2_) | copy-start | bytes 479236
  35.9 6.2 %collective-permute-start.10 = (f32[312,128]{1,0:T(8,128)S(1)}, f32[312,128]{1,0:T(8,128)S(1)}, u32[]{:S(2)}, u32[]{:S(2)}) collective-permute-start(f32[312,128]{1,0:T(8,128)S(1)} %collective-permute-done.9.refs_2_), channel_id=1, source_target_pairs={{0,1},{1,0},{2,3},{3,2},{4,5},{5,4},{6,7},{7,6},{8,9},{9,8},{10,11... | collective-permute-start | bytes 479240 | tf_op jit(solution)/shard_map/ppermute | solution.py:346
  41.0 2.4 %copy-start.5 = (f32[312,128]{1,0:T(8,128)}, f32[312,128]{1,0:T(8,128)S(1)}, u32[]{:S(2)}) copy-start(f32[312,128]{1,0:T(8,128)S(1)} %collective-permute-done.11.refs_4_) | copy-start | bytes 479236
  41.0 1.4 %collective-permute-start.12 = (f32[312,128]{1,0:T(8,128)S(1)}, f32[312,128]{1,0:T(8,128)S(1)}, u32[]{:S(2)}, u32[]{:S(2)}) collective-permute-start(f32[312,128]{1,0:T(8,128)S(1)} %collective-permute-done.11.refs_4_), channel_id=1, source_target_pairs={{0,1},{1,0},{2,3},{3,2},{4,5},{5,4},{6,7},{7,6},{8,9},{9,8},{10,11... | collective-permute-start | bytes 479240 | tf_op jit(solution)/shard_map/ppermute | solution.py:346
  41.1 2.3 %copy-start.6 = (f32[312,128]{1,0:T(8,128)}, f32[312,128]{1,0:T(8,128)S(1)}, u32[]{:S(2)}) copy-start(f32[312,128]{1,0:T(8,128)S(1)} %collective-permute-done.13.refs_6_) | copy-start | bytes 479236
  41.1 7.7 %collective-permute-start.1 = (f32[528,128]{1,0:T(8,128)S(1)}, f32[528,128]{1,0:T(8,128)S(1)}, u32[]{:S(2)}, u32[]{:S(2)}) collective-permute-start(f32[528,128]{1,0:T(8,128)S(1)} %collective-permute-done.refs_0_), channel_id=1, source_target_pairs={{0,1},{1,0},{2,3},{3,2},{4,5},{5,4},{6,7},{7,6},{8,9},{9,8},{10,11... | collective-permute-start | bytes 811016 | tf_op jit(solution)/shard_map/ppermute | solution.py:346
  41.5 7.3 %copy-start.1 = (f32[528,128]{1,0:T(8,128)}, f32[528,128]{1,0:T(8,128)S(1)}, u32[]{:S(2)}) copy-start(f32[528,128]{1,0:T(8,128)S(1)} %collective-permute-done.2.refs_2_) | copy-start | bytes 811012
  41.5 7.3 %collective-permute-start.3 = (f32[528,128]{1,0:T(8,128)S(1)}, f32[528,128]{1,0:T(8,128)S(1)}, u32[]{:S(2)}, u32[]{:S(2)}) collective-permute-start(f32[528,128]{1,0:T(8,128)S(1)} %collective-permute-done.2.refs_2_), channel_id=1, source_target_pairs={{0,1},{1,0},{2,3},{3,2},{4,5},{5,4},{6,7},{7,6},{8,9},{9,8},{10,11... | collective-permute-start | bytes 811016 | tf_op jit(solution)/shard_map/ppermute | solution.py:346
  41.6 1.8 %copy-start.7 = (f32[312,128]{1,0:T(8,128)}, f32[312,128]{1,0:T(8,128)S(1)}, u32[]{:S(2)}) copy-start(f32[312,128]{1,0:T(8,128)S(1)} %collective-permute-done.8.refs_1_) | copy-start | bytes 479236
  41.6 1.8 %collective-permute-start.14 = (f32[312,128]{1,0:T(8,128)S(1)}, f32[312,128]{1,0:T(8,128)S(1)}, u32[]{:S(2)}, u32[]{:S(2)}) collective-permute-start(f32[312,128]{1,0:T(8,128)S(1)} %collective-permute-done.13.refs_6_), channel_id=1, source_target_pairs={{0,1},{1,0},{2,3},{3,2},{4,5},{5,4},{6,7},{7,6},{8,9},{9,8},{10,11... | collective-permute-start | bytes 479240 | tf_op jit(solution)/shard_map/ppermute | solution.py:346
  42.0 1.4 %copy-start.8 = (f32[312,128]{1,0:T(8,128)}, f32[312,128]{1,0:T(8,128)S(1)}, u32[]{:S(2)}) copy-start(f32[312,128]{1,0:T(8,128)S(1)} %collective-permute-done.10.refs_3_) | copy-start | bytes 479236
  42.0 6.7 %collective-permute-start.5 = (f32[312,128]{1,0:T(8,128)S(1)}, f32[312,128]{1,0:T(8,128)S(1)}, u32[]{:S(2)}, u32[]{:S(2)}) collective-permute-start(f32[312,128]{1,0:T(8,128)S(1)} %collective-permute-done.4.refs_4_), channel_id=1, source_target_pairs={{0,1},{1,0},{2,3},{3,2},{4,5},{5,4},{6,7},{7,6},{8,9},{9,8},{10,11... | collective-permute-start | bytes 479240 | tf_op jit(solution)/shard_map/ppermute | solution.py:346
  42.4 1.0 %copy-start.9 = (f32[312,128]{1,0:T(8,128)}, f32[312,128]{1,0:T(8,128)S(1)}, u32[]{:S(2)}) copy-start(f32[312,128]{1,0:T(8,128)S(1)} %collective-permute-done.12.refs_5_) | copy-start | bytes 479236
  42.4 6.4 %collective-permute-start.7 = (f32[312,128]{1,0:T(8,128)S(1)}, f32[312,128]{1,0:T(8,128)S(1)}, u32[]{:S(2)}, u32[]{:S(2)}) collective-permute-start(f32[312,128]{1,0:T(8,128)S(1)} %collective-permute-done.6.refs_6_), channel_id=1, source_target_pairs={{0,1},{1,0},{2,3},{3,2},{4,5},{5,4},{6,7},{7,6},{8,9},{9,8},{10,11... | collective-permute-start | bytes 479240 | tf_op jit(solution)/shard_map/ppermute | solution.py:346
  43.4 0.7 %copy-start.10 = (f32[312,128]{1,0:T(8,128)}, f32[312,128]{1,0:T(8,128)S(1)}, u32[]{:S(2)}) copy-start(f32[312,128]{1,0:T(8,128)S(1)} %collective-permute-done.14.refs_7_) | copy-start | bytes 479236
  48.8 0.7 %copy-start.13 = (f32[312,128]{1,0:T(8,128)}, f32[312,128]{1,0:T(8,128)S(1)}, u32[]{:S(2)}) copy-start(f32[312,128]{1,0:T(8,128)S(1)} %collective-permute-done.5.refs_5_) | copy-start | bytes 479236
  48.8 0.7 %copy-start.14 = (f32[312,128]{1,0:T(8,128)}, f32[312,128]{1,0:T(8,128)S(1)}, u32[]{:S(2)}) copy-start(f32[312,128]{1,0:T(8,128)S(1)} %collective-permute-done.7.refs_7_) | copy-start | bytes 479236
  48.8 0.8 %copy-start.2 = (f32[528,128]{1,0:T(8,128)}, f32[528,128]{1,0:T(8,128)S(1)}, u32[]{:S(2)}) copy-start(f32[528,128]{1,0:T(8,128)S(1)} %collective-permute-done.1.refs_1_) | copy-start | bytes 811012
  48.8 0.9 %copy-start.3 = (f32[528,128]{1,0:T(8,128)}, f32[528,128]{1,0:T(8,128)S(1)}, u32[]{:S(2)}) copy-start(f32[528,128]{1,0:T(8,128)S(1)} %collective-permute-done.3.refs_3_) | copy-start | bytes 811012

commit v5 on v4

--- a/solution.py
+++ b/solution.py
@@ -9,6 +9,7 @@
 
 
 BOX_AZ = 11
+BOX_RG = 23
 STEP_AZ = 3
 STEP_RG = 6
 MARGIN = 8
@@ -23,20 +24,34 @@
     return high, low
 
 
-def windows(planes, group, first, parts=(0, 1), sign=None):
+def windows(planes, group, first, whole, parts=(0, 1), sign=None):
     per_az = 2 * STEP_RG
     rows = PAD_AZ // 2
-    inside = lax.broadcasted_iota(jnp.int32, (rows, LANES), 0) < BOX_AZ - rows
+    slot = rows // 2
+    spot = lax.broadcasted_iota(jnp.int32, (rows, LANES), 0)
+    early = spot < BOX_AZ - rows
+    late = (spot >= slot) & (spot < slot + BOX_AZ - rows)
     highs, lows = {}, {}
     for place, part in enumerate(parts):
-        for col in range(STEP_RG):
-            start = first + part * STEP_RG + col
-            top = planes[group, pl.ds(start, rows, stride=per_az), :]
-            bottom = planes[group, pl.ds(start + rows * per_az, rows, stride=per_az), :]
-            window = jnp.concatenate([top, jnp.where(inside, bottom, 0.0)], axis=0)
+
+        def load(col, az):
+            return planes[group, pl.ds(first + az * per_az + part * STEP_RG + col, rows, stride=per_az), :]
+
+        def ends(col, other=None):
+            kept = jnp.where(early, load(col, rows), 0.0)
+            return kept if other is None else jnp.where(late, load(other, rows - slot), kept)
+
+        tops = [load(col, 0) for col in range(STEP_RG)]
+        pairs = [(tops[0], tops[1]), (tops[2], tops[3])]
+        if whole:
+            pairs += [(tops[4], tops[5]), (ends(0, 1), ends(2, 3)), (ends(4, 5), jnp.zeros_like(tops[0]))]
+        else:
+            pairs += [(tops[4], ends(4)), (ends(0, 1), ends(2, 3)), (tops[5], ends(5))]
+        for unit, pair in enumerate(pairs):
+            window = jnp.concatenate(pair, axis=0)
             if place == 0 and sign is not None:
                 window = window * sign
-            highs[place, col], lows[place, col] = split(window)
+            highs[place, unit], lows[place, unit] = split(window)
     return highs, lows
 
 
@@ -58,25 +73,27 @@
     return [(which, 1 - part, col, -1 if part else 1) for which in thirds for part in range(2) for col in cols]
 
 
-BULK, REST, LAST = range(STEP_RG - 2), [STEP_RG - 2], [STEP_RG - 1]
+BULK, LAST = range(4), [4]
 LEFT, RIGHT = (0, 0, 1), (0, 1, 0)
 
 
-def products(left, rights):
-    def lhs_of(thirds, cols):
-        return stacked(left, real_keys(thirds, cols)).T
-
-    def rhs_of(cols):
-        sides = [stacked(right, keys(RIGHT, cols)) for right, kinds in rights for keys in kinds]
+def products(left, rights, whole):
+    def lhs_of(thirds, units):
+        return stacked(left, real_keys(thirds, units)).T
+
+    def rhs_of(units):
+        sides = [stacked(right, keys(RIGHT, units)) for right, kinds in rights for keys in kinds]
         return jnp.concatenate(sides, axis=1)
 
     dot = functools.partial(
         lax.dot_general, dimension_numbers=(((1,), (0,)), ((), ())), preferred_element_type=jnp.float32
     )
     high, low = lhs_of([0], BULK), lhs_of([1], BULK)
-    lhs = jnp.concatenate([high, high, low, lhs_of(LEFT, REST)], axis=1)
-    rhs = jnp.concatenate([rhs_of(BULK), rhs_of(REST)], axis=0)
-    return dot(lhs, rhs), dot(lhs_of(LEFT, LAST), rhs_of(LAST))
+    bulk = [high, high, low]
+    if whole:
+        lhs = jnp.concatenate(bulk + [lhs_of(LEFT, LAST)], axis=1)
+        return None, dot(lhs, jnp.concatenate([rhs_of(BULK), rhs_of(LAST)], axis=0))
+    return dot(jnp.concatenate(bulk, axis=1), rhs_of(BULK)), dot(lhs_of(LEFT, LAST), rhs_of(LAST))
 
 
 def square_iotas():
@@ -89,14 +106,21 @@
     return [jnp.where(up >= low, cut[0], cut[1])] + cut[2:]
 
 
-def box_sums(made, fresh, last_partial, pending, pair):
+def box_sums(made, group, groups, last_partial, pending, pair):
+    partials, lasts = made
+    fresh = group == groups - 1
     boxes = []
-    for i, (partial, last) in enumerate(zip(blocks_of(made[0]), blocks_of(made[1]))):
-        full = partial + last
+    lasts = blocks_of(lasts)
+    partials = [None] * len(lasts) if partials is None else blocks_of(partials)
+    for i, (partial, last) in enumerate(zip(partials, lasts)):
+        full = last if partial is None else partial + last
         boxes.append(full if fresh else full + pending[i])
-        pending[i] = full if fresh else full + pair[i]
-        pair[i] = full if fresh else full + last_partial[i]
-        last_partial[i] = partial
+        if group >= 1:
+            pending[i] = full if fresh else full + pair[i]
+        if group >= 2:
+            pair[i] = full if fresh else full + last_partial[i]
+        if partial is not None:
+            last_partial[i] = partial
     return boxes
 
 
@@ -117,15 +141,20 @@
                 prepare(group)
             made = make(row * (STEP_AZ * 2 * STEP_RG), group)
             if ready is not None:
-                finish(*ready[:2], box_sums(ready[2], ready[1] == groups - 1, *sums))
+                finish(*ready[:2], box_sums(ready[2], ready[1], groups, *sums))
             ready = (row, group, made)
-    finish(*ready[:2], box_sums(ready[2], groups == 1, *sums))
+    finish(*ready[:2], box_sums(ready[2], ready[1], groups, *sums))
+
+
+def needs_split():
+    return BOX_RG // STEP_RG
 
 
 def near_body(prepare, planes, out_ref, roots_ref, sums, out_rows, groups):
     def make(first, group):
-        pieces = windows(planes, group, first)
-        return products(pieces, [(pieces, (real_keys, imag_keys))])
+        whole = group < needs_split()
+        pieces = windows(planes, group, first, whole)
+        return products(pieces, [(pieces, (real_keys, imag_keys))], whole)
 
     def finish(row, group, boxes):
         roots = inverse_roots(boxes[0])
@@ -144,9 +173,10 @@
     copies = []
 
     def make(first, group):
-        pieces = windows(planes, group, first)
-        crossed = windows(near_planes, group, first, (far_half, 1 - far_half), sign)
-        return products(pieces, [(pieces, (real_keys, imag_keys)), (crossed, (real_keys, turned_keys))])
+        whole = group < needs_split()
+        pieces = windows(planes, group, first, whole)
+        crossed = windows(near_planes, group, first, whole, (far_half, 1 - far_half), sign)
+        return products(pieces, [(pieces, (real_keys, imag_keys)), (crossed, (real_keys, turned_keys))], whole)
 
     def finish(row, group, boxes):
         square, straight, turned = boxes

time: 57.6 us -> 56.7 us (0.984)
  Pallas kernels: 15.1 us -> 14.3 us
where the time goes in v5:
time: 56.7 us; the launch traced here: 56.3 us
  starting transfers between devices  24.4 us (43%)
  waiting for transfers between devices  15.9 us (28%)
  Pallas kernels  14.3 us (25%)
  local copies, waits for them, and re-layouts  1.51 us (3%)
    ppermute x15, starting transfers between devices, swap(): lax.ppermute(value, 'date', [(i, i ^ distance) for i in range(count)])  24.4 us
    ppermute x15, waiting for transfers between devices, swap(): lax.ppermute(value, 'date', [(i, i ^ distance) for i in range(count)])  15.9 us
    pallas_call x1, Pallas kernels, far_call(): pl.pallas_call(body, grid=(1,), in_specs=[whole_spec(operand) for operand...  6.89 us
    pallas_call x1, Pallas kernels, near_call(): pl.pallas_call(body, grid=(1,), in_specs=[whole_spec(operand) for operand...  4.41 us
    pallas_call x1, Pallas kernels, pack(): pl.pallas_call(functools.partial(pack_kernel, chips, groups, slab), grid=...  3 us
    unnamed x30, local copies, waits for them, and re-layouts  1.51 us
  transfers between devices with their start and end apart: 15, of which 4 were waited for; matrix products, arithmetic and copies ran while one was open for 0% of the time, Pallas kernels for 8%

profile of v5, /device:TPU:1, one launch (start us, length us, event | category | flops | bytes accessed | tf_op | source)
XLA Modules:
  0.0 56.3 jit_solution(6676343547442443277)
XLA Ops:
  0.0 3.0 %shard_map.17 = (f32[528,128]{1,0:T(8,128)}, f32[312,128]{1,0:T(8,128)}, f32[312,128]{1,0:T(8,128)}, f32[312,128]{1,0:T(8,128)}, f32[312,128]{1,0:T(8,128)}, /*index=5*/f32[312,128]{1,0:T(8,128)}, f32[312,128]{1,0:T(8,128)}) custom-call(f32[1536,144]{1,0:T(8,128)} %bitcast.3, f32[1536,144]{1,0:T(8,128)} %bitcast.4), custom_call_target="tpu_custom_call" | custom-call | tf_op jit(solution)/shard_map/pallas_call | solution.py:342
  3.0 3.2 %collective-permute-start = (f32[528,128]{1,0:T(8,128)}, f32[528,128]{1,0:T(8,128)S(1)}, u32[]{:S(2)}, u32[]{:S(2)}) collective-permute-start(f32[528,128]{1,0:T(8,128)} %get-tuple-element.15), channel_id=1, source_target_pairs={{0,8},{1,9},{2,10},{3,11},{4,12},{5,13},{6,14},{7,15},{8,0},{9,1},... | collective-permute-start | bytes 811016 | tf_op jit(solution)/shard_map/ppermute | solution.py:376
  6.2 1.1 %collective-permute-start.4 = (f32[312,128]{1,0:T(8,128)}, f32[312,128]{1,0:T(8,128)S(1)}, u32[]{:S(2)}, u32[]{:S(2)}) collective-permute-start(f32[312,128]{1,0:T(8,128)} %get-tuple-element.16), channel_id=1, source_target_pairs={{0,12},{1,13},{2,14},{3,15},{4,8},{5,9},{6,10},{7,11},{8,4},{9,5},... | collective-permute-start | bytes 479240 | tf_op jit(solution)/shard_map/ppermute | solution.py:376
  7.3 14.5 %collective-permute-done.refs_0_ = f32[528,128]{1,0:T(8,128)S(1)} collective-permute-done((f32[528,128]{1,0:T(8,128)}, f32[528,128]{1,0:T(8,128)S(1)}, u32[]{:S(2)}, u32[]{:S(2)}) %collective-permute-start) | collective-permute-done | bytes 270368 | tf_op jit(solution)/shard_map/ppermute | solution.py:376
  21.8 0.0 copy-start
  21.8 1.0 %collective-permute-start.2 = (f32[528,128]{1,0:T(8,128)S(1)}, f32[528,128]{1,0:T(8,128)S(1)}, u32[]{:S(2)}, u32[]{:S(2)}) collective-permute-start(f32[528,128]{1,0:T(8,128)S(1)} %collective-permute-done.refs_0_), channel_id=1, source_target_pairs={{0,2},{1,3},{2,0},{3,1},{4,6},{5,7},{6,4},{7,5},{8,10},{9,11},{10,... | collective-permute-start | bytes 811016 | tf_op jit(solution)/shard_map/ppermute | solution.py:376
  22.8 4.2 %collective-permute-start.6 = (f32[312,128]{1,0:T(8,128)}, f32[312,128]{1,0:T(8,128)S(1)}, u32[]{:S(2)}, u32[]{:S(2)}) collective-permute-start(f32[312,128]{1,0:T(8,128)} %get-tuple-element.17), channel_id=1, source_target_pairs={{0,14},{1,15},{2,12},{3,13},{4,10},{5,11},{6,8},{7,9},{8,6},{9,7},... | collective-permute-start | bytes 479240 | tf_op jit(solution)/shard_map/ppermute | solution.py:376
  27.0 1.2 %collective-permute-start.9 = (f32[312,128]{1,0:T(8,128)}, f32[312,128]{1,0:T(8,128)S(1)}, u32[]{:S(2)}, u32[]{:S(2)}) collective-permute-start(f32[312,128]{1,0:T(8,128)} %get-tuple-element.19), channel_id=1, source_target_pairs={{0,2},{1,3},{2,0},{3,1},{4,6},{5,7},{6,4},{7,5},{8,10},{9,11},{10,... | collective-permute-start | bytes 479240 | tf_op jit(solution)/shard_map/ppermute | solution.py:376
  28.3 0.0 collective-permute-start.11
  28.3 0.0 collective-permute-done.4.refs_4_
  28.3 0.0 copy-start.11
  28.3 1.4 %collective-permute-start.13 = (f32[312,128]{1,0:T(8,128)}, f32[312,128]{1,0:T(8,128)S(1)}, u32[]{:S(2)}, u32[]{:S(2)}) collective-permute-start(f32[312,128]{1,0:T(8,128)} %get-tuple-element.21), channel_id=1, source_target_pairs={{0,6},{1,7},{2,4},{3,5},{4,2},{5,3},{6,0},{7,1},{8,14},{9,15},{10,... | collective-permute-start | bytes 479240 | tf_op jit(solution)/shard_map/ppermute | solution.py:376
  29.7 0.4 collective-permute-done.6.refs_6_
  30.0 0.0 copy-start.12
  30.0 5.6 %collective-permute-start.8 = (f32[312,128]{1,0:T(8,128)}, f32[312,128]{1,0:T(8,128)S(1)}, u32[]{:S(2)}, u32[]{:S(2)}) collective-permute-start(f32[312,128]{1,0:T(8,128)} %get-tuple-element.18.refs_0_), channel_id=1, source_target_pairs={{0,1},{1,0},{2,3},{3,2},{4,5},{5,4},{6,7},{7,6},{8,9},{9,8},{10,11... | collective-permute-start | bytes 479240 | tf_op jit(solution)/shard_map/ppermute | solution.py:376
  35.6 0.2 collective-permute-done.9.refs_2_
  35.9 0.0 copy-start.4
  35.9 5.1 %collective-permute-start.10 = (f32[312,128]{1,0:T(8,128)S(1)}, f32[312,128]{1,0:T(8,128)S(1)}, u32[]{:S(2)}, u32[]{:S(2)}) collective-permute-start(f32[312,128]{1,0:T(8,128)S(1)} %collective-permute-done.9.refs_2_), channel_id=1, source_target_pairs={{0,1},{1,0},{2,3},{3,2},{4,5},{5,4},{6,7},{7,6},{8,9},{9,8},{10,11... | collective-permute-start | bytes 479240 | tf_op jit(solution)/shard_map/ppermute | solution.py:376
  41.0 0.0 collective-permute-done.11.refs_4_
  41.0 0.0 copy-start.5
  41.0 0.1 collective-permute-start.12
  41.1 0.0 collective-permute-done.13.refs_6_
  41.1 0.0 copy-start.6
  41.1 0.4 collective-permute-start.1
  41.5 0.0 collective-permute-done.2.refs_2_
  41.5 0.0 copy-start.1
  41.5 0.1 collective-permute-start.3
  41.6 0.0 collective-permute-done.8.refs_1_
  41.6 0.0 copy-start.7
  41.6 0.4 collective-permute-start.14
  42.0 0.0 collective-permute-done.10.refs_3_
  42.0 0.0 copy-start.8
  42.0 0.3 collective-permute-start.5
  42.4 0.0 collective-permute-done.12.refs_5_
  42.4 0.0 copy-start.9
  42.4 0.2 collective-permute-start.7
  42.6 0.8 %collective-permute-done.14.refs_7_ = f32[312,128]{1,0:T(8,128)S(1)} collective-permute-done((f32[312,128]{1,0:T(8,128)S(1)}, f32[312,128]{1,0:T(8,128)S(1)}, u32[]{:S(2)}, u32[]{:S(2)}) %collective-permute-start.14) | collective-permute-done | bytes 159776 | tf_op jit(solution)/shard_map/ppermute | solution.py:376
  43.4 0.0 copy-done.4
  43.4 0.0 copy-done.5
  43.4 0.0 copy-done.6
  43.4 0.0 copy-done.7
  43.4 0.0 copy-done.8
  43.4 0.0 copy-done.9
  43.4 0.0 copy-start.10
  43.4 0.6 %copy-done.10 = f32[312,128]{1,0:T(8,128)} copy-done((f32[312,128]{1,0:T(8,128)}, f32[312,128]{1,0:T(8,128)S(1)}, u32[]{:S(2)}) %copy-start.10) | copy-done | bytes 159768
  44.1 4.4 %shard_map.18 = (f32[8,264,128]{2,1,0:T(8,128)}, bf16[3,8,128,128]{3,2,1,0:T(8,128)(2,1)}, f32[3,8,1,128]{3,2,1,0:T(1,128)}) custom-call(f32[312,128]{1,0:T(8,128)} %get-tuple-element.18.refs_0_, f32[312,128]{1,0:T(8,128)} %copy-done.7, f32[312,128]{1,0:T(8,128)} %copy-done.4, f32[312,128]{1,0:T(8,128)} %copy-done.8, f32[312,128]{1,0:T(8,128)} %copy-done.5, ...), custom_call_target="tpu_custom_call" | custom-call | tf_op jit(solution)/shard_map/pallas_call | solution.py:228
  48.5 0.0 collective-permute-done.5.refs_5_
  48.5 0.0 copy-start.13
  48.5 0.0 collective-permute-done.7.refs_7_
  48.5 0.0 copy-start.14
  48.5 0.0 collective-permute-done.1.refs_1_
  48.5 0.0 copy-start.2
  48.5 0.0 collective-permute-done.3.refs_3_
  48.5 0.0 copy-start.3
  48.6 0.0 copy-done
  48.6 0.0 copy-done.11
  48.6 0.0 copy-done.12
  48.6 0.0 copy-done.1
  48.6 0.6 %copy-done.13 = f32[312,128]{1,0:T(8,128)} copy-done((f32[312,128]{1,0:T(8,128)}, f32[312,128]{1,0:T(8,128)S(1)}, u32[]{:S(2)}) %copy-start.13) | copy-done | bytes 159768
  49.2 0.1 copy-done.14
  49.2 0.1 copy-done.2
  49.3 0.1 copy-done.3
  49.4 6.9 %shard_map.19 = bf16[3,8,256,256]{3,2,1,0:T(8,128)(2,1)} custom-call(f32[528,128]{1,0:T(8,128)} %copy-done, f32[528,128]{1,0:T(8,128)} %copy-done.2, f32[528,128]{1,0:T(8,128)} %copy-done.1, f32[528,128]{1,0:T(8,128)} %copy-done.3, f32[312,128]{1,0:T(8,128)} %copy-done.11, f32[312,128]{1,0:T(8,128)} %copy-done.13, f32[312,128]{1,0:T(8,128)} %copy-done.12, ...), custom_call_target="tpu_custom_call" | custom-call | tf_op jit(solution)/shard_map/pallas_call | solution.py:241
Async XLA Ops:
  3.0 18.8 %collective-permute-start = (f32[528,128]{1,0:T(8,128)}, f32[528,128]{1,0:T(8,128)S(1)}, u32[]{:S(2)}, u32[]{:S(2)}) collective-permute-start(f32[528,128]{1,0:T(8,128)} %get-tuple-element.15), channel_id=1, source_target_pairs={{0,8},{1,9},{2,10},{3,11},{4,12},{5,13},{6,14},{7,15},{8,0},{9,1},... | collective-permute-start | bytes 811016 | tf_op jit(solution)/shard_map/ppermute | solution.py:376
  6.2 22.1 %collective-permute-start.4 = (f32[312,128]{1,0:T(8,128)}, f32[312,128]{1,0:T(8,128)S(1)}, u32[]{:S(2)}, u32[]{:S(2)}) collective-permute-start(f32[312,128]{1,0:T(8,128)} %get-tuple-element.16), channel_id=1, source_target_pairs={{0,12},{1,13},{2,14},{3,15},{4,8},{5,9},{6,10},{7,11},{8,4},{9,5},... | collective-permute-start | bytes 479240 | tf_op jit(solution)/shard_map/ppermute | solution.py:376
  21.8 26.7 %copy-start = (f32[528,128]{1,0:T(8,128)}, f32[528,128]{1,0:T(8,128)S(1)}, u32[]{:S(2)}) copy-start(f32[528,128]{1,0:T(8,128)S(1)} %collective-permute-done.refs_0_) | copy-start | bytes 811012
  21.8 19.7 %collective-permute-start.2 = (f32[528,128]{1,0:T(8,128)S(1)}, f32[528,128]{1,0:T(8,128)S(1)}, u32[]{:S(2)}, u32[]{:S(2)}) collective-permute-start(f32[528,128]{1,0:T(8,128)S(1)} %collective-permute-done.refs_0_), channel_id=1, source_target_pairs={{0,2},{1,3},{2,0},{3,1},{4,6},{5,7},{6,4},{7,5},{8,10},{9,11},{10,... | collective-permute-start | bytes 811016 | tf_op jit(solution)/shard_map/ppermute | solution.py:376
  22.8 7.2 %collective-permute-start.6 = (f32[312,128]{1,0:T(8,128)}, f32[312,128]{1,0:T(8,128)S(1)}, u32[]{:S(2)}, u32[]{:S(2)}) collective-permute-start(f32[312,128]{1,0:T(8,128)} %get-tuple-element.17), channel_id=1, source_target_pairs={{0,14},{1,15},{2,12},{3,13},{4,10},{5,11},{6,8},{7,9},{8,6},{9,7},... | collective-permute-start | bytes 479240 | tf_op jit(solution)/shard_map/ppermute | solution.py:376
  27.0 8.9 %collective-permute-start.9 = (f32[312,128]{1,0:T(8,128)}, f32[312,128]{1,0:T(8,128)S(1)}, u32[]{:S(2)}, u32[]{:S(2)}) collective-permute-start(f32[312,128]{1,0:T(8,128)} %get-tuple-element.19), channel_id=1, source_target_pairs={{0,2},{1,3},{2,0},{3,1},{4,6},{5,7},{6,4},{7,5},{8,10},{9,11},{10,... | collective-permute-start | bytes 479240 | tf_op jit(solution)/shard_map/ppermute | solution.py:376
  28.3 12.7 %collective-permute-start.11 = (f32[312,128]{1,0:T(8,128)}, f32[312,128]{1,0:T(8,128)S(1)}, u32[]{:S(2)}, u32[]{:S(2)}) collective-permute-start(f32[312,128]{1,0:T(8,128)} %get-tuple-element.20), channel_id=1, source_target_pairs={{0,4},{1,5},{2,6},{3,7},{4,0},{5,1},{6,2},{7,3},{8,12},{9,13},{10,... | collective-permute-start | bytes 479240 | tf_op jit(solution)/shard_map/ppermute | solution.py:376
  28.3 20.3 %copy-start.11 = (f32[312,128]{1,0:T(8,128)}, f32[312,128]{1,0:T(8,128)S(1)}, u32[]{:S(2)}) copy-start(f32[312,128]{1,0:T(8,128)S(1)} %collective-permute-done.4.refs_4_) | copy-start | bytes 479236
  28.3 12.8 %collective-permute-start.13 = (f32[312,128]{1,0:T(8,128)}, f32[312,128]{1,0:T(8,128)S(1)}, u32[]{:S(2)}, u32[]{:S(2)}) collective-permute-start(f32[312,128]{1,0:T(8,128)} %get-tuple-element.21), channel_id=1, source_target_pairs={{0,6},{1,7},{2,4},{3,5},{4,2},{5,3},{6,0},{7,1},{8,14},{9,15},{10,... | collective-permute-start | bytes 479240 | tf_op jit(solution)/shard_map/ppermute | solution.py:376
  30.0 18.6 %copy-start.12 = (f32[312,128]{1,0:T(8,128)}, f32[312,128]{1,0:T(8,128)S(1)}, u32[]{:S(2)}) copy-start(f32[312,128]{1,0:T(8,128)S(1)} %collective-permute-done.6.refs_6_) | copy-start | bytes 479236
  30.0 11.6 %collective-permute-start.8 = (f32[312,128]{1,0:T(8,128)}, f32[312,128]{1,0:T(8,128)S(1)}, u32[]{:S(2)}, u32[]{:S(2)}) collective-permute-start(f32[312,128]{1,0:T(8,128)} %get-tuple-element.18.refs_0_), channel_id=1, source_target_pairs={{0,1},{1,0},{2,3},{3,2},{4,5},{5,4},{6,7},{7,6},{8,9},{9,8},{10,11... | collective-permute-start | bytes 479240 | tf_op jit(solution)/shard_map/ppermute | solution.py:376
  35.9 7.5 %copy-start.4 = (f32[312,128]{1,0:T(8,128)}, f32[312,128]{1,0:T(8,128)S(1)}, u32[]{:S(2)}) copy-start(f32[312,128]{1,0:T(8,128)S(1)} %collective-permute-done.9.refs_2_) | copy-start | bytes 479236
  35.9 6.2 %collective-permute-start.10 = (f32[312,128]{1,0:T(8,128)S(1)}, f32[312,128]{1,0:T(8,128)S(1)}, u32[]{:S(2)}, u32[]{:S(2)}) collective-permute-start(f32[312,128]{1,0:T(8,128)S(1)} %collective-permute-done.9.refs_2_), channel_id=1, source_target_pairs={{0,1},{1,0},{2,3},{3,2},{4,5},{5,4},{6,7},{7,6},{8,9},{9,8},{10,11... | collective-permute-start | bytes 479240 | tf_op jit(solution)/shard_map/ppermute | solution.py:376
  41.0 2.4 %copy-start.5 = (f32[312,128]{1,0:T(8,128)}, f32[312,128]{1,0:T(8,128)S(1)}, u32[]{:S(2)}) copy-start(f32[312,128]{1,0:T(8,128)S(1)} %collective-permute-done.11.refs_4_) | copy-start | bytes 479236
  41.0 1.4 %collective-permute-start.12 = (f32[312,128]{1,0:T(8,128)S(1)}, f32[312,128]{1,0:T(8,128)S(1)}, u32[]{:S(2)}, u32[]{:S(2)}) collective-permute-start(f32[312,128]{1,0:T(8,128)S(1)} %collective-permute-done.11.refs_4_), channel_id=1, source_target_pairs={{0,1},{1,0},{2,3},{3,2},{4,5},{5,4},{6,7},{7,6},{8,9},{9,8},{10,11... | collective-permute-start | bytes 479240 | tf_op jit(solution)/shard_map/ppermute | solution.py:376
  41.1 2.3 %copy-start.6 = (f32[312,128]{1,0:T(8,128)}, f32[312,128]{1,0:T(8,128)S(1)}, u32[]{:S(2)}) copy-start(f32[312,128]{1,0:T(8,128)S(1)} %collective-permute-done.13.refs_6_) | copy-start | bytes 479236
  41.1 7.4 %collective-permute-start.1 = (f32[528,128]{1,0:T(8,128)S(1)}, f32[528,128]{1,0:T(8,128)S(1)}, u32[]{:S(2)}, u32[]{:S(2)}) collective-permute-start(f32[528,128]{1,0:T(8,128)S(1)} %collective-permute-done.refs_0_), channel_id=1, source_target_pairs={{0,1},{1,0},{2,3},{3,2},{4,5},{5,4},{6,7},{7,6},{8,9},{9,8},{10,11... | collective-permute-start | bytes 811016 | tf_op jit(solution)/shard_map/ppermute | solution.py:376
  41.5 7.1 %copy-start.1 = (f32[528,128]{1,0:T(8,128)}, f32[528,128]{1,0:T(8,128)S(1)}, u32[]{:S(2)}) copy-start(f32[528,128]{1,0:T(8,128)S(1)} %collective-permute-done.2.refs_2_) | copy-start | bytes 811012
  41.5 7.0 %collective-permute-start.3 = (f32[528,128]{1,0:T(8,128)S(1)}, f32[528,128]{1,0:T(8,128)S(1)}, u32[]{:S(2)}, u32[]{:S(2)}) collective-permute-start(f32[528,128]{1,0:T(8,128)S(1)} %collective-permute-done.2.refs_2_), channel_id=1, source_target_pairs={{0,1},{1,0},{2,3},{3,2},{4,5},{5,4},{6,7},{7,6},{8,9},{9,8},{10,11... | collective-permute-start | bytes 811016 | tf_op jit(solution)/shard_map/ppermute | solution.py:376
  41.6 1.8 %copy-start.7 = (f32[312,128]{1,0:T(8,128)}, f32[312,128]{1,0:T(8,128)S(1)}, u32[]{:S(2)}) copy-start(f32[312,128]{1,0:T(8,128)S(1)} %collective-permute-done.8.refs_1_) | copy-start | bytes 479236
  41.6 1.8 %collective-permute-start.14 = (f32[312,128]{1,0:T(8,128)S(1)}, f32[312,128]{1,0:T(8,128)S(1)}, u32[]{:S(2)}, u32[]{:S(2)}) collective-permute-start(f32[312,128]{1,0:T(8,128)S(1)} %collective-permute-done.13.refs_6_), channel_id=1, source_target_pairs={{0,1},{1,0},{2,3},{3,2},{4,5},{5,4},{6,7},{7,6},{8,9},{9,8},{10,11... | collective-permute-start | bytes 479240 | tf_op jit(solution)/shard_map/ppermute | solution.py:376
  42.0 1.4 %copy-start.8 = (f32[312,128]{1,0:T(8,128)}, f32[312,128]{1,0:T(8,128)S(1)}, u32[]{:S(2)}) copy-start(f32[312,128]{1,0:T(8,128)S(1)} %collective-permute-done.10.refs_3_) | copy-start | bytes 479236
  42.0 6.5 %collective-permute-start.5 = (f32[312,128]{1,0:T(8,128)S(1)}, f32[312,128]{1,0:T(8,128)S(1)}, u32[]{:S(2)}, u32[]{:S(2)}) collective-permute-start(f32[312,128]{1,0:T(8,128)S(1)} %collective-permute-done.4.refs_4_), channel_id=1, source_target_pairs={{0,1},{1,0},{2,3},{3,2},{4,5},{5,4},{6,7},{7,6},{8,9},{9,8},{10,11... | collective-permute-start | bytes 479240 | tf_op jit(solution)/shard_map/ppermute | solution.py:376
  42.4 1.0 %copy-start.9 = (f32[312,128]{1,0:T(8,128)}, f32[312,128]{1,0:T(8,128)S(1)}, u32[]{:S(2)}) copy-start(f32[312,128]{1,0:T(8,128)S(1)} %collective-permute-done.12.refs_5_) | copy-start | bytes 479236
  42.4 6.1 %collective-permute-start.7 = (f32[312,128]{1,0:T(8,128)S(1)}, f32[312,128]{1,0:T(8,128)S(1)}, u32[]{:S(2)}, u32[]{:S(2)}) collective-permute-start(f32[312,128]{1,0:T(8,128)S(1)} %collective-permute-done.6.refs_6_), channel_id=1, source_target_pairs={{0,1},{1,0},{2,3},{3,2},{4,5},{5,4},{6,7},{7,6},{8,9},{9,8},{10,11... | collective-permute-start | bytes 479240 | tf_op jit(solution)/shard_map/ppermute | solution.py:376
  43.4 0.7 %copy-start.10 = (f32[312,128]{1,0:T(8,128)}, f32[312,128]{1,0:T(8,128)S(1)}, u32[]{:S(2)}) copy-start(f32[312,128]{1,0:T(8,128)S(1)} %collective-permute-done.14.refs_7_) | copy-start | bytes 479236
  48.5 0.7 %copy-start.13 = (f32[312,128]{1,0:T(8,128)}, f32[312,128]{1,0:T(8,128)S(1)}, u32[]{:S(2)}) copy-start(f32[312,128]{1,0:T(8,128)S(1)} %collective-permute-done.5.refs_5_) | copy-start | bytes 479236
  48.5 0.7 %copy-start.14 = (f32[312,128]{1,0:T(8,128)}, f32[312,128]{1,0:T(8,128)S(1)}, u32[]{:S(2)}) copy-start(f32[312,128]{1,0:T(8,128)S(1)} %collective-permute-done.7.refs_7_) | copy-start | bytes 479236
  48.5 0.8 %copy-start.2 = (f32[528,128]{1,0:T(8,128)}, f32[528,128]{1,0:T(8,128)S(1)}, u32[]{:S(2)}) copy-start(f32[528,128]{1,0:T(8,128)S(1)} %collective-permute-done.1.refs_1_) | copy-start | bytes 811012
  48.5 0.9 %copy-start.3 = (f32[528,128]{1,0:T(8,128)}, f32[528,128]{1,0:T(8,128)S(1)}, u32[]{:S(2)}) copy-start(f32[528,128]{1,0:T(8,128)S(1)} %collective-permute-done.3.refs_3_) | copy-start | bytes 811012
